TPU v7x, 32 devices: a whole 2x2x4 slice. The times are simulated.
32 devices in a mesh: dp: 8 (over z, x), tensor: 4 (over y, core).
Axes of the slice: x: 2, y: 2, z: 4, core: 2. Of those that a mesh axis runs over, the one named last changes fastest.
Arguments:
- tokens: bfloat16 [8192, 2048], P(('dp', 'tensor')), may hold values from -6 to 6
- parents: int32 [8, 8], P('dp'), may hold values from 0 to 6, as said below
- attn_gain: bfloat16 [2048], P('dp'), may hold values from 0.099609375 to 1.8984375
- w_query: bfloat16 [2048, 2048], P('dp', 'tensor'), may hold values from -0.125 to 0.125
- key_matrix: bfloat16 [2048, 1024], P('dp', 'tensor'), may hold values from -0.125 to 0.125
- value_matrix: bfloat16 [2048, 1024], P('dp', 'tensor'), may hold values from -0.125 to 0.125
- w_out: bfloat16 [2048, 2048], P('tensor', 'dp'), may hold values from -0.5 to 0.5
- mlp_gain: bfloat16 [2048], P('dp'), may hold values from 0.099609375 to 1.8984375
- w_gate: bfloat16 [2048, 8192], P('dp', 'tensor'), may hold values from -0.125 to 0.125
- w_up: bfloat16 [2048, 8192], P('dp', 'tensor'), may hold values from -0.125 to 0.125
- w_down: bfloat16 [8192, 2048], P('tensor', 'dp'), may hold values from -0.0625 to 0.0625
- cotangent: bfloat16 [8192, 2048], P(('dp', 'tensor')), may hold values from -6 to 6
Outputs:
- output: bfloat16 [8192, 2048], P(('dp', 'tensor'))
- grad_tokens: bfloat16 [8192, 2048], P(('dp', 'tensor'))
- grad_attn_gain: float32 [2048], P('dp')
- grad_query: float32 [2048, 2048], P('dp', 'tensor')
- grad_key: float32 [2048, 1024], P('dp', 'tensor')
- grad_value: float32 [2048, 1024], P('dp', 'tensor')
- grad_out: float32 [2048, 2048], P('tensor', 'dp')
- grad_mlp_gain: float32 [2048], P('dp')
- grad_gate: float32 [2048, 8192], P('dp', 'tensor')
- grad_up: float32 [2048, 8192], P('dp', 'tensor')
- grad_down: float32 [8192, 2048], P('tensor', 'dp')
Inputs may be any that keep to these rules, and one draw needn't show every extreme that they name: parents[t, 0] is 0, parents[t, b] is below b for b >= 1, and the last segment's parent is segment 8 - 2, so segment 0 is each tree's root and every segment's ancestors come earlier.
All inputs are finite; a program needn't handle non-finite values.
Results may differ from a plain program's by a relative error of at most 0.014.
Values may be sent and summed in bfloat16 or wider, within the bound.
A program may use at most 256 MiB of HBM per device.

v0:
```python
import jax
import jax.numpy as jnp
from jax import lax
from jax.sharding import PartitionSpec as P

HEAD_SIZE = 256
BLK = 128


EPS = 1e-06
THETA = 1000042.0
NEG = -1e30
HIGH = lax.Precision.HIGHEST


def tree_tables(parent_row, tree_len, block_len):
    blocks = parent_row.shape[0]
    nodes = jnp.arange(blocks, dtype=jnp.int32)
    hops = (parent_row[:, None] == nodes[None, :]).astype(jnp.float32)
    reach = jnp.eye(blocks, dtype=jnp.float32)
    walk = reach
    for hop_count in range(blocks):
        walk = jnp.dot(walk, hops, precision=HIGH)
        reach = jnp.maximum(reach, walk)
    depth = jnp.sum(reach, axis=1) - 1.0
    rows = jnp.arange(tree_len, dtype=jnp.int32)
    member = (rows[:, None] // block_len == nodes[None, :]).astype(jnp.float32)
    visible = jnp.dot(jnp.dot(member, reach, precision=HIGH), member.T, precision=HIGH) > 0.5
    allowed_mask = visible & (rows[None, :] <= rows[:, None])
    place = jnp.dot(member, depth, precision=HIGH) * block_len + (rows % block_len).astype(
        jnp.float32
    )
    return (allowed_mask, place)


def rope_tables(place, head_dim):
    half = head_dim // 2
    freq = THETA ** (-2.0 * jnp.arange(half, dtype=jnp.float32) / head_dim)
    angle = place[:, None] * freq[None, :]
    cosine_table = jnp.cos(angle)
    sine_table = jnp.sin(angle)
    return (
        jnp.concatenate([cosine_table, cosine_table], -1),
        jnp.concatenate([sine_table, sine_table], -1),
    )


def apply_rotation(values, cosine_table, sine_table, sign):
    half = values.shape[-1] // 2
    turned = jnp.concatenate([-values[..., half:], values[..., :half]], -1)
    return values * cosine_table[:, None, :] + sign * turned * sine_table[:, None, :]


def normalize(values):
    inverse = lax.rsqrt(jnp.mean(values * values, axis=-1, keepdims=True) + EPS)
    return (values * inverse, inverse)


def norm_back(grad_normed, gain, scaled, inverse):
    grad_scaled = grad_normed * gain
    inner = jnp.mean(grad_scaled * scaled, axis=-1, keepdims=True)
    return (inverse * (grad_scaled - scaled * inner), jnp.sum(grad_normed * scaled, axis=0))


def dot_last(left, right):
    return lax.dot_general(
        left, right, (((1,), (1,)), ((), ())), preferred_element_type=jnp.float32
    )


def dot_first(left, right):
    return lax.dot_general(
        left, right, (((0,), (0,)), ((), ())), preferred_element_type=jnp.float32
    )


def gather_attention(attn_gain, w_query, key_matrix, value_matrix, w_out):
    return (
        lax.all_gather(attn_gain, "dp", axis=0, tiled=True),
        lax.all_gather(w_query, "dp", axis=0, tiled=True),
        lax.all_gather(key_matrix, "dp", axis=0, tiled=True),
        lax.all_gather(value_matrix, "dp", axis=0, tiled=True),
        lax.all_gather(w_out, "dp", axis=1, tiled=True),
    )


def gather_mlp(mlp_gain, w_gate, w_up, w_down):
    return (
        lax.all_gather(mlp_gain, "dp", axis=0, tiled=True),
        lax.all_gather(w_gate, "dp", axis=0, tiled=True),
        lax.all_gather(w_up, "dp", axis=0, tiled=True),
        lax.all_gather(w_down, "dp", axis=1, tiled=True),
    )


def tree_scores(grouped, key, allowed_mask, scale):
    raw = jnp.einsum("qkgd,skd->kgqs", grouped, key, preferred_element_type=jnp.float32)
    return jnp.where(allowed_mask[None, None], raw * scale, NEG)


def body(
    tokens,
    parents,
    attn_gain,
    w_query,
    key_matrix,
    value_matrix,
    w_out,
    mlp_gain,
    w_gate,
    w_up,
    w_down,
    cotangent,
):
    rows = tokens.shape[0]
    tree_len = rows * lax.axis_size("tensor")
    local_q = w_query.shape[1] // HEAD_SIZE
    local_kv = key_matrix.shape[1] // HEAD_SIZE
    query_group = local_q // local_kv
    scale = HEAD_SIZE ** (-0.5)
    allowed_mask, place = tree_tables(parents[0], tree_len, BLK)
    cosine_table, sine_table = rope_tables(place, HEAD_SIZE)
    gain_a, query_w, key_w, value_w, out_w = gather_attention(
        attn_gain, w_query, key_matrix, value_matrix, w_out
    )
    gain_af = gain_a.astype(jnp.float32)
    inputs = tokens.astype(jnp.float32)
    scaled_a, inverse_a = normalize(inputs)
    normed_a = (scaled_a * gain_af).astype(jnp.bfloat16)
    normed_all = lax.all_gather(normed_a, "tensor", axis=0, tiled=True)
    query_raw = jnp.dot(normed_all, query_w, preferred_element_type=jnp.float32)
    unrotated_key = jnp.dot(normed_all, key_w, preferred_element_type=jnp.float32)
    unprojected_value = jnp.dot(normed_all, value_w, preferred_element_type=jnp.float32)
    query_rows = apply_rotation(
        query_raw.reshape(tree_len, local_q, HEAD_SIZE), cosine_table, sine_table, 1.0
    ).astype(jnp.bfloat16)
    key = apply_rotation(
        unrotated_key.reshape(tree_len, local_kv, HEAD_SIZE), cosine_table, sine_table, 1.0
    ).astype(jnp.bfloat16)
    value_rows = unprojected_value.reshape(tree_len, local_kv, HEAD_SIZE).astype(jnp.bfloat16)
    grouped = query_rows.reshape(tree_len, local_kv, query_group, HEAD_SIZE)
    scores = tree_scores(grouped, key, allowed_mask, scale)
    top = jnp.max(scores, axis=-1, keepdims=True)
    weights = jnp.exp(scores - top)
    total = jnp.sum(weights, axis=-1, keepdims=True)
    probs = (weights / total).astype(jnp.bfloat16)
    log_total = top + jnp.log(total)
    attended_rows = jnp.einsum(
        "kgqs,skd->qkgd", probs, value_rows, preferred_element_type=jnp.float32
    )
    attended_rows = attended_rows.reshape(tree_len, local_q * HEAD_SIZE).astype(jnp.bfloat16)
    mixed = inputs + lax.psum_scatter(
        jnp.dot(attended_rows, out_w, preferred_element_type=jnp.float32),
        "tensor",
        scatter_dimension=0,
        tiled=True,
    )
    gain_m, gate_w, up_w, down_w = gather_mlp(mlp_gain, w_gate, w_up, w_down)
    gain_mf = gain_m.astype(jnp.float32)
    scaled_m, inverse_m = normalize(mixed)
    normed_m = (scaled_m * gain_mf).astype(jnp.bfloat16)
    normed_m_all = lax.all_gather(normed_m, "tensor", axis=0, tiled=True)
    gate = jnp.dot(normed_m_all, gate_w, preferred_element_type=jnp.float32)
    upper = jnp.dot(normed_m_all, up_w, preferred_element_type=jnp.float32)
    sigma = jax.nn.sigmoid(gate)
    swish = gate * sigma
    hidden = (swish * upper).astype(jnp.bfloat16)
    output = (
        mixed
        + lax.psum_scatter(
            jnp.dot(hidden, down_w, preferred_element_type=jnp.float32).astype(jnp.bfloat16),
            "tensor",
            scatter_dimension=0,
            tiled=True,
        ).astype(jnp.float32)
    ).astype(jnp.bfloat16)
    gain_m, gate_w, up_w, down_w = gather_mlp(mlp_gain, w_gate, w_up, w_down)
    gain_mf = gain_m.astype(jnp.float32)
    grad_all = lax.all_gather(cotangent, "tensor", axis=0, tiled=True)
    grad_hidden = dot_last(grad_all, down_w)
    grad_gate_act = (grad_hidden * upper * sigma * (1.0 + gate * (1.0 - sigma))).astype(
        jnp.bfloat16
    )
    grad_up_act = (grad_hidden * swish).astype(jnp.bfloat16)
    grad_normed_m = lax.psum_scatter(
        dot_last(grad_gate_act, gate_w) + dot_last(grad_up_act, up_w),
        "tensor",
        scatter_dimension=0,
        tiled=True,
    )
    grad_through, gain_m_part = norm_back(grad_normed_m, gain_mf, scaled_m, inverse_m)
    grad_mixed = cotangent.astype(jnp.float32) + grad_through
    grad_gate = dot_first(normed_m_all, grad_gate_act)
    grad_up = dot_first(normed_m_all, grad_up_act)
    grad_down = dot_first(hidden, grad_all)
    gain_m_sum, grad_gate, grad_up, grad_down = (
        lax.psum_scatter(gain_m_part, "dp", scatter_dimension=0, tiled=True),
        lax.psum_scatter(grad_gate, "dp", scatter_dimension=0, tiled=True),
        lax.psum_scatter(grad_up, "dp", scatter_dimension=0, tiled=True),
        lax.psum_scatter(grad_down, "dp", scatter_dimension=1, tiled=True),
    )
    gain_a, query_w, key_w, value_w, out_w = gather_attention(
        attn_gain, w_query, key_matrix, value_matrix, w_out
    )
    gain_af = gain_a.astype(jnp.float32)
    grad_mixed_low = grad_mixed.astype(jnp.bfloat16)
    grad_mixed_all = lax.all_gather(grad_mixed_low, "tensor", axis=0, tiled=True)
    grad_attended = dot_last(grad_mixed_all, out_w).astype(jnp.bfloat16)
    grad_grouped = grad_attended.reshape(tree_len, local_kv, query_group, HEAD_SIZE)
    scores = tree_scores(grouped, key, allowed_mask, scale)
    probs_full = jnp.exp(scores - log_total)
    probs_back = probs_full.astype(jnp.bfloat16)
    grad_value_act = jnp.einsum(
        "kgqs,qkgd->skd", probs_back, grad_grouped, preferred_element_type=jnp.float32
    )
    grad_probs = jnp.einsum(
        "qkgd,skd->kgqs", grad_grouped, value_rows, preferred_element_type=jnp.float32
    )
    inner = jnp.sum(probs_full * grad_probs, axis=-1, keepdims=True)
    grad_scores = (probs_full * (grad_probs - inner) * scale).astype(jnp.bfloat16)
    grad_query_rot = jnp.einsum(
        "kgqs,skd->qkgd", grad_scores, key, preferred_element_type=jnp.float32
    )
    grad_key_rot = jnp.einsum(
        "kgqs,qkgd->skd", grad_scores, grouped, preferred_element_type=jnp.float32
    )
    grad_query_act = (
        apply_rotation(
            grad_query_rot.reshape(tree_len, local_q, HEAD_SIZE), cosine_table, sine_table, -1.0
        )
        .astype(jnp.bfloat16)
        .reshape(tree_len, local_q * HEAD_SIZE)
    )
    grad_key_act = (
        apply_rotation(grad_key_rot, cosine_table, sine_table, -1.0)
        .astype(jnp.bfloat16)
        .reshape(tree_len, local_kv * HEAD_SIZE)
    )
    grad_value_low = grad_value_act.astype(jnp.bfloat16).reshape(tree_len, local_kv * HEAD_SIZE)
    grad_normed_a = lax.psum_scatter(
        dot_last(grad_query_act, query_w)
        + dot_last(grad_key_act, key_w)
        + dot_last(grad_value_low, value_w),
        "tensor",
        scatter_dimension=0,
        tiled=True,
    )
    grad_input_part, gain_a_part = norm_back(grad_normed_a, gain_af, scaled_a, inverse_a)
    grad_tokens = (grad_mixed + grad_input_part).astype(jnp.bfloat16)
    grad_out = dot_first(attended_rows, grad_mixed_all)
    grad_query = dot_first(normed_all, grad_query_act)
    grad_key = dot_first(normed_all, grad_key_act)
    grad_value = dot_first(normed_all, grad_value_low)
    gain_a_sum, grad_query, grad_key, grad_value, grad_out = (
        lax.psum_scatter(gain_a_part, "dp", scatter_dimension=0, tiled=True),
        lax.psum_scatter(grad_query, "dp", scatter_dimension=0, tiled=True),
        lax.psum_scatter(grad_key, "dp", scatter_dimension=0, tiled=True),
        lax.psum_scatter(grad_value, "dp", scatter_dimension=0, tiled=True),
        lax.psum_scatter(grad_out, "dp", scatter_dimension=1, tiled=True),
    )
    grad_attn_gain, grad_mlp_gain = lax.psum((gain_a_sum, gain_m_sum), "tensor")
    return (
        output,
        grad_tokens,
        grad_attn_gain,
        grad_query,
        grad_key,
        grad_value,
        grad_out,
        grad_mlp_gain,
        grad_gate,
        grad_up,
        grad_down,
    )


def solution(mesh):
    in_specs = (
        P(("dp", "tensor"), None),
        P("dp", None),
        P("dp"),
        P("dp", "tensor"),
        P("dp", "tensor"),
        P("dp", "tensor"),
        P("tensor", "dp"),
        P("dp"),
        P("dp", "tensor"),
        P("dp", "tensor"),
        P("tensor", "dp"),
        P(("dp", "tensor"), None),
    )
    out_specs = (
        P(("dp", "tensor"), None),
        P(("dp", "tensor"), None),
        P("dp"),
        P("dp", "tensor"),
        P("dp", "tensor"),
        P("dp", "tensor"),
        P("tensor", "dp"),
        P("dp"),
        P("dp", "tensor"),
        P("dp", "tensor"),
        P("tensor", "dp"),
    )
    return jax.shard_map(body, mesh=mesh, in_specs=in_specs, out_specs=out_specs, check_vma=False)
```

profile of v0, /device:TPU:0, one launch (start us, length us, event | category | flops | bytes accessed | tf_op | source)
XLA Modules:
  0.0 2263.9 jit_solution(5037500792913839293)
XLA Ops:
  8.6 22.2 all-gather
  53.2 35.5 %all-gather.14.cloned.1.call-done = bf16[1024,2048]{1,0:T(8,128)(2,1)} async-done(((bf16[256,2048]{1,0:T(8,128)(2,1)}), bf16[1024,2048]{1,0:T(8,128)(2,1)}) %all-gather.14.cloned.1.call-update) | async-done | bytes 4194320 | tf_op jit(solution)/shard_map/all_gather | solution.py:130
  92.6 47.7 %all-gather.20.cloned.1.call-done = bf16[2048,512]{1,0:T(8,128)(2,1)} async-done(((bf16[256,512]{1,0:T(8,128)(2,1)}), bf16[2048,512]{1,0:T(8,128)(2,1)}) %all-gather.20.cloned.1.call-update) | async-done | bytes 2097168 | tf_op jit(solution)/shard_map/all_gather | solution.py:80
  149.7 31.2 %all-gather.16.cloned.1.call-done = bf16[2048,256]{1,0:T(8,128)(2,1)} async-done(((bf16[256,256]{1,0:T(8,128)(2,1)}), bf16[2048,256]{1,0:T(8,128)(2,1)}) %all-gather.16.cloned.1.call-update) | async-done | bytes 1048592 | tf_op jit(solution)/shard_map/all_gather | solution.py:82
  191.4 41.2 %all-gather.22.cloned.1.call-done = bf16[512,2048]{1,0:T(8,128)(2,1)} async-done(((bf16[512,256]{1,0:T(8,128)(2,1)}), bf16[512,2048]{1,0:T(8,128)(2,1)}) %all-gather.22.cloned.1.call-update) | async-done | bytes 2097168 | tf_op jit(solution)/shard_map/all_gather | solution.py:83
  241.0 17.7 all-gather.1
  258.7 51.5 %reduce-scatter.12.cloned.1.call-done = f32[256,2048]{1,0:T(8,128)} async-done(((f32[1024,2048]{1,0:T(8,128)}), f32[256,2048]{1,0:T(8,128)}) %reduce-scatter.12.cloned.1.call-update) | async-done | bytes 2097168 | tf_op jit(solution)/shard_map/reduce_scatter | solution.py:152
  315.8 121.8 %all-gather.26.cloned.1.call-done = bf16[2048,2048]{1,0:T(8,128)(2,1)} async-done(((bf16[256,2048]{1,0:T(8,128)(2,1)}), bf16[2048,2048]{1,0:T(8,128)(2,1)}) %all-gather.26.cloned.1.call-update) | async-done | bytes 8388624 | tf_op jit(solution)/shard_map/all_gather | solution.py:90
  437.6 34.9 %all-gather.24.cloned.1.call-done = bf16[1024,2048]{1,0:T(8,128)(2,1)} async-done(((bf16[256,2048]{1,0:T(8,128)(2,1)}), bf16[1024,2048]{1,0:T(8,128)(2,1)}) %all-gather.24.cloned.1.call-update) | async-done | bytes 4194320 | tf_op jit(solution)/shard_map/all_gather | solution.py:162
  486.9 112.9 %all-gather.28.cloned.1.call-done = bf16[2048,2048]{1,0:T(8,128)(2,1)} async-done(((bf16[256,2048]{1,0:T(8,128)(2,1)}), bf16[2048,2048]{1,0:T(8,128)(2,1)}) %all-gather.28.cloned.1.call-update) | async-done | bytes 8388624 | tf_op jit(solution)/shard_map/all_gather | solution.py:91
  614.2 19.7 all-gather.32.cloned.1.call-done
  634.0 127.7 %all-gather.30.cloned.1.call-done = bf16[2048,2048]{1,0:T(8,128)(2,1)} async-done(((bf16[2048,256]{1,0:T(8,128)(2,1)}), bf16[2048,2048]{1,0:T(8,128)(2,1)}) %all-gather.30.cloned.1.call-update) | async-done | bytes 8388624 | tf_op jit(solution)/shard_map/all_gather | solution.py:92
  761.6 21.8 multiply_convert_fusion
  811.6 70.0 %reduce-scatter.16.cloned.1.call-done = f32[256,2048]{1,0:T(8,128)} async-done(((f32[1024,2048]{1,0:T(8,128)}), f32[256,2048]{1,0:T(8,128)}) %reduce-scatter.16.cloned.1.call-update) | async-done | bytes 2097168 | tf_op jit(solution)/shard_map/reduce_scatter | solution.py:185
  886.8 34.6 %all-gather.34.cloned.1.call-done = bf16[1024,2048]{1,0:T(8,128)(2,1)} async-done(((bf16[256,2048]{1,0:T(8,128)(2,1)}), bf16[1024,2048]{1,0:T(8,128)(2,1)}) %all-gather.34.cloned.1.call-update) | async-done | bytes 4194320 | tf_op jit(solution)/shard_map/all_gather | solution.py:207
  1022.5 15.9 fusion.106
  1042.7 37.2 %all-reduce.2 = (f32[2048]{0:T(1024)S(1)}, f32[2048]{0:T(1024)S(1)}) all-reduce(f32[2048]{0:T(1024)S(1)} %get-tuple-element.13, f32[2048]{0:T(1024)S(1)} %copy-done.27), channel_id=6, replica_groups=mesh['dp'=8,'tensor'=4] {'dp'}, use_global_device_ids=true, to_apply=%region_13.14.clone | all-reduce | flops 4096 | bytes 32768
  1091.6 51.7 %reduce-scatter.22.cloned.1.call-done = f32[256,256]{1,0:T(8,128)} async-done(((f32[2048,256]{1,0:T(8,128)}), f32[256,256]{1,0:T(8,128)}) %reduce-scatter.22.cloned.1.call-update) | async-done | bytes 262160 | tf_op jit(solution)/shard_map/reduce_scatter | solution.py:257
  1143.2 70.6 %reduce-scatter.24.cloned.1.call-done = f32[256,256]{1,0:T(8,128)} async-done(((f32[2048,256]{1,0:T(8,128)}), f32[256,256]{1,0:T(8,128)}) %reduce-scatter.24.cloned.1.call-update) | async-done | bytes 262160 | tf_op jit(solution)/shard_map/reduce_scatter | solution.py:258
  1213.8 91.0 %reduce-scatter.20.cloned.1.call-done = f32[256,512]{1,0:T(8,128)} async-done(((f32[2048,512]{1,0:T(8,128)}), f32[256,512]{1,0:T(8,128)}) %reduce-scatter.20.cloned.1.call-update) | async-done | bytes 524304 | tf_op jit(solution)/shard_map/reduce_scatter | solution.py:256
  1304.8 92.9 %reduce-scatter.26.cloned.1.call-done = f32[512,256]{1,0:T(8,128)} async-done(((f32[512,2048]{1,0:T(8,128)}), f32[512,256]{1,0:T(8,128)}) %reduce-scatter.26.cloned.1.call-update) | async-done | bytes 524304 | tf_op jit(solution)/shard_map/reduce_scatter | solution.py:259
  1397.7 286.6 %reduce-scatter.28.cloned.1.call-done = f32[256,2048]{1,0:T(8,128)} async-done(((f32[2048,2048]{1,0:T(8,128)}), f32[256,2048]{1,0:T(8,128)}) %reduce-scatter.28.cloned.1.call-update) | async-done | bytes 2097168 | tf_op jit(solution)/shard_map/reduce_scatter | solution.py:198
  1684.3 286.5 %reduce-scatter.30.cloned.1.call-done = f32[256,2048]{1,0:T(8,128)} async-done(((f32[2048,2048]{1,0:T(8,128)}), f32[256,2048]{1,0:T(8,128)}) %reduce-scatter.30.cloned.1.call-update) | async-done | bytes 2097168 | tf_op jit(solution)/shard_map/reduce_scatter | solution.py:199
  1970.8 286.1 %reduce-scatter.32.cloned.1.call-done = f32[2048,256]{1,0:T(8,128)} async-done(((f32[2048,2048]{1,0:T(8,128)}), f32[2048,256]{1,0:T(8,128)}) %reduce-scatter.32.cloned.1.call-update) | async-done | bytes 2097168 | tf_op jit(solution)/shard_map/reduce_scatter | solution.py:200
  (210 shorter events, 239.2 us)
Async XLA Ops:
  7.2 46.1 %all-gather.18.cloned.1.call-start = ((), (), s32[]{:S(2)}) async-start(), calls=%async_computation.13 | async-start | bytes 1179648 | tf_op jit(solution)/shard_map/all_gather | solution.py:81
  7.9 80.9 %all-gather.14.cloned.1.call-start = ((), (), s32[]{:S(2)}) async-start(), calls=%async_computation.11 | async-start | bytes 5242880 | tf_op jit(solution)/shard_map/all_gather | solution.py:130
  35.5 104.7 %all-gather.20.cloned.1.call-start = ((), (), s32[]{:S(2)}) async-start(), calls=%async_computation.14 | async-start | bytes 2359296 | tf_op jit(solution)/shard_map/all_gather | solution.py:80
  36.2 144.7 %all-gather.16.cloned.1.call-start = ((), (), s32[]{:S(2)}) async-start(), calls=%async_computation.12 | async-start | bytes 1179648 | tf_op jit(solution)/shard_map/all_gather | solution.py:82
  36.8 195.8 %all-gather.22.cloned.1.call-start = ((), (), s32[]{:S(2)}) async-start(), calls=%async_computation.15 | async-start | bytes 2359296 | tf_op jit(solution)/shard_map/all_gather | solution.py:83
  37.4 272.9 %reduce-scatter.12.cloned.1.call-start = ((), (), s32[]{:S(2)}) async-start(), calls=%async_computation.16 | async-start | bytes 10485760 | tf_op jit(solution)/shard_map/reduce_scatter | solution.py:152
  240.2 197.4 %all-gather.26.cloned.1.call-start = ((), (), s32[]{:S(2)}) async-start(), calls=%async_computation.18 | async-start | bytes 9437184 | tf_op jit(solution)/shard_map/all_gather | solution.py:90
  240.9 231.5 %all-gather.24.cloned.1.call-start = ((), (), s32[]{:S(2)}) async-start(), calls=%async_computation.17 | async-start | bytes 5242880 | tf_op jit(solution)/shard_map/all_gather | solution.py:162
  258.7 625.8 %copy-start.23 = (f32[8,1,256]{2,1,0:T(1,128)}, f32[8,1,256]{2,1,0:T(1,128)S(1)}, u32[]{:S(2)}) copy-start(f32[8,1,256]{2,1,0:T(1,128)S(1)} %convert_element_type.146) | copy-start | bytes 24580
  312.2 572.3 %copy-start.1 = (f32[256,2048]{1,0:T(8,128)}, f32[256,2048]{1,0:T(8,128)S(1)}, u32[]{:S(2)}) copy-start(f32[256,2048]{1,0:T(8,128)S(1)} %get-tuple-element.20) | copy-start | bytes 6291460
  313.6 286.1 %all-gather.28.cloned.1.call-start = ((), (), s32[]{:S(2)}) async-start(), calls=%async_computation.19 | async-start | bytes 9437184 | tf_op jit(solution)/shard_map/all_gather | solution.py:91
  314.4 319.6 %all-gather.32.cloned.1.call-start = ((), (), s32[]{:S(2)}) async-start(), calls=%async_computation.22 | async-start | bytes 5242880 | tf_op jit(solution)/shard_map/all_gather | solution.py:179
  315.0 446.7 %all-gather.30.cloned.1.call-start = ((), (), s32[]{:S(2)}) async-start(), calls=%async_computation.20 | async-start | bytes 9437184 | tf_op jit(solution)/shard_map/all_gather | solution.py:92
  315.7 565.9 %reduce-scatter.16.cloned.1.call-start = ((), (), s32[]{:S(2)}) async-start(), calls=%async_computation.23 | async-start | bytes 10485760 | tf_op jit(solution)/shard_map/reduce_scatter | solution.py:185
  811.6 109.8 %all-gather.34.cloned.1.call-start = ((), (), s32[]{:S(2)}) async-start(), calls=%async_computation.24 | async-start | bytes 5242880 | tf_op jit(solution)/shard_map/all_gather | solution.py:207
  886.7 153.6 %reduce-scatter.18.cloned.1.call-start = ((), (), s32[]{:S(2)}) async-start(), calls=%async_computation.25 | async-start | bytes 10485760 | tf_op jit(solution)/shard_map/reduce_scatter | solution.py:240
  952.5 133.7 %reduce-scatter.14.cloned.1.call-start = ((), (), s32[]{:S(2)}) async-start(), calls=%async_computation.21 | async-start | bytes 5242880 | tf_op jit(solution)/shard_map/reduce_scatter | solution.py:170
  966.7 176.6 %reduce-scatter.22.cloned.1.call-start = ((), (), s32[]{:S(2)}) async-start(), calls=%async_computation.27 | async-start | bytes 2359296 | tf_op jit(solution)/shard_map/reduce_scatter | solution.py:257
  971.8 242.0 %reduce-scatter.24.cloned.1.call-start = ((), (), s32[]{:S(2)}) async-start(), calls=%async_computation.28 | async-start | bytes 2359296 | tf_op jit(solution)/shard_map/reduce_scatter | solution.py:258
  976.8 328.0 %reduce-scatter.20.cloned.1.call-start = ((), (), s32[]{:S(2)}) async-start(), calls=%async_computation.26 | async-start | bytes 4718592 | tf_op jit(solution)/shard_map/reduce_scatter | solution.py:256
  983.5 414.2 %reduce-scatter.26.cloned.1.call-start = ((), (), s32[]{:S(2)}) async-start(), calls=%async_computation.29 | async-start | bytes 4718592 | tf_op jit(solution)/shard_map/reduce_scatter | solution.py:259
  991.4 692.8 %reduce-scatter.28.cloned.1.call-start = ((), (), s32[]{:S(2)}) async-start(), calls=%async_computation.30 | async-start | bytes 18874368 | tf_op jit(solution)/shard_map/reduce_scatter | solution.py:198
  1007.1 963.6 %reduce-scatter.30.cloned.1.call-start = ((), (), s32[]{:S(2)}) async-start(), calls=%async_computation.31 | async-start | bytes 18874368 | tf_op jit(solution)/shard_map/reduce_scatter | solution.py:199
  1022.5 1234.4 %reduce-scatter.32.cloned.1.call-start = ((), (), s32[]{:S(2)}) async-start(), calls=%async_computation.32 | async-start | bytes 18874368 | tf_op jit(solution)/shard_map/reduce_scatter | solution.py:200
  (42 other events, 1247.9 us)
Sparse Core Ops, SparseCore 0:
  10.1 43.0 all-gather.17
  55.4 33.3 all-gather.13
  90.9 49.2 all-gather.19
  142.2 38.6 all-gather.15
  182.8 49.8 all-gather.21
  240.3 69.9 reduce-scatter.11
  312.6 124.9 all-gather.25
  439.8 32.6 all-gather.23
  474.8 124.9 all-gather.27
  601.3 32.6 all-gather.31
  636.2 125.3 all-gather.29
  811.7 69.8 reduce-scatter.15
  886.8 34.4 all-gather.33
  952.6 71.7 reduce-scatter.17
  1026.9 44.4 reduce-scatter.13
  1075.4 67.7 reduce-scatter.21
  1147.2 66.5 reduce-scatter.23
  1217.9 86.8 reduce-scatter.19
  1309.4 88.2 reduce-scatter.25
  1401.9 282.3 reduce-scatter.27
  1689.1 281.6 reduce-scatter.29
  1975.1 281.6 reduce-scatter.31
where the time goes:
time: 2270 us; the launch traced here: 2260 us
  waiting for transfers between devices  1900 us (84%)
  matrix products  215 us (9%)
  blocking collectives  83.4 us (4%)
  other arithmetic  30.8 us (1%)
    reduce_scatter x1, waiting for transfers between devices, body(): lax.psum_scatter(grad_gate, 'dp', scatter_dimension=0, tiled=True)  287 us
    reduce_scatter x1, waiting for transfers between devices, body(): lax.psum_scatter(grad_up, 'dp', scatter_dimension=0, tiled=True)  287 us
    reduce_scatter x1, waiting for transfers between devices, body(): lax.psum_scatter(grad_down, 'dp', scatter_dimension=1, tiled=True)  286 us
    all_gather x1, waiting for transfers between devices, gather_mlp(): lax.all_gather(w_down, 'dp', axis=1, tiled=True)  128 us
    all_gather x1, waiting for transfers between devices, gather_mlp(): lax.all_gather(w_gate, 'dp', axis=0, tiled=True)  122 us
    all_gather x1, waiting for transfers between devices, gather_mlp(): lax.all_gather(w_up, 'dp', axis=0, tiled=True)  113 us
    reduce_scatter x1, waiting for transfers between devices, body(): lax.psum_scatter(grad_out, 'dp', scatter_dimension=1, tiled=True)  92.9 us
    reduce_scatter x1, waiting for transfers between devices, body(): lax.psum_scatter(grad_query, 'dp', scatter_dimension=0, tiled=True)  91 us
  transfers between devices with their start and end apart: 22, of which 20 were waited for; matrix products, arithmetic and copies ran while one was open for 7% of the time, Pallas kernels for 0%

commit v1 on v0

v1 whole, which is shorter than its diff:
```python
import jax
import jax.numpy as jnp
from jax import lax
from jax.sharding import PartitionSpec as P

HEAD_SIZE = 256
BLK = 128


EPS = 1e-06
THETA = 1000042.0
NEG = -1e30
HIGH = lax.Precision.HIGHEST
F32 = jnp.float32
BF16 = jnp.bfloat16


def tree_tables(parent_row, rows, block_len):
    blocks = parent_row.shape[0]
    nodes = jnp.arange(blocks, dtype=jnp.int32)
    hops = (parent_row[:, None] == nodes[None, :]).astype(F32)
    reach = jnp.eye(blocks, dtype=F32)
    walk = reach
    for hop_count in range(blocks):
        walk = jnp.dot(walk, hops, precision=HIGH)
        reach = jnp.maximum(reach, walk)
    depth = jnp.sum(reach, axis=1) - 1.0
    member = (rows[:, None] // block_len == nodes[None, :]).astype(F32)
    visible = jnp.dot(jnp.dot(member, reach, precision=HIGH), member.T, precision=HIGH) > 0.5
    allowed_mask = visible & (rows[None, :] <= rows[:, None])
    place = jnp.dot(member, depth, precision=HIGH) * block_len + (rows % block_len).astype(F32)
    return (allowed_mask, place)


def rope_tables(place, head_dim):
    half = head_dim // 2
    freq = THETA ** (-2.0 * jnp.arange(half, dtype=F32) / head_dim)
    angle = place[:, None] * freq[None, :]
    cosine_table = jnp.cos(angle)
    sine_table = jnp.sin(angle)
    return (
        jnp.concatenate([cosine_table, cosine_table], -1),
        jnp.concatenate([sine_table, sine_table], -1),
    )


def apply_rotation(values, cosine_table, sine_table, sign):
    half = values.shape[-1] // 2
    turned = jnp.concatenate([-values[..., half:], values[..., :half]], -1)
    return values * cosine_table[:, None, :] + sign * turned * sine_table[:, None, :]


def normalize(values):
    inverse = lax.rsqrt(jnp.mean(values * values, axis=-1, keepdims=True) + EPS)
    return (values * inverse, inverse)


def norm_back(grad_normed, gain, scaled, inverse):
    grad_scaled = grad_normed * gain
    inner = jnp.mean(grad_scaled * scaled, axis=-1, keepdims=True)
    return inverse * (grad_scaled - scaled * inner)


def dot_nn(left, right):
    return jnp.dot(left, right, preferred_element_type=F32)


def dot_nt(left, right):
    return lax.dot_general(left, right, (((1,), (1,)), ((), ())), preferred_element_type=F32)


def dot_tn(left, right):
    return lax.dot_general(left, right, (((0,), (0,)), ((), ())), preferred_element_type=F32)


def after(value, *earlier):
    return lax.optimization_barrier((value,) + earlier)[0]


def make_body(dp, tp):
    devices = dp * tp
    outer = dp // 2
    assert tp == 4 and dp == 2 * outer and outer & (outer - 1) == 0
    X = tp

    def swap(value, mask):
        return lax.ppermute(value, ("dp", "tensor"), [(i, i ^ mask) for i in range(devices)])

    def zmask(k):
        return k * 2 * tp

    def relative(value, zi):
        width = value.shape[-1] // outer
        step = 1
        while step < outer:
            blocks = [value[..., i * width : (i + 1) * width] for i in range(outer)]
            swapped = jnp.concatenate([blocks[i ^ step] for i in range(outer)], -1)
            value = jnp.where((zi // step) % 2 == 1, swapped, value)
            step *= 2
        return value

    def gather_tensor(a0):
        a1 = swap(a0, 1)
        a2 = swap(a0, 2)
        a3 = swap(a2, 1)
        return [a0, a1, a2, a3]

    def gather_units(a0):
        rows = a0.shape[0] // 2
        ay = swap(a0, 2)
        ax = swap(a0, X)
        d0 = swap(ax[:rows], 2)
        d1 = swap(ay[rows:], X)
        axy = jnp.concatenate([d0, d1], 0)
        even = [a0, ay, ax, axy]
        odd = [swap(e, 1) for e in even]
        return [even[0], odd[0], even[1], odd[1], even[2], odd[2], even[3], odd[3]]

    def scatter_tensor(part):
        b = part.astype(BF16)
        got = swap(jnp.stack([b[1], b[3]]), 1).astype(F32)
        own = part[0] + got[0]
        far = (part[2] + got[1]).astype(BF16)
        return own + swap(far, 2).astype(F32)

    def scatter_units(part):
        rows = part.shape[1] // 2
        got = swap(jnp.stack([part[1], part[3], part[5], part[7]]), 1).astype(F32)
        s0 = part[0].astype(F32) + got[0]
        sy = part[2].astype(F32) + got[1]
        sx = part[4].astype(F32) + got[2]
        sxy = (part[6].astype(F32) + got[3]).astype(BF16)
        top = swap(sxy[:rows], X).astype(F32)
        bottom = swap(sxy[rows:], 2).astype(F32)
        sy = jnp.concatenate([sy[:rows] + top, sy[rows:]], 0).astype(BF16)
        sx = jnp.concatenate([sx[:rows], sx[rows:] + bottom], 0).astype(BF16)
        return s0 + swap(sy, 2).astype(F32) + swap(sx, X).astype(F32)

    def body(
        tokens,
        parents,
        attn_gain,
        w_query,
        key_matrix,
        value_matrix,
        w_out,
        mlp_gain,
        w_gate,
        w_up,
        w_down,
        cotangent,
    ):
        di = lax.axis_index("dp")
        ti = lax.axis_index("tensor")
        zi = di // 2
        upper_x = di % 2 == 1
        rows, model = tokens.shape
        tree_len = rows * tp
        q_width = w_query.shape[1]
        kv_width = key_matrix.shape[1]
        local_q = q_width // HEAD_SIZE
        local_kv = kv_width // HEAD_SIZE
        group = local_q // local_kv
        qkv_width = q_width + 2 * kv_width
        shard = w_query.shape[0]
        units = w_gate.shape[1] // 2
        scale = HEAD_SIZE ** (-0.5)

        def order_x(mine, theirs, axis):
            low = jnp.where(upper_x, theirs, mine)
            high = jnp.where(upper_x, mine, theirs)
            return jnp.concatenate([low, high], axis)

        gains = jnp.stack([attn_gain, mlp_gain])
        gains = order_x(gains, swap(gains, X), 1)
        gains = jnp.concatenate([gains] + [swap(gains, zmask(k)) for k in range(1, outer)], 1)
        gain_a = gains[0].astype(F32)
        gain_m = gains[1].astype(F32)

        wa = jnp.concatenate([w_query, key_matrix, value_matrix, w_out.T], 1)
        wa_z = [wa] + [swap(wa, zmask(k)) for k in range(1, outer)]
        wa_x = [swap(w, X) for w in wa_z]
        wa_all = [order_x(a, b, 0) for a, b in zip(wa_z, wa_x)]
        w_qkv = jnp.concatenate([w[:, :qkv_width] for w in wa_all], 0)
        w_o = jnp.concatenate([w[:, qkv_width:] for w in wa_all], 0)

        def halves(w):
            low, high = w[:, :units], w[:, units:]
            return jnp.where(upper_x, high, low), jnp.where(upper_x, low, high)

        def paired(w):
            keep, send = halves(w)
            return order_x(keep, swap(send, X), 0)

        pieces = [paired(w) for w in (w_gate, w_up, w_down.T)]
        started = after((pieces[0], pieces[1]), wa_z[-1])
        pieces = [started[0], started[1], pieces[2]]
        gate_z = [swap(pieces[0], zmask(k)) for k in range(1, outer)]
        up_z = [swap(pieces[1], zmask(k)) for k in range(1, outer)]
        pieces[2] = after(pieces[2], gate_z[-1])
        down_z = [swap(pieces[2], zmask(k)) for k in range(1, outer)]
        gate_w = jnp.concatenate([pieces[0]] + gate_z, 0)
        up_w = jnp.concatenate([pieces[1]] + up_z, 0)
        down_w = jnp.concatenate([pieces[2]] + down_z, 0)

        row_ids = jnp.concatenate(
            [(ti ^ j) * rows + jnp.arange(rows, dtype=jnp.int32) for j in range(tp)]
        )
        allowed_mask, place = tree_tables(parents[0], row_ids, BLK)
        cosine_table, sine_table = rope_tables(place, HEAD_SIZE)
        inputs = relative(tokens, zi).astype(F32)
        scaled_a, inverse_a = normalize(inputs)
        normed_a = (scaled_a * gain_a).astype(BF16)
        normed_all = jnp.concatenate(gather_tensor(normed_a), 0)
        qkv = dot_nn(normed_all, w_qkv)
        query_rows = apply_rotation(
            qkv[:, :q_width].reshape(tree_len, local_q, HEAD_SIZE), cosine_table, sine_table, 1.0
        ).astype(BF16)
        key = apply_rotation(
            qkv[:, q_width : q_width + kv_width].reshape(tree_len, local_kv, HEAD_SIZE),
            cosine_table,
            sine_table,
            1.0,
        ).astype(BF16)
        value_rows = qkv[:, q_width + kv_width :].reshape(tree_len, local_kv, HEAD_SIZE)
        value_rows = value_rows.astype(BF16)
        grouped = query_rows.reshape(tree_len, local_kv, group, HEAD_SIZE)
        raw = jnp.einsum("qkgd,skd->kgqs", grouped, key, preferred_element_type=F32)
        scores = jnp.where(allowed_mask[None, None], raw * scale, NEG)
        top = jnp.max(scores, axis=-1, keepdims=True)
        weights = jnp.exp(scores - top)
        total = jnp.sum(weights, axis=-1, keepdims=True)
        probs = (weights / total).astype(BF16)
        attended = jnp.einsum("kgqs,skd->qkgd", probs, value_rows, preferred_element_type=F32)
        attended = attended.reshape(tree_len, q_width).astype(BF16)
        mixed = inputs + scatter_tensor(dot_nt(attended, w_o).reshape(tp, rows, model))

        scaled_m, inverse_m = normalize(mixed)
        normed_m = (scaled_m * gain_m).astype(BF16)
        normed_m_all = jnp.concatenate(gather_units(normed_m), 0)
        cot = relative(cotangent, zi)
        cot_all = jnp.concatenate(gather_units(cot), 0)
        gate = dot_nn(normed_m_all, gate_w)
        upper = dot_nn(normed_m_all, up_w)
        sigma = jax.nn.sigmoid(gate)
        swish = gate * sigma
        hidden = (swish * upper).astype(BF16)
        grad_down = dot_tn(cot_all, hidden).astype(BF16)

        grad_hidden = dot_nn(cot_all, down_w)
        grad_gate_act = (grad_hidden * upper * sigma * (1.0 + gate * (1.0 - sigma))).astype(BF16)
        grad_up_act = (grad_hidden * swish).astype(BF16)
        grad_normed_m = scatter_units(
            (dot_nt(grad_gate_act, gate_w) + dot_nt(grad_up_act, up_w))
            .astype(BF16)
            .reshape(2 * tp, rows, model)
        )
        grad_mixed = cot.astype(F32) + norm_back(grad_normed_m, gain_m, scaled_m, inverse_m)
        grad_gate = dot_tn(normed_m_all, grad_gate_act).astype(BF16)
        grad_up = dot_tn(normed_m_all, grad_up_act).astype(BF16)
        mlp_part = dot_nt(hidden, down_w).astype(BF16).reshape(2 * tp, rows, model)
        output = relative((mixed + scatter_units(mlp_part)).astype(BF16), zi)

        def reduce_z(grad):
            block = grad.reshape(outer, 2 * shard, grad.shape[1])
            total = block[0].astype(F32)
            for k in range(1, outer):
                total = total + swap(block[k], zmask(k)).astype(F32)
            return total

        def unpaired(grad):
            s = reduce_z(grad)
            keep = jnp.where(upper_x, s[shard:], s[:shard])
            send = jnp.where(upper_x, s[:shard], s[shard:]).astype(BF16)
            return order_x(keep, swap(send, X).astype(F32), 1)

        grad_down = unpaired(grad_down)
        grad_gate = unpaired(grad_gate)
        grad_up = unpaired(grad_up)

        grad_mixed_all = jnp.concatenate(gather_tensor(grad_mixed.astype(BF16)), 0)
        grad_attended = dot_nn(grad_mixed_all, w_o).astype(BF16)
        grad_grouped = grad_attended.reshape(tree_len, local_kv, group, HEAD_SIZE)
        grad_value_act = jnp.einsum(
            "kgqs,qkgd->skd", probs, grad_grouped, preferred_element_type=F32
        )
        grad_probs = jnp.einsum(
            "qkgd,skd->kgqs", grad_grouped, value_rows, preferred_element_type=F32
        )
        probs_full = probs.astype(F32)
        inner = jnp.sum(probs_full * grad_probs, axis=-1, keepdims=True)
        grad_scores = (probs_full * (grad_probs - inner) * scale).astype(BF16)
        grad_query_rot = jnp.einsum(
            "kgqs,skd->qkgd", grad_scores, key, preferred_element_type=F32
        )
        grad_key_rot = jnp.einsum(
            "kgqs,qkgd->skd", grad_scores, grouped, preferred_element_type=F32
        )
        grad_query_act = apply_rotation(
            grad_query_rot.reshape(tree_len, local_q, HEAD_SIZE), cosine_table, sine_table, -1.0
        )
        grad_key_act = apply_rotation(grad_key_rot, cosine_table, sine_table, -1.0)
        grad_qkv = jnp.concatenate(
            [
                grad_query_act.astype(BF16).reshape(tree_len, q_width),
                grad_key_act.astype(BF16).reshape(tree_len, kv_width),
                grad_value_act.astype(BF16).reshape(tree_len, kv_width),
            ],
            1,
        )
        grad_normed_a = scatter_tensor(dot_nt(grad_qkv, w_qkv).reshape(tp, rows, model))
        grad_input = norm_back(grad_normed_a, gain_a, scaled_a, inverse_a)
        grad_tokens = relative((grad_mixed + grad_input).astype(BF16), zi)
        grad_wa = jnp.concatenate(
            [
                dot_tn(normed_all, grad_qkv).astype(BF16),
                dot_tn(grad_mixed_all, attended).astype(BF16),
            ],
            1,
        ).reshape(outer, 2, shard, qkv_width + q_width)
        keep = jnp.where(upper_x, grad_wa[:, 1], grad_wa[:, 0])
        send = jnp.where(upper_x, grad_wa[:, 0], grad_wa[:, 1])
        pair_sum = keep.astype(F32) + swap(send, X).astype(F32)
        far = pair_sum.astype(BF16)
        total_a = pair_sum[0]
        for k in range(1, outer):
            total_a = total_a + swap(far[k], zmask(k)).astype(F32)
        grad_query = total_a[:, :q_width]
        grad_key = total_a[:, q_width : q_width + kv_width]
        grad_value = total_a[:, q_width + kv_width : qkv_width]
        grad_out = total_a[:, qkv_width:].T

        gain_sum_a = (
            jnp.sum(w_query.astype(F32) * grad_query, 1)
            + jnp.sum(key_matrix.astype(F32) * grad_key, 1)
            + jnp.sum(value_matrix.astype(F32) * grad_value, 1)
        )
        gain_sum_m = jnp.sum(w_gate.astype(F32) * grad_gate, 1) + jnp.sum(
            w_up.astype(F32) * grad_up, 1
        )

        def sum_tensor(v):
            v = v + swap(v, 1)
            return v + swap(v, 2)

        grad_attn_gain = sum_tensor(gain_sum_a) / attn_gain.astype(F32)
        grad_mlp_gain = sum_tensor(gain_sum_m) / mlp_gain.astype(F32)
        return (
            output,
            grad_tokens,
            grad_attn_gain,
            grad_query,
            grad_key,
            grad_value,
            grad_out,
            grad_mlp_gain,
            grad_gate,
            grad_up,
            grad_down.T,
        )

    return body


def solution(mesh):
    in_specs = (
        P(("dp", "tensor"), None),
        P("dp", None),
        P("dp"),
        P("dp", "tensor"),
        P("dp", "tensor"),
        P("dp", "tensor"),
        P("tensor", "dp"),
        P("dp"),
        P("dp", "tensor"),
        P("dp", "tensor"),
        P("tensor", "dp"),
        P(("dp", "tensor"), None),
    )
    out_specs = (
        P(("dp", "tensor"), None),
        P(("dp", "tensor"), None),
        P("dp"),
        P("dp", "tensor"),
        P("dp", "tensor"),
        P("dp", "tensor"),
        P("tensor", "dp"),
        P("dp"),
        P("dp", "tensor"),
        P("dp", "tensor"),
        P("tensor", "dp"),
    )
    body = make_body(mesh.shape["dp"], mesh.shape["tensor"])
    return jax.shard_map(body, mesh=mesh, in_specs=in_specs, out_specs=out_specs, check_vma=False)
```

time: 2270 us -> 1110 us (0.49)
  waiting for transfers between devices: 1900 us -> 618 us
  starting transfers between devices: 0.88 us -> 103 us
  local copies, waits for them, and re-layouts: 13.7 us -> 99.8 us
  blocking collectives: 83.4 us -> 0 us
  other arithmetic: 30.8 us -> 103 us
  matrix products: 215 us -> 175 us
    reduce_scatter x11 -> x0, waiting for transfers between devices: 1290 us -> none  [the longest x1 287 us: body(): lax.psum_scatter(grad_gate, 'dp', scatter_dimension=0, tiled=True)]
    ppermute x0 -> x79, waiting for transfers between devices: none -> 618 us  [swap(): lax.ppermute(value, ('dp', 'tensor'), [(i, i ^ mask) for i in range(devic...]
    all_gather x11 -> x0, waiting for transfers between devices: 613 us -> none  [the longest x1 128 us: gather_mlp(): lax.all_gather(w_down, 'dp', axis=1, tiled=True)]
    ppermute x0 -> x79, starting transfers between devices: none -> 103 us  [swap(): lax.ppermute(value, ('dp', 'tensor'), [(i, i ^ mask) for i in range(devic...]
    unnamed x93 -> x275, local copies, waits for them, and re-layouts: 11.7 us -> 55 us
    all_gather x2 -> x0, blocking collectives: 39.9 us -> none  [the longest x1 22.2 us: gather_attention(): lax.all_gather(attn_gain, 'dp', axis=0, tiled=True)]
    dot_general x25 -> x19, matrix products: 203 us -> 164 us  [the longest x5 63.7 us: dot_nn(): return jnp.dot(left, right, preferred_element_type=F32)]
    unnamed x1 -> x0, blocking collectives: 37.2 us -> none
  transfers between devices with their start and end apart: 22 -> 79, of which waited for: 20 -> 26; matrix products, arithmetic and copies ran while one was open for 7% -> 26% of each run, Pallas kernels for 0% -> 0%
where the time goes in v1:
time: 1110 us; the launch traced here: 1100 us
  waiting for transfers between devices  618 us (56%)
  matrix products  175 us (16%)
  other arithmetic  103 us (9%)
  starting transfers between devices  103 us (9%)
  local copies, waits for them, and re-layouts  99.8 us (9%)
    ppermute x79, waiting for transfers between devices, swap(): lax.ppermute(value, ('dp', 'tensor'), [(i, i ^ mask) for i in range(devic...  618 us
    ppermute x79, starting transfers between devices, swap(): lax.ppermute(value, ('dp', 'tensor'), [(i, i ^ mask) for i in range(devic...  103 us
    dot_general x5, matrix products, dot_nn(): return jnp.dot(left, right, preferred_element_type=F32)  63.7 us
    unnamed x275, local copies, waits for them, and re-layouts  55 us
    dot_general x5, matrix products, dot_tn(): lax.dot_general(left, right, (((0,), (0,)), ((), ())), preferred_element_...  47.3 us
    dot_general x5, matrix products, dot_nt(): lax.dot_general(left, right, (((1,), (1,)), ((), ())), preferred_element_...  46.1 us
  transfers between devices with their start and end apart: 79, of which 26 were waited for; matrix products, arithmetic and copies ran while one was open for 26% of the time, Pallas kernels for 0%

profile of v1, /device:TPU:0, one launch (start us, length us, event | category | flops | bytes accessed | tf_op | source)
XLA Modules:
  0.0 1102.1 jit_solution(389019918434119606)
XLA Ops:
  73.5 17.2 %collective-permute-done.10 = bf16[256,1536]{0,1:T(8,128)(2,1)S(1)} collective-permute-done((bf16[256,1536]{0,1:T(8,128)(2,1)}, bf16[256,1536]{0,1:T(8,128)(2,1)S(1)}, u32[]{:S(2)}, u32[]{:S(2)}) %collective-permute-start.10) | collective-permute-done | bytes 786464 | tf_op jit(solution)/shard_map/ppermute | solution.py:87
  92.2 16.6 %collective-permute-done.9 = bf16[256,1536]{0,1:T(8,128)(2,1)S(1)} collective-permute-done((bf16[256,1536]{0,1:T(8,128)(2,1)}, bf16[256,1536]{0,1:T(8,128)(2,1)S(1)}, u32[]{:S(2)}, u32[]{:S(2)}) %collective-permute-start.9) | collective-permute-done | bytes 786464 | tf_op jit(solution)/shard_map/ppermute | solution.py:87
  111.7 13.9 %collective-permute-done.13 = bf16[256,1536]{0,1:T(8,128)(2,1)S(1)} collective-permute-done((bf16[256,1536]{0,1:T(8,128)(2,1)}, bf16[256,1536]{0,1:T(8,128)(2,1)S(1)}, u32[]{:S(2)}, u32[]{:S(2)}) %collective-permute-start.13) | collective-permute-done | bytes 786464 | tf_op jit(solution)/shard_map/ppermute | solution.py:87
  201.8 18.9 %collective-permute-start.29 = (bf16[512,1024]{0,1:T(8,128)(2,1)S(1)}, bf16[512,1024]{0,1:T(8,128)(2,1)S(1)}, u32[]{:S(2)}, u32[]{:S(2)}) collective-permute-start(bf16[512,1024]{0,1:T(8,128)(2,1)S(1)} %get-tuple-element.15), channel_id=1, source_target_pairs={{0,8},{1,9},{2,10},{3,11},{4,12},{5,13},{6,14},{7,15},{8,0},{9,1},... | collective-permute-start | bytes 3145736 | tf_op jit(solution)/shard_map/ppermute | solution.py:87
  228.2 59.4 %collective-permute-done.27 = bf16[512,1024]{0,1:T(8,128)(2,1)S(1)} collective-permute-done((bf16[512,1024]{0,1:T(8,128)(2,1)S(1)}, bf16[512,1024]{0,1:T(8,128)(2,1)S(1)}, u32[]{:S(2)}, u32[]{:S(2)}) %collective-permute-start.27) | collective-permute-done | bytes 1048608 | tf_op jit(solution)/shard_map/ppermute | solution.py:87
  292.0 62.0 %collective-permute-done.30 = bf16[512,1024]{0,1:T(8,128)(2,1)S(1)} collective-permute-done((bf16[512,1024]{0,1:T(8,128)(2,1)S(1)}, bf16[512,1024]{0,1:T(8,128)(2,1)S(1)}, u32[]{:S(2)}, u32[]{:S(2)}) %collective-permute-start.30) | collective-permute-done | bytes 1048608 | tf_op jit(solution)/shard_map/ppermute | solution.py:87
  368.3 55.6 %collective-permute-done.33 = bf16[512,1024]{0,1:T(8,128)(2,1)S(1)} collective-permute-done((bf16[512,1024]{0,1:T(8,128)(2,1)S(1)}, bf16[512,1024]{0,1:T(8,128)(2,1)S(1)}, u32[]{:S(2)}, u32[]{:S(2)}) %collective-permute-start.33) | collective-permute-done | bytes 1048608 | tf_op jit(solution)/shard_map/ppermute | solution.py:87
  424.0 21.3 %collective-permute-done.34 = bf16[512,1024]{0,1:T(8,128)(2,1)S(1)} collective-permute-done((bf16[512,1024]{0,1:T(8,128)(2,1)S(1)}, bf16[512,1024]{0,1:T(8,128)(2,1)S(1)}, u32[]{:S(2)}, u32[]{:S(2)}) %collective-permute-start.34) | collective-permute-done | bytes 1048608 | tf_op jit(solution)/shard_map/ppermute | solution.py:87
  447.2 13.4 %fusion.146 = f32[2048,1024]{1,0:T(8,128)} fusion(bf16[2048,2048]{1,0:T(8,128)(2,1)} %constant_dynamic-update-slice_fusion.26, bf16[2048,1024]{0,1:T(8,128)(2,1)S(1)} %constant_dynamic-update-slice_fusion.22), kind=kOutput, calls=%fused_computation.368 | convolution fusion | flops 8589934592 | bytes 20971520 | tf_op jit(solution)/shard_map/dot_general | solution.py:65
  469.3 13.2 %fusion.145 = f32[2048,1024]{1,0:T(8,128)} fusion(bf16[2048,2048]{1,0:T(8,128)(2,1)} %constant_dynamic-update-slice_fusion.5, bf16[2048,1024]{0,1:T(8,128)(2,1)S(1)} %constant_dynamic-update-slice_fusion.18), kind=kOutput, calls=%fused_computation.367 | convolution fusion | flops 8589934592 | bytes 20971520 | tf_op jit(solution)/shard_map/dot_general | solution.py:65
  482.6 24.2 %multiply_convert_fusion.1 = (bf16[2048,1024]{1,0:T(8,128)(2,1)}, bf16[2048,1024]{1,0:T(8,128)(2,1)}, bf16[2048,1024]{1,0:T(8,128)(2,1)}) fusion(f32[2048,1024]{1,0:T(8,128)} %fusion.146, f32[2048,1024]{1,0:T(8,128)} %fusion.145, bf16[2048,2048]{1,0:T(8,128)(2,1)} %constant_dynamic-update-slice_fusion.5, bf16[2048,1024]{0,1:T(8,128)(2,1)} %copy-done.81), kind=kOutput, calls=%fused_computation.9 | convolution fusion | flops 8621391872 | bytes 41943040 | tf_op jit(solution)/shard_map/dot_general | solution.py:65
  506.8 14.1 %convolution_convert_fusion.2 = bf16[2048,1024]{0,1:T(8,128)(2,1)} fusion(bf16[2048,2048]{1,0:T(8,128)(2,1)} %constant_dynamic-update-slice_fusion.26, bf16[2048,1024]{1,0:T(8,128)(2,1)} %get-tuple-element.51), kind=kOutput, calls=%fused_computation.32 | convolution fusion | flops 8592031744 | bytes 16777216 | tf_op jit(solution)/shard_map/dot_general | solution.py:73
  538.2 11.7 %fusion.147 = f32[2048,2048]{1,0:T(8,128)} fusion(bf16[2048,1024]{1,0:T(8,128)(2,1)S(1)} %copy-done.112, bf16[2048,1024]{0,1:T(8,128)(2,1)S(1)} %copy-done.80), kind=kOutput, calls=%fused_computation.369 | convolution fusion | flops 8589934592 | bytes 25165824 | tf_op jit(solution)/shard_map/dot_general | solution.py:69
  549.9 14.3 %add_convert_fusion = bf16[2048,2048]{1,0:T(8,128)(2,1)S(1)} fusion(f32[2048,2048]{1,0:T(8,128)} %fusion.147, bf16[2048,1024]{1,0:T(8,128)(2,1)} %get-tuple-element.49, bf16[2048,1024]{0,1:T(8,128)(2,1)} %copy-done.81), kind=kOutput, calls=%fused_computation | convolution fusion | flops 8598323200 | bytes 33554432 | tf_op jit(solution)/shard_map/dot_general | solution.py:69
  567.6 13.1 %convolution_convert_fusion.3 = bf16[2048,1024]{0,1:T(8,128)(2,1)S(1)} fusion(bf16[2048,2048]{1,0:T(8,128)(2,1)} %constant_dynamic-update-slice_fusion.5, bf16[2048,1024]{1,0:T(8,128)(2,1)} %get-tuple-element.50), kind=kOutput, calls=%fused_computation.33 | convolution fusion | flops 8592031744 | bytes 16777216 | tf_op jit(solution)/shard_map/dot_general | solution.py:73
  587.9 13.0 %convolution_convert_fusion.4 = bf16[2048,1024]{0,1:T(8,128)(2,1)S(1)} fusion(bf16[2048,2048]{1,0:T(8,128)(2,1)} %constant_dynamic-update-slice_fusion.5, bf16[2048,1024]{1,0:T(8,128)(2,1)} %get-tuple-element.49), kind=kOutput, calls=%fused_computation.34 | convolution fusion | flops 8592031744 | bytes 16777216 | tf_op jit(solution)/shard_map/dot_general | solution.py:73
  650.8 25.8 %collective-permute-done.76 = bf16[512,1024]{0,1:T(8,128)(2,1)} collective-permute-done((bf16[512,1024]{0,1:T(8,128)(2,1)}, bf16[512,1024]{0,1:T(8,128)(2,1)}, u32[]{:S(2)}, u32[]{:S(2)}) %collective-permute-start.76) | collective-permute-done | bytes 1048608 | tf_op jit(solution)/shard_map/ppermute | solution.py:87
  686.1 30.2 %collective-permute-done.69 = bf16[512,1024]{0,1:T(8,128)(2,1)S(1)} collective-permute-done((bf16[512,1024]{0,1:T(8,128)(2,1)S(1)}, bf16[512,1024]{0,1:T(8,128)(2,1)S(1)}, u32[]{:S(2)}, u32[]{:S(2)}) %collective-permute-start.69) | collective-permute-done | bytes 1048608 | tf_op jit(solution)/shard_map/ppermute | solution.py:87
  724.7 95.9 %collective-permute-done.70 = bf16[512,1024]{0,1:T(8,128)(2,1)} collective-permute-done((bf16[512,1024]{0,1:T(8,128)(2,1)}, bf16[512,1024]{0,1:T(8,128)(2,1)}, u32[]{:S(2)}, u32[]{:S(2)}) %collective-permute-start.70) | collective-permute-done | bytes 1048608 | tf_op jit(solution)/shard_map/ppermute | solution.py:87
  825.0 37.9 %collective-permute-done.66 = bf16[512,1024]{0,1:T(8,128)(2,1)} collective-permute-done((bf16[512,1024]{0,1:T(8,128)(2,1)}, bf16[512,1024]{0,1:T(8,128)(2,1)}, u32[]{:S(2)}, u32[]{:S(2)}) %collective-permute-start.66) | collective-permute-done | bytes 1048608 | tf_op jit(solution)/shard_map/ppermute | solution.py:87
  929.1 12.4 %fusion.128 = (bf16[4,1,256,1536]{2,1,0,3:T(2,128)(2,1)S(1)}, bf16[4,1,256,1536]{2,1,0,3:T(2,128)(2,1)S(1)}) fusion(bf16[4,2,256,1536]{2,1,0,3:T(2,128)(2,1)} %reshape.448), kind=kLoop, calls=%fused_computation.350 | loop fusion | bytes 12582912 | tf_op jit(solution)/shard_map/slice | solution.py:321
  968.5 50.4 %collective-permute-done.59 = bf16[4,256,1536]{1,2,0:T(8,128)(2,1)} collective-permute-done((bf16[4,256,1536]{1,2,0:T(8,128)(2,1)}, bf16[4,256,1536]{1,2,0:T(8,128)(2,1)}, u32[]{:S(2)}, u32[]{:S(2)}) %collective-permute-start.59) | collective-permute-done | bytes 3145760 | tf_op jit(solution)/shard_map/ppermute | solution.py:87
  1032.3 26.4 %collective-permute-done.60 = bf16[256,1536]{0,1:T(8,128)(2,1)S(1)} collective-permute-done((bf16[256,1536]{0,1:T(8,128)(2,1)S(1)}, bf16[256,1536]{0,1:T(8,128)(2,1)S(1)}, u32[]{:S(2)}, u32[]{:S(2)}) %collective-permute-start.60) | collective-permute-done | bytes 786464 | tf_op jit(solution)/shard_map/ppermute | solution.py:87
  1060.0 34.1 %collective-permute-done.61 = bf16[256,1536]{0,1:T(8,128)(2,1)S(1)} collective-permute-done((bf16[256,1536]{0,1:T(8,128)(2,1)S(1)}, bf16[256,1536]{0,1:T(8,128)(2,1)S(1)}, u32[]{:S(2)}, u32[]{:S(2)}) %collective-permute-start.61) | collective-permute-done | bytes 786464 | tf_op jit(solution)/shard_map/ppermute | solution.py:87
  (587 shorter events, 403.7 us)
Async XLA Ops:
  65.9 104.9 %collective-permute-start.44 = (bf16[256,2048]{1,0:T(8,128)(2,1)S(1)}, bf16[256,2048]{1,0:T(8,128)(2,1)S(1)}, u32[]{:S(2)}, u32[]{:S(2)}) collective-permute-start(bf16[256,2048]{1,0:T(8,128)(2,1)S(1)} %copy-done.33), channel_id=1, source_target_pairs={{0,4},{1,5},{2,6},{3,7},{4,0},{5,1},{6,2},{7,3},{8,12},{9,13},{10,... | collective-permute-start | bytes 3145736 | tf_op jit(solution)/shard_map/ppermute | solution.py:87
  69.0 107.2 %collective-permute-start.42 = (bf16[256,2048]{1,0:T(8,128)(2,1)S(1)}, bf16[256,2048]{1,0:T(8,128)(2,1)S(1)}, u32[]{:S(2)}, u32[]{:S(2)}) collective-permute-start(bf16[256,2048]{1,0:T(8,128)(2,1)S(1)} %copy-done.33), channel_id=1, source_target_pairs={{0,2},{1,3},{2,0},{3,1},{4,6},{5,7},{6,4},{7,5},{8,10},{9,11},{10,... | collective-permute-start | bytes 3145736 | tf_op jit(solution)/shard_map/ppermute | solution.py:87
  169.5 118.5 %collective-permute-start.14 = (bf16[2,256,2048]{2,1,0:T(8,128)(2,1)S(1)}, bf16[2,256,2048]{2,1,0:T(8,128)(2,1)S(1)}, u32[]{:S(2)}, u32[]{:S(2)}) collective-permute-start(bf16[2,256,2048]{2,1,0:T(8,128)(2,1)S(1)} %pad_maximum_fusion.10), channel_id=1, source_target_pairs={{0,1},{1,0},{2,3},{3,2},{4,5},{5,4},{6,7},{7,6},{8,9},{9,8},{10,11... | collective-permute-start | bytes 6291464 | tf_op jit(solution)/shard_map/ppermute | solution.py:87
  176.5 111.1 %collective-permute-start.27 = (bf16[512,1024]{0,1:T(8,128)(2,1)S(1)}, bf16[512,1024]{0,1:T(8,128)(2,1)S(1)}, u32[]{:S(2)}, u32[]{:S(2)}) collective-permute-start(bf16[512,1024]{0,1:T(8,128)(2,1)S(1)} %get-tuple-element.14), channel_id=1, source_target_pairs={{0,16},{1,17},{2,18},{3,19},{4,20},{5,21},{6,22},{7,23},{8,24},{9,... | collective-permute-start | bytes 3145736 | tf_op jit(solution)/shard_map/ppermute | solution.py:87
  198.2 156.0 %collective-permute-start.31 = (bf16[512,1024]{0,1:T(8,128)(2,1)S(1)}, bf16[512,1024]{0,1:T(8,128)(2,1)S(1)}, u32[]{:S(2)}, u32[]{:S(2)}) collective-permute-start(bf16[512,1024]{0,1:T(8,128)(2,1)S(1)} %get-tuple-element.15), channel_id=1, source_target_pairs={{0,24},{1,25},{2,26},{3,27},{4,28},{5,29},{6,30},{7,31},{8,16},{9,... | collective-permute-start | bytes 3145736 | tf_op jit(solution)/shard_map/ppermute | solution.py:87
  201.8 89.4 %collective-permute-start.29 = (bf16[512,1024]{0,1:T(8,128)(2,1)S(1)}, bf16[512,1024]{0,1:T(8,128)(2,1)S(1)}, u32[]{:S(2)}, u32[]{:S(2)}) collective-permute-start(bf16[512,1024]{0,1:T(8,128)(2,1)S(1)} %get-tuple-element.15), channel_id=1, source_target_pairs={{0,8},{1,9},{2,10},{3,11},{4,12},{5,13},{6,14},{7,15},{8,0},{9,1},... | collective-permute-start | bytes 3145736 | tf_op jit(solution)/shard_map/ppermute | solution.py:87
  224.9 129.1 %collective-permute-start.30 = (bf16[512,1024]{0,1:T(8,128)(2,1)S(1)}, bf16[512,1024]{0,1:T(8,128)(2,1)S(1)}, u32[]{:S(2)}, u32[]{:S(2)}) collective-permute-start(bf16[512,1024]{0,1:T(8,128)(2,1)S(1)} %get-tuple-element.15), channel_id=1, source_target_pairs={{0,16},{1,17},{2,18},{3,19},{4,20},{5,21},{6,22},{7,23},{8,24},{9,... | collective-permute-start | bytes 3145736 | tf_op jit(solution)/shard_map/ppermute | solution.py:87
  287.6 68.3 %collective-permute-start.43 = (bf16[256,2048]{1,0:T(8,128)(2,1)S(1)}, bf16[256,2048]{1,0:T(8,128)(2,1)S(1)}, u32[]{:S(2)}, u32[]{:S(2)}) collective-permute-start(bf16[256,2048]{1,0:T(8,128)(2,1)S(1)} %collective-permute-done.42), channel_id=1, source_target_pairs={{0,1},{1,0},{2,3},{3,2},{4,5},{5,4},{6,7},{7,6},{8,9},{9,8},{10,11... | collective-permute-start | bytes 3145736 | tf_op jit(solution)/shard_map/ppermute | solution.py:87
  289.9 68.6 %collective-permute-start.45 = (bf16[256,2048]{1,0:T(8,128)(2,1)S(1)}, bf16[256,2048]{1,0:T(8,128)(2,1)S(1)}, u32[]{:S(2)}, u32[]{:S(2)}) collective-permute-start(bf16[256,2048]{1,0:T(8,128)(2,1)S(1)} %collective-permute-done.44), channel_id=1, source_target_pairs={{0,1},{1,0},{2,3},{3,2},{4,5},{5,4},{6,7},{7,6},{8,9},{9,8},{10,11... | collective-permute-start | bytes 3145736 | tf_op jit(solution)/shard_map/ppermute | solution.py:87
  291.3 70.8 %collective-permute-start.15 = (bf16[256,2048]{1,0:T(8,128)(2,1)S(1)}, bf16[256,2048]{1,0:T(8,128)(2,1)S(1)}, u32[]{:S(2)}, u32[]{:S(2)}) collective-permute-start(bf16[256,2048]{1,0:T(8,128)(2,1)S(1)} %fusion.48), channel_id=1, source_target_pairs={{0,2},{1,3},{2,0},{3,1},{4,6},{5,7},{6,4},{7,5},{8,10},{9,11},{10,... | collective-permute-start | bytes 3145736 | tf_op jit(solution)/shard_map/ppermute | solution.py:87
  354.2 91.3 %collective-permute-start.35 = (bf16[512,1024]{0,1:T(8,128)(2,1)S(1)}, bf16[512,1024]{0,1:T(8,128)(2,1)S(1)}, u32[]{:S(2)}, u32[]{:S(2)}) collective-permute-start(bf16[512,1024]{0,1:T(8,128)(2,1)S(1)} %pad_maximum_fusion.20), channel_id=1, source_target_pairs={{0,24},{1,25},{2,26},{3,27},{4,28},{5,29},{6,30},{7,31},{8,16},{9,... | collective-permute-start | bytes 3145736 | tf_op jit(solution)/shard_map/ppermute | solution.py:87
  355.9 89.4 %collective-permute-start.34 = (bf16[512,1024]{0,1:T(8,128)(2,1)S(1)}, bf16[512,1024]{0,1:T(8,128)(2,1)S(1)}, u32[]{:S(2)}, u32[]{:S(2)}) collective-permute-start(bf16[512,1024]{0,1:T(8,128)(2,1)S(1)} %pad_maximum_fusion.20), channel_id=1, source_target_pairs={{0,16},{1,17},{2,18},{3,19},{4,20},{5,21},{6,22},{7,23},{8,24},{9,... | collective-permute-start | bytes 3145736 | tf_op jit(solution)/shard_map/ppermute | solution.py:87
  364.3 81.4 %collective-permute-start.19 = (bf16[256,2048]{1,0:T(8,128)(2,1)S(1)}, bf16[256,2048]{1,0:T(8,128)(2,1)S(1)}, u32[]{:S(2)}, u32[]{:S(2)}) collective-permute-start(bf16[256,2048]{1,0:T(8,128)(2,1)S(1)} %get-tuple-element.37), channel_id=1, source_target_pairs={{0,4},{1,5},{2,6},{3,7},{4,0},{5,1},{6,2},{7,3},{8,12},{9,13},{10,... | collective-permute-start | bytes 3145736 | tf_op jit(solution)/shard_map/ppermute | solution.py:87
  365.0 81.3 %collective-permute-start.17 = (bf16[256,2048]{1,0:T(8,128)(2,1)S(1)}, bf16[256,2048]{1,0:T(8,128)(2,1)S(1)}, u32[]{:S(2)}, u32[]{:S(2)}) collective-permute-start(bf16[256,2048]{1,0:T(8,128)(2,1)S(1)} %get-tuple-element.37), channel_id=1, source_target_pairs={{0,2},{1,3},{2,0},{3,1},{4,6},{5,7},{6,4},{7,5},{8,10},{9,11},{10,... | collective-permute-start | bytes 3145736 | tf_op jit(solution)/shard_map/ppermute | solution.py:87
  533.2 77.0 %collective-permute-start.36 = (bf16[4,256,2048]{2,1,0:T(8,128)(2,1)}, bf16[4,256,2048]{2,1,0:T(8,128)(2,1)}, u32[]{:S(2)}, u32[]{:S(2)}) collective-permute-start(bf16[4,256,2048]{2,1,0:T(8,128)(2,1)} %pad_maximum_fusion.3), channel_id=1, source_target_pairs={{0,1},{1,0},{2,3},{3,2},{4,5},{5,4},{6,7},{7,6},{8,9},{9,8},{10,11... | collective-permute-start | bytes 12582920 | tf_op jit(solution)/shard_map/ppermute | solution.py:87
  585.0 91.6 %collective-permute-start.76 = (bf16[512,1024]{0,1:T(8,128)(2,1)}, bf16[512,1024]{0,1:T(8,128)(2,1)}, u32[]{:S(2)}, u32[]{:S(2)}) collective-permute-start(bf16[512,1024]{0,1:T(8,128)(2,1)} %get-tuple-element.67), channel_id=1, source_target_pairs={{0,16},{1,17},{2,18},{3,19},{4,20},{5,21},{6,22},{7,23},{8,24},{9,... | collective-permute-start | bytes 3145736 | tf_op jit(solution)/shard_map/ppermute | solution.py:87
  685.3 135.3 %collective-permute-start.70 = (bf16[512,1024]{0,1:T(8,128)(2,1)}, bf16[512,1024]{0,1:T(8,128)(2,1)}, u32[]{:S(2)}, u32[]{:S(2)}) collective-permute-start(bf16[512,1024]{0,1:T(8,128)(2,1)} %get-tuple-element.70), channel_id=1, source_target_pairs={{0,16},{1,17},{2,18},{3,19},{4,20},{5,21},{6,22},{7,23},{8,24},{9,... | collective-permute-start | bytes 3145736 | tf_op jit(solution)/shard_map/ppermute | solution.py:87
  716.4 107.3 %collective-permute-start.65 = (bf16[512,1024]{0,1:T(8,128)(2,1)}, bf16[512,1024]{0,1:T(8,128)(2,1)}, u32[]{:S(2)}, u32[]{:S(2)}) collective-permute-start(bf16[512,1024]{0,1:T(8,128)(2,1)} %get-tuple-element.71), channel_id=1, source_target_pairs={{0,8},{1,9},{2,10},{3,11},{4,12},{5,13},{6,14},{7,15},{8,0},{9,1},... | collective-permute-start | bytes 3145736 | tf_op jit(solution)/shard_map/ppermute | solution.py:87
  716.4 108.7 %collective-permute-start.67 = (bf16[512,1024]{0,1:T(8,128)(2,1)}, bf16[512,1024]{0,1:T(8,128)(2,1)S(1)}, u32[]{:S(2)}, u32[]{:S(2)}) collective-permute-start(bf16[512,1024]{0,1:T(8,128)(2,1)} %get-tuple-element.72), channel_id=1, source_target_pairs={{0,24},{1,25},{2,26},{3,27},{4,28},{5,29},{6,30},{7,31},{8,16},{9,... | collective-permute-start | bytes 3145736 | tf_op jit(solution)/shard_map/ppermute | solution.py:87
  719.1 143.9 %collective-permute-start.66 = (bf16[512,1024]{0,1:T(8,128)(2,1)}, bf16[512,1024]{0,1:T(8,128)(2,1)}, u32[]{:S(2)}, u32[]{:S(2)}) collective-permute-start(bf16[512,1024]{0,1:T(8,128)(2,1)} %get-tuple-element.73), channel_id=1, source_target_pairs={{0,16},{1,17},{2,18},{3,19},{4,20},{5,21},{6,22},{7,23},{8,24},{9,... | collective-permute-start | bytes 3145736 | tf_op jit(solution)/shard_map/ppermute | solution.py:87
  724.0 227.4 %collective-permute-start.78 = (bf16[256,1024]{0,1:T(8,128)(2,1)}, bf16[256,1024]{0,1:T(8,128)(2,1)S(1)}, u32[]{:S(2)}, u32[]{:S(2)}) collective-permute-start(bf16[256,1024]{0,1:T(8,128)(2,1)} %select_convert_fusion), channel_id=1, source_target_pairs={{0,4},{1,5},{2,6},{3,7},{4,0},{5,1},{6,2},{7,3},{8,12},{9,13},{10,... | collective-permute-start | bytes 1572872 | tf_op jit(solution)/shard_map/ppermute | solution.py:87
  878.6 73.0 %collective-permute-start.73 = (f32[256]{0:T(256)S(1)}, f32[256]{0:T(256)S(1)}, u32[]{:S(2)}, u32[]{:S(2)}) collective-permute-start(f32[256]{0:T(256)S(1)} %add.325), channel_id=1, source_target_pairs={{0,1},{1,0},{2,3},{3,2},{4,5},{5,4},{6,7},{7,6},{8,9},{9,8},{10,11... | collective-permute-start | bytes 3080 | tf_op jit(solution)/shard_map/ppermute | solution.py:87
  948.0 70.8 %collective-permute-start.59 = (bf16[4,256,1536]{1,2,0:T(8,128)(2,1)}, bf16[4,256,1536]{1,2,0:T(8,128)(2,1)}, u32[]{:S(2)}, u32[]{:S(2)}) collective-permute-start(bf16[4,256,1536]{1,2,0:T(8,128)(2,1)} %select_bitcast_fusion), channel_id=1, source_target_pairs={{0,4},{1,5},{2,6},{3,7},{4,0},{5,1},{6,2},{7,3},{8,12},{9,13},{10,... | collective-permute-start | bytes 9437192 | tf_op jit(solution)/shard_map/ppermute | solution.py:87
  1024.8 69.3 %collective-permute-start.61 = (bf16[256,1536]{0,1:T(8,128)(2,1)S(1)}, bf16[256,1536]{0,1:T(8,128)(2,1)S(1)}, u32[]{:S(2)}, u32[]{:S(2)}) collective-permute-start(bf16[256,1536]{0,1:T(8,128)(2,1)S(1)} %get-tuple-element.80), channel_id=1, source_target_pairs={{0,16},{1,17},{2,18},{3,19},{4,20},{5,21},{6,22},{7,23},{8,24},{9,... | collective-permute-start | bytes 2359304 | tf_op jit(solution)/shard_map/ppermute | solution.py:87
  (175 other events, 4209.4 us)

commit v2 on v1

v2 whole, which is shorter than its diff:
```python
import functools

import jax
import jax.numpy as jnp
from jax import lax
from jax.experimental import pallas as pl
from jax.experimental.pallas import tpu as pltpu
from jax.sharding import PartitionSpec as P

HEAD_SIZE = 256
BLK = 128


EPS = 1e-06
THETA = 1000042.0
NEG = -1e30
HIGH = lax.Precision.HIGHEST
F32 = jnp.float32
BF16 = jnp.bfloat16
MESH = pl.DeviceIdType.MESH
VMEM_LIMIT = 56 * 2**20


def tree_tables(parent_row, tree_len, block_len):
    blocks = parent_row.shape[0]
    nodes = jnp.arange(blocks, dtype=jnp.int32)
    hops = (parent_row[:, None] == nodes[None, :]).astype(F32)
    reach = jnp.eye(blocks, dtype=F32)
    walk = reach
    for hop_count in range(blocks):
        walk = jnp.dot(walk, hops, precision=HIGH)
        reach = jnp.maximum(reach, walk)
    depth = jnp.sum(reach, axis=1) - 1.0
    rows = jnp.arange(tree_len, dtype=jnp.int32)
    member = (rows[:, None] // block_len == nodes[None, :]).astype(F32)
    visible = jnp.dot(jnp.dot(member, reach, precision=HIGH), member.T, precision=HIGH) > 0.5
    allowed_mask = visible & (rows[None, :] <= rows[:, None])
    place = jnp.dot(member, depth, precision=HIGH) * block_len + (rows % block_len).astype(F32)
    return (allowed_mask, place)


def rope_tables(place, head_dim):
    half = head_dim // 2
    freq = THETA ** (-2.0 * jnp.arange(half, dtype=F32) / head_dim)
    angle = place[:, None] * freq[None, :]
    return (jnp.cos(angle), jnp.sin(angle))


def rotate(values, cosine, sine, sign):
    half = values.shape[-1] // 2
    first, second = values[..., :half], values[..., half:]
    return jnp.concatenate(
        [first * cosine - sign * second * sine, second * cosine + sign * first * sine], -1
    )


def normalize(values):
    inverse = lax.rsqrt(jnp.mean(values * values, axis=-1, keepdims=True) + EPS)
    return (values * inverse, inverse)


def norm_back(grad_scaled, scaled, inverse):
    inner = jnp.mean(grad_scaled * scaled, axis=-1, keepdims=True)
    return inverse * (grad_scaled - scaled * inner)


def dot_nn(left, right):
    return jnp.dot(left, right, preferred_element_type=F32)


def dot_nt(left, right):
    return lax.dot_general(left, right, (((1,), (1,)), ((), ())), preferred_element_type=F32)


def dot_tn(left, right):
    return lax.dot_general(left, right, (((0,), (0,)), ((), ())), preferred_element_type=F32)


def flip(index, mask):
    out = index
    bit = 1
    while bit <= mask:
        if mask & bit:
            out = out + bit * (1 - 2 * (index // bit % 2))
        bit *= 2
    return out


class Links:
    def __init__(self, tp, send_sems, recv_sems, local_sems):
        self.tp = tp
        self.di = lax.axis_index("dp")
        self.ti = lax.axis_index("tensor")
        self.send_sems, self.recv_sems, self.local_sems = send_sems, recv_sems, local_sems
        self.used = 0
        self.used_local = 0

    def partner(self, mask):
        return (flip(self.di, mask // self.tp), flip(self.ti, mask % self.tp))

    def greet(self, masks):
        barrier = pltpu.get_barrier_semaphore()
        for mask in masks:
            pl.semaphore_signal(barrier, inc=1, device_id=self.partner(mask), device_id_type=MESH)
        pl.semaphore_wait(barrier, len(masks))

    def remote(self, src, dst, mask):
        index = self.used
        self.used += 1
        return pltpu.make_async_remote_copy(
            src_ref=src,
            dst_ref=dst,
            send_sem=self.send_sems.at[index],
            recv_sem=self.recv_sems.at[index],
            device_id=self.partner(mask),
            device_id_type=MESH,
        )

    def send(self, src, dst, mask):
        copy = self.remote(src, dst, mask)
        copy.start()
        return copy

    def local(self, src, dst):
        copy = pltpu.make_async_copy(src, dst, self.local_sems.at[self.used_local])
        self.used_local += 1
        copy.start()
        return copy


class Spread:
    def __init__(self, links, outer, block_of):
        self.links, self.outer = links, outer
        self.block_of = block_of
        self.zi = links.di // 2
        self.middle = (self.zi == 1) | (self.zi == 2)

    def start(self):
        links, at = self.links, self.block_of
        step = 2 * links.tp
        self.copies = {}
        if self.outer != 4:
            for k in range(1, self.outer):
                self.copies[k] = links.send(at(0), at(k), k * step)
            return
        self.copies[2] = links.send(at(0), at(2), 2 * step)
        self.copies[1] = links.send(at(0), at(1), step)
        self.copies[3] = links.remote(at(0), at(3), 3 * step)
        self.onward = links.remote(at(2), at(3), step)

        @pl.when(self.middle)
        def _():
            self.copies[3].start()

    def forward(self):
        if self.outer != 4:
            return
        self.copies[2].wait_recv()

        @pl.when(self.middle)
        def _():
            self.onward.start()

    def arrive(self, k):
        if self.outer != 4 or k == 1:
            self.copies[k].wait_recv()
        elif k == 3:

            @pl.when(self.middle)
            def _():
                self.copies[3].wait_recv()

            @pl.when(jnp.logical_not(self.middle))
            def _():
                self.onward.wait_recv()

    def sent(self):
        if self.outer != 4:
            for copy in self.copies.values():
                copy.wait_send()
            return
        self.copies[1].wait_send()
        self.copies[2].wait_send()

        @pl.when(self.middle)
        def _():
            self.copies[3].wait_send()
            self.onward.wait_send()


def gather_units(links, full, rows):
    tp = links.tp

    def block(m, lo=0, n=None):
        return full.at[pl.ds(m * rows + lo, rows if n is None else n)]

    half = rows // 2
    sent = []

    def send(m, mask, lo=0, n=None):
        copy = links.send(block(m, lo, n), block(m ^ mask, lo, n), mask)
        sent.append(copy)
        return copy

    x = send(0, tp)
    y = send(0, 2)
    c0 = send(0, 1)
    yield
    y.wait_recv()
    low = send(2, tp, half, half)
    c2 = send(2, 1)
    x.wait_recv()
    high = send(tp, 2, 0, half)
    c4 = send(tp, 1)
    yield
    low.wait_recv()
    high.wait_recv()
    c6 = send(tp + 2, 1)
    yield
    for copy in (c0, c2, c4, c6):
        copy.wait_recv()
    for copy in sent:
        copy.wait_send()
    yield


def run(stages):
    for _ in stages:
        pass


def pipe(body, grid, in_specs, out_specs, *refs):
    pltpu.emit_pipeline(body, grid=grid, in_specs=in_specs, out_specs=out_specs)(*refs)


def rows_spec(rows, width):
    return pl.BlockSpec((rows, width), lambda i: (i, 0))


def whole_spec(rows, width):
    return pl.BlockSpec((rows, width), lambda i: (0, 0))


def forward_kernel(
    outer,
    tp,
    wa,
    wg,
    wu,
    wd,
    x,
    xh,
    cot,
    cosine,
    sine,
    bias,
    wa_all,
    gate_w,
    up_w,
    down_w,
    xh_all,
    qkv,
    probs,
    att,
    x1,
    h2,
    cot_all,
    gate,
    upper,
    hid,
    grad_down,
    part,
    got_c,
    got_y,
    far,
    send_sems,
    recv_sems,
    local_sems,
):
    links = Links(tp, send_sems, recv_sems, local_sems)
    step = 2 * tp
    shard, attn_width = wa.shape
    units = gate_w.shape[1]
    rows, model = xh.shape
    tree_len = rows * tp
    q_width = att.shape[1]
    qkv_width = qkv.shape[1]
    kv_width = (qkv_width - q_width) // 2
    xi = links.di % 2
    ti = links.ti
    links.greet([1, 2, tp] + [k * step for k in range(1, outer)])

    def tree_rows(mask):
        return pl.ds(pl.multiple_of(flip(ti, mask) * rows, rows), rows)

    own_wa = wa_all.at[pl.ds(pl.multiple_of(xi * shard, shard), shard)]
    own_copy = links.local(wa, own_wa)
    here = [links.local(xh, xh_all.at[tree_rows(0)])]

    def wa_block(k):
        return wa_all.at[pl.ds(pl.multiple_of((2 * k + xi) * shard, shard), shard)]

    tok_y = links.send(xh, xh_all.at[tree_rows(0)], 2)
    tok_c = links.send(xh, xh_all.at[tree_rows(0)], 1)
    own_copy.wait()
    attn = Spread(links, outer, wa_block)
    attn.start()
    across = [links.send(wa_block(0), wa_block(0), tp)]
    mine = pl.ds(pl.multiple_of(xi * units, units), units)
    peers = pl.ds(pl.multiple_of((1 - xi) * units, units), units)
    place = pl.ds(pl.multiple_of(xi * shard, shard), shard)
    pair = []
    for w, full in ((wg, gate_w), (wu, up_w), (wd, down_w)):
        here.append(links.local(w.at[:, mine], full.at[place]))
        pair.append(links.send(w.at[:, peers], full.at[place], tp))
    tok_y.wait_recv()
    tok_yc = links.send(xh_all.at[tree_rows(2)], xh_all.at[tree_rows(2)], 1)

    def mlp_spread(full):
        return Spread(links, outer, lambda k: full.at[pl.ds(k * 2 * shard, 2 * shard)])

    attn.forward()
    for k in range(1, outer):
        if k != 2 or outer != 4:
            attn.arrive(k)
        across.append(links.send(wa_block(k), wa_block(k), tp))
    for copy in here:
        copy.wait()
    spreads = [mlp_spread(full) for full in (gate_w, up_w, down_w)]
    pair[0].wait_recv()
    spreads[0].start()
    pair[1].wait_recv()
    spreads[1].start()
    pair[2].wait_recv()
    tok_c.wait_recv()
    tok_yc.wait_recv()
    for copy in across:
        copy.wait_recv()

    head = HEAD_SIZE

    def project(x_ref, w_ref, cos_ref, sin_ref, out_ref):
        raw = dot_nn(x_ref[...], w_ref[...])
        for slot in range((q_width + kv_width) // head):
            cols = slice(slot * head, (slot + 1) * head)
            out_ref[:, cols] = rotate(raw[:, cols], cos_ref[...], sin_ref[...], 1.0).astype(BF16)
        out_ref[:, q_width + kv_width :] = raw[:, q_width + kv_width :].astype(BF16)

    pipe(
        project,
        (tp,),
        [
            rows_spec(rows, model),
            whole_spec(model, qkv_width),
            rows_spec(rows, head // 2),
            rows_spec(rows, head // 2),
        ],
        [rows_spec(rows, qkv_width)],
        xh_all,
        wa_all.at[:, pl.ds(0, qkv_width)],
        cosine,
        sine,
        qkv,
    )
    spreads[0].forward()

    group = q_width // kv_width

    def attend(q_ref, k_ref, v_ref, b_ref, p_ref, o_ref):
        scores = dot_nt(q_ref[...], k_ref[...]) * (head**-0.5) + b_ref[...].astype(F32)
        weights = jnp.exp(scores - jnp.max(scores, axis=-1, keepdims=True))
        weights = (weights / jnp.sum(weights, axis=-1, keepdims=True)).astype(BF16)
        p_ref[0] = weights
        o_ref[...] = dot_nn(weights, v_ref[...]).astype(BF16)

    pipe(
        attend,
        (tp, q_width // head),
        [
            pl.BlockSpec((rows, head), lambda i, h: (i, h)),
            pl.BlockSpec((tree_len, head), lambda i, h: (0, q_width // head + h // group)),
            pl.BlockSpec((tree_len, head), lambda i, h: (0, (q_width + kv_width) // head + h // group)),
            pl.BlockSpec((rows, tree_len), lambda i, h: (i, 0)),
        ],
        [
            pl.BlockSpec((1, rows, tree_len), lambda i, h: (h, i, 0)),
            pl.BlockSpec((rows, head), lambda i, h: (i, h)),
        ],
        qkv,
        qkv,
        qkv,
        bias,
        probs,
        att,
    )

    def out_project(a_ref, w_ref, o_ref):
        o_ref[...] = dot_nt(a_ref[...], w_ref[...]).astype(BF16)

    pipe(
        out_project,
        (tp,),
        [rows_spec(rows, q_width), whole_spec(model, q_width)],
        [rows_spec(rows, model)],
        att,
        wa_all.at[:, pl.ds(qkv_width, q_width)],
        part,
    )
    rc = [
        links.send(part.at[tree_rows(3)], got_c.at[1], 1),
        links.send(part.at[tree_rows(1)], got_c.at[0], 1),
    ]
    spreads[1].forward()
    spreads[2].start()
    strip = rows // 4

    def add(a_ref, b_ref, o_ref):
        o_ref[...] = (a_ref[...].astype(F32) + b_ref[...].astype(F32)).astype(BF16)

    rc[0].wait_recv()
    spec = rows_spec(strip, model)
    pipe(add, (4,), [spec, spec], [spec], part.at[tree_rows(2)], got_c.at[1], far)
    ry = links.send(far, got_y, 2)
    rc[1].wait_recv()
    ry.wait_recv()

    def residual(x_ref, a_ref, b_ref, c_ref, x1_ref, h_ref):
        total = x_ref[...] + (
            a_ref[...].astype(F32) + b_ref[...].astype(F32) + c_ref[...].astype(F32)
        )
        x1_ref[...] = total
        h_ref[...] = normalize(total)[0].astype(BF16)

    pipe(
        residual,
        (4,),
        [spec] * 4,
        [spec] * 2,
        x,
        part.at[tree_rows(0)],
        got_c.at[0],
        got_y,
        x1,
        h2.at[pl.ds(0, rows)],
    )
    run(gather_units(links, h2, rows))
    here_c = links.local(cot, cot_all.at[pl.ds(0, rows)])
    here_c.wait()
    stages = gather_units(links, cot_all, rows)
    next(stages)

    for spread in spreads[:2]:
        for k in range(1, outer):
            spread.arrive(k)
    next(stages)

    def expand(x_ref, g_ref, u_ref, go_ref, uo_ref, h_ref):
        g = dot_nn(x_ref[...], g_ref[...])
        u = dot_nn(x_ref[...], u_ref[...])
        go_ref[...] = g.astype(BF16)
        uo_ref[...] = u.astype(BF16)
        h_ref[...] = (g * jax.nn.sigmoid(g) * u).astype(BF16)

    pipe(
        expand,
        (2 * tp,),
        [rows_spec(rows, model), whole_spec(model, units), whole_spec(model, units)],
        [rows_spec(rows, units)] * 3,
        h2,
        gate_w,
        up_w,
        gate,
        upper,
        hid,
    )
    spreads[2].forward()
    run(stages)

    def weight_grad(a_ref, b_ref, o_ref):
        o_ref[...] = dot_tn(a_ref[...], b_ref[...]).astype(BF16)

    tokens = 2 * tree_len
    pipe(
        weight_grad,
        (4,),
        [pl.BlockSpec((tokens, model // 4), lambda i: (0, i)), whole_spec(tokens, units)],
        [rows_spec(model // 4, units)],
        cot_all,
        hid,
        grad_down,
    )
    for k in range(1, outer):
        spreads[2].arrive(k)
    for spread in spreads + [attn]:
        spread.sent()
    for copy in across + pair + rc + [tok_y, tok_c, tok_yc, ry]:
        copy.wait_send()


def forward_call(outer, tp, wa, wg, wu, wd, x, xh, cot, cosine, sine, bias, q_width, qkv_width):
    shard, attn_width = wa.shape
    rows, model = xh.shape
    tree_len = rows * tp
    units = wg.shape[1] // 2
    heads = q_width // HEAD_SIZE

    def out(shape, dtype=BF16):
        return jax.ShapeDtypeStruct(shape, dtype)

    shapes = [
        out((model, attn_width)),
        out((model, units)),
        out((model, units)),
        out((model, units)),
        out((tree_len, model)),
        out((tree_len, qkv_width)),
        out((heads, tree_len, tree_len)),
        out((tree_len, q_width)),
        out((rows, model), F32),
        out((2 * tree_len, model)),
        out((2 * tree_len, model)),
        out((2 * tree_len, units)),
        out((2 * tree_len, units)),
        out((2 * tree_len, units)),
        out((model, units)),
        out((tree_len, model)),
        out((2, rows, model)),
        out((rows, model)),
        out((rows, model)),
    ]
    count = 40 + 5 * outer
    return pl.pallas_call(
        functools.partial(forward_kernel, outer, tp),
        out_shape=shapes,
        in_specs=[pl.BlockSpec(memory_space=pl.ANY)] * 10,
        out_specs=[pl.BlockSpec(memory_space=pl.ANY)] * len(shapes),
        scratch_shapes=[
            pltpu.SemaphoreType.DMA((count,)),
            pltpu.SemaphoreType.DMA((count,)),
            pltpu.SemaphoreType.DMA((12,)),
        ],
        compiler_params=pltpu.CompilerParams(
            collective_id=0, has_side_effects=True, vmem_limit_bytes=VMEM_LIMIT
        ),
        name="layer_forward",
    )(wa, wg, wu, wd, x, xh, cot, cosine, sine, bias)


def make_body(dp, tp):
    devices = dp * tp
    outer = dp // 2
    assert tp == 4 and dp == 2 * outer and outer & (outer - 1) == 0
    X = tp

    def swap(value, mask):
        return lax.ppermute(value, ("dp", "tensor"), [(i, i ^ mask) for i in range(devices)])

    def zmask(k):
        return k * 2 * tp

    def relative(value, zi):
        width = value.shape[-1] // outer
        step = 1
        while step < outer:
            blocks = [value[..., i * width : (i + 1) * width] for i in range(outer)]
            swapped = jnp.concatenate([blocks[i ^ step] for i in range(outer)], -1)
            value = jnp.where((zi // step) % 2 == 1, swapped, value)
            step *= 2
        return value

    def scatter_units(part):
        rows = part.shape[1] // 2
        got = swap(jnp.stack([part[1], part[3], part[5], part[7]]), 1).astype(F32)
        s0 = part[0].astype(F32) + got[0]
        sy = part[2].astype(F32) + got[1]
        sx = part[4].astype(F32) + got[2]
        sxy = (part[6].astype(F32) + got[3]).astype(BF16)
        top = swap(sxy[:rows], X).astype(F32)
        bottom = swap(sxy[rows:], 2).astype(F32)
        sy = jnp.concatenate([sy[:rows] + top, sy[rows:]], 0).astype(BF16)
        sx = jnp.concatenate([sx[:rows], sx[rows:] + bottom], 0).astype(BF16)
        return s0 + swap(sy, 2).astype(F32) + swap(sx, X).astype(F32)

    def body(
        tokens,
        parents,
        attn_gain,
        w_query,
        key_matrix,
        value_matrix,
        w_out,
        mlp_gain,
        w_gate,
        w_up,
        w_down,
        cotangent,
    ):
        di = lax.axis_index("dp")
        ti = lax.axis_index("tensor")
        zi = di // 2
        upper_x = di % 2 == 1
        rows, model = tokens.shape
        tree_len = rows * tp
        q_width = w_query.shape[1]
        kv_width = key_matrix.shape[1]
        local_q = q_width // HEAD_SIZE
        local_kv = kv_width // HEAD_SIZE
        group = local_q // local_kv
        qkv_width = q_width + 2 * kv_width
        shard = w_query.shape[0]
        units = w_gate.shape[1] // 2
        scale = HEAD_SIZE ** (-0.5)
        gain_a = attn_gain.astype(F32)[:, None]
        gain_m = mlp_gain.astype(F32)[:, None]

        def order_x(mine, theirs, axis):
            low = jnp.where(upper_x, theirs, mine)
            high = jnp.where(upper_x, mine, theirs)
            return jnp.concatenate([low, high], axis)

        w_qkv_own = jnp.concatenate([w_query, key_matrix, value_matrix], 1).astype(F32)
        wa = jnp.concatenate([(w_qkv_own * gain_a).astype(BF16), w_out.T], 1)
        wg = (w_gate.astype(F32) * gain_m).astype(BF16)
        wu = (w_up.astype(F32) * gain_m).astype(BF16)
        allowed_mask, place = tree_tables(parents[0], tree_len, BLK)
        cosine, sine = rope_tables(place, HEAD_SIZE)
        bias = jnp.where(allowed_mask, 0.0, NEG).astype(BF16)
        inputs = relative(tokens, zi).astype(F32)
        scaled_a, inverse_a = normalize(inputs)
        cot = relative(cotangent, zi)
        (
            wa_all,
            gate_w,
            up_w,
            down_w,
            normed_all,
            qkv,
            probs,
            attended,
            mixed,
            normed_m_all,
            cot_all,
            gate,
            upper,
            hidden,
            grad_down,
        ) = forward_call(
            outer,
            tp,
            wa,
            wg,
            wu,
            w_down.T,
            inputs,
            scaled_a.astype(BF16),
            cot,
            cosine,
            sine,
            bias,
            q_width,
            qkv_width,
        )[:15]
        w_qkv = wa_all[:, :qkv_width]
        w_o = wa_all[:, qkv_width:]
        query_rows = qkv[:, :q_width]
        key = qkv[:, q_width : q_width + kv_width].reshape(tree_len, local_kv, HEAD_SIZE)
        value_rows = qkv[:, q_width + kv_width :].reshape(tree_len, local_kv, HEAD_SIZE)
        grouped = query_rows.reshape(tree_len, local_kv, group, HEAD_SIZE)
        probs = probs.reshape(local_kv, group, tree_len, tree_len)

        scaled_m, inverse_m = normalize(mixed)
        gate = gate.astype(F32)
        sigma = jax.nn.sigmoid(gate)
        grad_hidden = dot_nn(cot_all, down_w)
        grad_gate_act = (
            grad_hidden * upper.astype(F32) * sigma * (1.0 + gate * (1.0 - sigma))
        ).astype(BF16)
        grad_up_act = (grad_hidden * gate * sigma).astype(BF16)
        grad_normed_m = scatter_units(
            (dot_nt(grad_gate_act, gate_w) + dot_nt(grad_up_act, up_w))
            .astype(BF16)
            .reshape(2 * tp, rows, model)
        )
        grad_mixed = cot.astype(F32) + norm_back(grad_normed_m, scaled_m, inverse_m)
        grad_gate = dot_tn(normed_m_all, grad_gate_act).astype(BF16)
        grad_up = dot_tn(normed_m_all, grad_up_act).astype(BF16)
        mlp_part = dot_nt(hidden, down_w).astype(BF16).reshape(2 * tp, rows, model)
        output = relative((mixed + scatter_units(mlp_part)).astype(BF16), zi)

        def reduce_z(grad):
            block = grad.reshape(outer, 2 * shard, grad.shape[1])
            total = block[0].astype(F32)
            for k in range(1, outer):
                total = total + swap(block[k], zmask(k)).astype(F32)
            return total

        def unpaired(grad):
            s = reduce_z(grad)
            keep = jnp.where(upper_x, s[shard:], s[:shard])
            send = jnp.where(upper_x, s[:shard], s[shard:]).astype(BF16)
            return order_x(keep, swap(send, X).astype(F32), 1)

        grad_down = unpaired(grad_down)
        grad_gate = unpaired(grad_gate)
        grad_up = unpaired(grad_up)

        order = [(ti ^ j) * rows for j in range(tp)]

        def gather_tensor(a0):
            a1 = swap(a0, 1)
            a2 = swap(a0, 2)
            a3 = swap(a2, 1)
            full = jnp.zeros((tree_len, model), a0.dtype)
            for start, a in zip(order, (a0, a1, a2, a3)):
                full = lax.dynamic_update_slice(full, a, (start, 0))
            return full

        def scatter_tensor(part):
            blocks = [lax.dynamic_slice(part, (start, 0), (rows, model)) for start in order]
            b = [block.astype(BF16) for block in blocks]
            got = swap(jnp.stack([b[1], b[3]]), 1).astype(F32)
            far = (blocks[2] + got[1]).astype(BF16)
            return blocks[0] + got[0] + swap(far, 2).astype(F32)

        grad_mixed_all = gather_tensor(grad_mixed.astype(BF16))
        grad_attended = dot_nn(grad_mixed_all, w_o).astype(BF16)
        grad_grouped = grad_attended.reshape(tree_len, local_kv, group, HEAD_SIZE)
        grad_value_act = jnp.einsum(
            "kgqs,qkgd->skd", probs, grad_grouped, preferred_element_type=F32
        )
        grad_probs = jnp.einsum(
            "qkgd,skd->kgqs", grad_grouped, value_rows, preferred_element_type=F32
        )
        probs_full = probs.astype(F32)
        inner = jnp.sum(probs_full * grad_probs, axis=-1, keepdims=True)
        grad_scores = (probs_full * (grad_probs - inner) * scale).astype(BF16)
        grad_query_rot = jnp.einsum(
            "kgqs,skd->qkgd", grad_scores, key, preferred_element_type=F32
        )
        grad_key_rot = jnp.einsum(
            "kgqs,qkgd->skd", grad_scores, grouped, preferred_element_type=F32
        )
        turn_back = (cosine[:, None], sine[:, None], -1.0)
        grad_query_act = rotate(
            grad_query_rot.reshape(tree_len, local_q, HEAD_SIZE), *turn_back
        )
        grad_key_act = rotate(grad_key_rot, *turn_back)
        grad_qkv = jnp.concatenate(
            [
                grad_query_act.astype(BF16).reshape(tree_len, q_width),
                grad_key_act.astype(BF16).reshape(tree_len, kv_width),
                grad_value_act.astype(BF16).reshape(tree_len, kv_width),
            ],
            1,
        )
        grad_normed_a = scatter_tensor(dot_nt(grad_qkv, w_qkv))
        grad_input = norm_back(grad_normed_a, scaled_a, inverse_a)
        grad_tokens = relative((grad_mixed + grad_input).astype(BF16), zi)
        grad_wa = jnp.concatenate(
            [
                dot_tn(normed_all, grad_qkv).astype(BF16),
                dot_tn(grad_mixed_all, attended).astype(BF16),
            ],
            1,
        ).reshape(outer, 2, shard, qkv_width + q_width)
        keep = jnp.where(upper_x, grad_wa[:, 1], grad_wa[:, 0])
        send = jnp.where(upper_x, grad_wa[:, 0], grad_wa[:, 1])
        pair_sum = keep.astype(F32) + swap(send, X).astype(F32)
        far = pair_sum.astype(BF16)
        total_a = pair_sum[0]
        for k in range(1, outer):
            total_a = total_a + swap(far[k], zmask(k)).astype(F32)

        grad_qkv_w = total_a[:, :qkv_width]
        gain_sum_a = jnp.sum(w_qkv_own * grad_qkv_w, 1)
        gain_sum_m = jnp.sum(w_gate.astype(F32) * grad_gate, 1) + jnp.sum(
            w_up.astype(F32) * grad_up, 1
        )
        grad_qkv_w = grad_qkv_w * gain_a

        def sum_tensor(v):
            v = v + swap(v, 1)
            return v + swap(v, 2)

        return (
            output,
            grad_tokens,
            sum_tensor(gain_sum_a),
            grad_qkv_w[:, :q_width],
            grad_qkv_w[:, q_width : q_width + kv_width],
            grad_qkv_w[:, q_width + kv_width :],
            total_a[:, qkv_width:].T,
            sum_tensor(gain_sum_m),
            grad_gate * gain_m,
            grad_up * gain_m,
            grad_down.T,
        )

    return body


def solution(mesh):
    in_specs = (
        P(("dp", "tensor"), None),
        P("dp", None),
        P("dp"),
        P("dp", "tensor"),
        P("dp", "tensor"),
        P("dp", "tensor"),
        P("tensor", "dp"),
        P("dp"),
        P("dp", "tensor"),
        P("dp", "tensor"),
        P("tensor", "dp"),
        P(("dp", "tensor"), None),
    )
    out_specs = (
        P(("dp", "tensor"), None),
        P(("dp", "tensor"), None),
        P("dp"),
        P("dp", "tensor"),
        P("dp", "tensor"),
        P("dp", "tensor"),
        P("tensor", "dp"),
        P("dp"),
        P("dp", "tensor"),
        P("dp", "tensor"),
        P("tensor", "dp"),
    )
    body = make_body(mesh.shape["dp"], mesh.shape["tensor"])
    return jax.shard_map(body, mesh=mesh, in_specs=in_specs, out_specs=out_specs, check_vma=False)
```

time: 1110 us -> 976 us (0.88)
  Pallas kernels: 0 us -> 396 us
  waiting for transfers between devices: 618 us -> 242 us
  matrix products: 175 us -> 118 us
  local copies, waits for them, and re-layouts: 99.8 us -> 46.7 us
  starting transfers between devices: 103 us -> 64.8 us
  other arithmetic: 103 us -> 89 us
    pallas_call x0 -> x1, Pallas kernels: none -> 396 us  [forward_call(): pl.pallas_call(functools.partial(forward_kernel, outer, tp), out_shape=sh...]
    ppermute x79 -> x35, waiting for transfers between devices: 618 us -> 242 us  [swap(): lax.ppermute(value, ('dp', 'tensor'), [(i, i ^ mask) for i in range(devic...]
    dot_general x5 -> x2, matrix products: 63.7 us -> 22.7 us  [dot_nn(): return jnp.dot(left, right, preferred_element_type=F32)]
    unnamed x275 -> x126, local copies, waits for them, and re-layouts: 55 us -> 16 us
    ppermute x79 -> x35, starting transfers between devices: 103 us -> 64.8 us  [swap(): lax.ppermute(value, ('dp', 'tensor'), [(i, i ^ mask) for i in range(devic...]
    dot_general x5 -> x4, matrix products: 47.3 us -> 31.7 us  [dot_tn(): lax.dot_general(left, right, (((0,), (0,)), ((), ())), preferred_element_...]
    reshape x2 -> x0, local copies, waits for them, and re-layouts: 11.2 us -> none  [the longest x1 11.1 us: body(): grad_wa = jnp.concatenate([dot_tn(normed_all, grad_qkv).astype(BF16), dot...]
    dot_general x5 -> x4, matrix products: 46.1 us -> 51.1 us  [dot_nt(): lax.dot_general(left, right, (((1,), (1,)), ((), ())), preferred_element_...]
  transfers between devices with their start and end apart: 79 -> 35, of which waited for: 26 -> 11; matrix products, arithmetic and copies ran while one was open for 26% -> 20% of each run, Pallas kernels for 0% -> 0%
where the time goes in v2:
time: 976 us; the launch traced here: 958 us
  Pallas kernels  396 us (41%)
  waiting for transfers between devices  242 us (25%)
  matrix products  118 us (12%)
  other arithmetic  89 us (9%)
  starting transfers between devices  64.8 us (7%)
  local copies, waits for them, and re-layouts  46.7 us (5%)
    pallas_call x1, Pallas kernels, forward_call(): pl.pallas_call(functools.partial(forward_kernel, outer, tp), out_shape=sh...  396 us
    ppermute x35, waiting for transfers between devices, swap(): lax.ppermute(value, ('dp', 'tensor'), [(i, i ^ mask) for i in range(devic...  242 us
    ppermute x35, starting transfers between devices, swap(): lax.ppermute(value, ('dp', 'tensor'), [(i, i ^ mask) for i in range(devic...  64.8 us
    dot_general x4, matrix products, dot_nt(): lax.dot_general(left, right, (((1,), (1,)), ((), ())), preferred_element_...  51.1 us
    dot_general x4, matrix products, dot_tn(): lax.dot_general(left, right, (((0,), (0,)), ((), ())), preferred_element_...  31.7 us
    dot_general x2, matrix products, dot_nn(): return jnp.dot(left, right, preferred_element_type=F32)  22.7 us
  transfers between devices with their start and end apart: 35, of which 11 were waited for; matrix products, arithmetic and copies ran while one was open for 20% of the time, Pallas kernels for 0%

profile of v2, /device:TPU:0, one launch (start us, length us, event | category | flops | bytes accessed | tf_op | source)
XLA Modules:
  0.0 958.2 jit_solution(12591767257860277746)
XLA Ops:
  24.4 395.6 %layer_forward.1 = (bf16[2048,1536]{1,0:T(8,128)(2,1)}, bf16[2048,1024]{1,0:T(8,128)(2,1)}, bf16[2048,1024]{1,0:T(8,128)(2,1)}, bf16[2048,1024]{1,0:T(8,128)(2,1...) custom-call(bf16[256,1536]{1,0:T(8,128)(2,1)} %pad_maximum_fusion.12, ...), custom_call_target="tpu_custom_call" | custom-call | tf_op jit(solution)/shard_map/layer_forward/pallas_call | solution.py:532
  420.0 18.6 %fusion.8 = (bf16[2048,1024]{1,0:T(8,128)(2,1)S(1)}, f32[2048,1024]{1,0:T(8,128)}) fusion(bf16[2048,1024]{1,0:T(8,128)(2,1)} %get-tuple-element.31, bf16[2048,1024]{1,0:T(8,128)(2,1)} %get-tuple-element.30, bf16[2048,2048]{1,0:T(8,128)(2,1)} %get-tuple-element.29, bf16[2048,1024]{1,0:T(8,128)(2,1)} %get-tuple-element.28), kind=kOutput, calls=%fused_computation.14 | convolution fusion | flops 8615100416 | bytes 33554432 | tf_op jit(solution)/shard_map/dot_general | solution.py:68
  438.6 9.6 %convolution_convert_fusion.3 = bf16[2048,1024]{1,0:T(8,128)(2,1)S(1)} fusion(bf16[2048,2048]{1,0:T(8,128)(2,1)S(1)} %copy-done.46, bf16[2048,1024]{1,0:T(8,128)(2,1)S(1)} %get-tuple-element.155), kind=kOutput, calls=%fused_computation.31 | convolution fusion | flops 8592031744 | bytes 16777216 | tf_op jit(solution)/shard_map/dot_general | solution.py:76
  456.2 9.8 %convolution_convert_fusion = bf16[2048,2048]{1,0:T(8,128)(2,1)S(1)} fusion(bf16[2048,1024]{1,0:T(8,128)(2,1)S(1)} %copy-done.50, bf16[2048,1024]{1,0:T(8,128)(2,1)S(1)} %copy-done.49), kind=kOutput, calls=%fused_computation.18 | convolution fusion | flops 8594128896 | bytes 16777216 | tf_op jit(solution)/shard_map/dot_general | solution.py:72
  473.1 11.7 %fusion.127 = f32[2048,2048]{1,0:T(8,128)} fusion(bf16[2048,1024]{1,0:T(8,128)(2,1)S(1)} %get-tuple-element.155, bf16[2048,1024]{1,0:T(8,128)(2,1)S(1)} %copy-done.48), kind=kOutput, calls=%fused_computation.253 | convolution fusion | flops 8589934592 | bytes 25165824 | tf_op jit(solution)/shard_map/dot_general | solution.py:72
  484.8 20.3 %add_convert_fusion = bf16[2048,2048]{1,0:T(8,128)(2,1)} fusion(f32[2048,2048]{1,0:T(8,128)} %fusion.127, bf16[2048,1024]{1,0:T(8,128)(2,1)} %get-tuple-element.33, f32[2048,1024]{1,0:T(8,128)} %get-tuple-element.156, bf16[2048,1024]{1,0:T(8,128)(2,1)} %get-tuple-element.31), kind=kOutput, calls=%fused_computation | convolution fusion | flops 8613003264 | bytes 41943040 | tf_op jit(solution)/shard_map/dot_general | solution.py:72
  514.0 13.0 %convolution_convert_fusion.2 = bf16[2048,1024]{1,0:T(8,128)(2,1)S(1)} fusion(bf16[2048,2048]{1,0:T(8,128)(2,1)S(1)} %bitcast.232, f32[2048,1024]{1,0:T(8,128)} %get-tuple-element.156, bf16[2048,1024]{1,0:T(8,128)(2,1)} %get-tuple-element.31), kind=kOutput, calls=%fused_computation.30 | convolution fusion | flops 8606711808 | bytes 25165824 | tf_op jit(solution)/shard_map/dot_general | solution.py:76
  533.2 5.6 fusion.33
  542.1 5.6 fusion.26
  553.7 11.1 %collective-permute-done.6 = bf16[128,2048]{1,0:T(8,128)(2,1)S(1)} collective-permute-done((bf16[128,2048]{1,0:T(8,128)(2,1)S(1)}, bf16[128,2048]{1,0:T(8,128)(2,1)S(1)}, u32[]{:S(2)}, u32[]{:S(2)}) %collective-permute-start.6) | collective-permute-done | bytes 524320 | tf_op jit(solution)/shard_map/ppermute | solution.py:556
  567.0 9.4 collective-permute-done.8
  585.3 59.2 %collective-permute-done.26 = bf16[512,1024]{1,0:T(8,128)(2,1)} collective-permute-done((bf16[512,1024]{1,0:T(8,128)(2,1)}, bf16[512,1024]{1,0:T(8,128)(2,1)}, u32[]{:S(2)}, u32[]{:S(2)}) %collective-permute-start.26) | collective-permute-done | bytes 1048608 | tf_op jit(solution)/shard_map/ppermute | solution.py:556
  653.6 13.8 %collective-permute-start.31 = (bf16[512,1024]{1,0:T(8,128)(2,1)S(1)}, bf16[512,1024]{1,0:T(8,128)(2,1)S(1)}, u32[]{:S(2)}, u32[]{:S(2)}) collective-permute-start(bf16[512,1024]{1,0:T(8,128)(2,1)S(1)} %copy-done.30), channel_id=1, source_target_pairs={{0,8},{1,9},{2,10},{3,11},{4,12},{5,13},{6,14},{7,15},{8,0},{9,1},... | collective-permute-start | bytes 3145736 | tf_op jit(solution)/shard_map/ppermute | solution.py:556
  674.1 5.3 multiply_reduce_fusion.1
  680.6 5.0 constant_dynamic-update-slice_fusion.3
  686.7 21.3 %collective-permute-done.31 = bf16[512,1024]{1,0:T(8,128)(2,1)S(1)} collective-permute-done((bf16[512,1024]{1,0:T(8,128)(2,1)S(1)}, bf16[512,1024]{1,0:T(8,128)(2,1)S(1)}, u32[]{:S(2)}, u32[]{:S(2)}) %collective-permute-start.31) | collective-permute-done | bytes 1048608 | tf_op jit(solution)/shard_map/ppermute | solution.py:556
  709.0 33.4 %collective-permute-done.32 = bf16[512,1024]{1,0:T(8,128)(2,1)S(1)} collective-permute-done((bf16[512,1024]{1,0:T(8,128)(2,1)S(1)}, bf16[512,1024]{1,0:T(8,128)(2,1)S(1)}, u32[]{:S(2)}, u32[]{:S(2)}) %collective-permute-start.32) | collective-permute-done | bytes 1048608 | tf_op jit(solution)/shard_map/ppermute | solution.py:556
  766.0 9.2 fusion.12
  775.3 6.7 convolution_convert_fusion.1
  787.9 8.7 copy.47
  819.5 52.5 %collective-permute-done.15 = bf16[4,256,1536]{2,1,0:T(8,128)(2,1)} collective-permute-done((bf16[4,256,1536]{2,1,0:T(8,128)(2,1)}, bf16[4,256,1536]{2,1,0:T(8,128)(2,1)}, u32[]{:S(2)}, u32[]{:S(2)}) %collective-permute-start.15) | collective-permute-done | bytes 3145760 | tf_op jit(solution)/shard_map/ppermute | solution.py:556
  874.9 21.9 %collective-permute-start.16 = (bf16[256,1536]{1,0:T(8,128)(2,1)S(1)}, bf16[256,1536]{1,0:T(8,128)(2,1)S(1)}, u32[]{:S(2)}, u32[]{:S(2)}) collective-permute-start(bf16[256,1536]{1,0:T(8,128)(2,1)S(1)} %get-tuple-element.95), channel_id=1, source_target_pairs={{0,8},{1,9},{2,10},{3,11},{4,12},{5,13},{6,14},{7,15},{8,0},{9,1},... | collective-permute-start | bytes 2359304 | tf_op jit(solution)/shard_map/ppermute | solution.py:556
  902.5 26.2 %collective-permute-done.16 = bf16[256,1536]{1,0:T(8,128)(2,1)S(1)} collective-permute-done((bf16[256,1536]{1,0:T(8,128)(2,1)S(1)}, bf16[256,1536]{1,0:T(8,128)(2,1)S(1)}, u32[]{:S(2)}, u32[]{:S(2)}) %collective-permute-start.16) | collective-permute-done | bytes 786464 | tf_op jit(solution)/shard_map/ppermute | solution.py:556
  928.7 23.2 %collective-permute-done.17 = bf16[256,1536]{1,0:T(8,128)(2,1)S(1)} collective-permute-done((bf16[256,1536]{1,0:T(8,128)(2,1)S(1)}, bf16[256,1536]{1,0:T(8,128)(2,1)S(1)}, u32[]{:S(2)}, u32[]{:S(2)}) %collective-permute-start.17) | collective-permute-done | bytes 786464 | tf_op jit(solution)/shard_map/ppermute | solution.py:556
  (303 shorter events, 159.4 us)
Async XLA Ops:
  451.8 126.9 %collective-permute-start.21 = (bf16[512,1024]{1,0:T(8,128)(2,1)}, bf16[512,1024]{1,0:T(8,128)(2,1)}, u32[]{:S(2)}, u32[]{:S(2)}) collective-permute-start(bf16[512,1024]{1,0:T(8,128)(2,1)} %get-tuple-element.92), channel_id=1, source_target_pairs={{0,8},{1,9},{2,10},{3,11},{4,12},{5,13},{6,14},{7,15},{8,0},{9,1},... | collective-permute-start | bytes 3145736 | tf_op jit(solution)/shard_map/ppermute | solution.py:556
  451.8 130.4 %collective-permute-start.22 = (bf16[512,1024]{1,0:T(8,128)(2,1)}, bf16[512,1024]{1,0:T(8,128)(2,1)}, u32[]{:S(2)}, u32[]{:S(2)}) collective-permute-start(bf16[512,1024]{1,0:T(8,128)(2,1)} %get-tuple-element.94), channel_id=1, source_target_pairs={{0,16},{1,17},{2,18},{3,19},{4,20},{5,21},{6,22},{7,23},{8,24},{9,... | collective-permute-start | bytes 3145736 | tf_op jit(solution)/shard_map/ppermute | solution.py:556
  452.8 130.4 %collective-permute-start.23 = (bf16[512,1024]{1,0:T(8,128)(2,1)}, bf16[512,1024]{1,0:T(8,128)(2,1)}, u32[]{:S(2)}, u32[]{:S(2)}) collective-permute-start(bf16[512,1024]{1,0:T(8,128)(2,1)} %get-tuple-element.93), channel_id=1, source_target_pairs={{0,24},{1,25},{2,26},{3,27},{4,28},{5,29},{6,30},{7,31},{8,16},{9,... | collective-permute-start | bytes 3145736 | tf_op jit(solution)/shard_map/ppermute | solution.py:556
  471.7 58.2 %collective-permute-start = (bf16[4,256,2048]{2,1,0:T(8,128)(2,1)}, bf16[4,256,2048]{2,1,0:T(8,128)(2,1)}, u32[]{:S(2)}, u32[]{:S(2)}) collective-permute-start(bf16[4,256,2048]{2,1,0:T(8,128)(2,1)} %pad_maximum_fusion.1), channel_id=1, source_target_pairs={{0,1},{1,0},{2,3},{3,2},{4,5},{5,4},{6,7},{7,6},{8,9},{9,8},{10,11... | collective-permute-start | bytes 12582920 | tf_op jit(solution)/shard_map/ppermute | solution.py:556
  510.4 29.7 %collective-permute-start.5 = (bf16[4,256,2048]{2,1,0:T(8,128)(2,1)}, bf16[4,256,2048]{2,1,0:T(8,128)(2,1)S(1)}, u32[]{:S(2)}, u32[]{:S(2)}) collective-permute-start(bf16[4,256,2048]{2,1,0:T(8,128)(2,1)} %pad_maximum_fusion.2), channel_id=1, source_target_pairs={{0,1},{1,0},{2,3},{3,2},{4,5},{5,4},{6,7},{7,6},{8,9},{9,8},{10,11... | collective-permute-start | bytes 12582920 | tf_op jit(solution)/shard_map/ppermute | solution.py:556
  553.5 30.8 %collective-permute-start.25 = (bf16[512,1024]{1,0:T(8,128)(2,1)}, bf16[512,1024]{1,0:T(8,128)(2,1)}, u32[]{:S(2)}, u32[]{:S(2)}) collective-permute-start(bf16[512,1024]{1,0:T(8,128)(2,1)} %get-tuple-element.89), channel_id=1, source_target_pairs={{0,8},{1,9},{2,10},{3,11},{4,12},{5,13},{6,14},{7,15},{8,0},{9,1},... | collective-permute-start | bytes 3145736 | tf_op jit(solution)/shard_map/ppermute | solution.py:556
  576.4 68.1 %collective-permute-start.26 = (bf16[512,1024]{1,0:T(8,128)(2,1)}, bf16[512,1024]{1,0:T(8,128)(2,1)}, u32[]{:S(2)}, u32[]{:S(2)}) collective-permute-start(bf16[512,1024]{1,0:T(8,128)(2,1)} %get-tuple-element.91), channel_id=1, source_target_pairs={{0,16},{1,17},{2,18},{3,19},{4,20},{5,21},{6,22},{7,23},{8,24},{9,... | collective-permute-start | bytes 3145736 | tf_op jit(solution)/shard_map/ppermute | solution.py:556
  578.7 74.8 %collective-permute-start.27 = (bf16[512,1024]{1,0:T(8,128)(2,1)}, bf16[512,1024]{1,0:T(8,128)(2,1)}, u32[]{:S(2)}, u32[]{:S(2)}) collective-permute-start(bf16[512,1024]{1,0:T(8,128)(2,1)} %get-tuple-element.90), channel_id=1, source_target_pairs={{0,24},{1,25},{2,26},{3,27},{4,28},{5,29},{6,30},{7,31},{8,16},{9,... | collective-permute-start | bytes 3145736 | tf_op jit(solution)/shard_map/ppermute | solution.py:556
  582.2 88.2 %collective-permute-start.2 = (bf16[256,2048]{1,0:T(8,128)(2,1)}, bf16[256,2048]{1,0:T(8,128)(2,1)}, u32[]{:S(2)}, u32[]{:S(2)}) collective-permute-start(bf16[256,2048]{1,0:T(8,128)(2,1)} %pad_maximum_fusion.7), channel_id=1, source_target_pairs={{0,2},{1,3},{2,0},{3,1},{4,6},{5,7},{6,4},{7,5},{8,10},{9,11},{10,... | collective-permute-start | bytes 3145736 | tf_op jit(solution)/shard_map/ppermute | solution.py:556
  583.2 87.3 %collective-permute-start.4 = (bf16[256,2048]{1,0:T(8,128)(2,1)}, bf16[256,2048]{1,0:T(8,128)(2,1)}, u32[]{:S(2)}, u32[]{:S(2)}) collective-permute-start(bf16[256,2048]{1,0:T(8,128)(2,1)} %pad_maximum_fusion.8), channel_id=1, source_target_pairs={{0,4},{1,5},{2,6},{3,7},{4,0},{5,1},{6,2},{7,3},{8,12},{9,13},{10,... | collective-permute-start | bytes 3145736 | tf_op jit(solution)/shard_map/ppermute | solution.py:556
  584.3 88.8 %collective-permute-start.7 = (bf16[256,2048]{1,0:T(8,128)(2,1)}, bf16[256,2048]{1,0:T(8,128)(2,1)}, u32[]{:S(2)}, u32[]{:S(2)}) collective-permute-start(bf16[256,2048]{1,0:T(8,128)(2,1)} %pad_maximum_fusion.9), channel_id=1, source_target_pairs={{0,2},{1,3},{2,0},{3,1},{4,6},{5,7},{6,4},{7,5},{8,10},{9,11},{10,... | collective-permute-start | bytes 3145736 | tf_op jit(solution)/shard_map/ppermute | solution.py:556
  653.6 54.4 %collective-permute-start.31 = (bf16[512,1024]{1,0:T(8,128)(2,1)S(1)}, bf16[512,1024]{1,0:T(8,128)(2,1)S(1)}, u32[]{:S(2)}, u32[]{:S(2)}) collective-permute-start(bf16[512,1024]{1,0:T(8,128)(2,1)S(1)} %copy-done.30), channel_id=1, source_target_pairs={{0,8},{1,9},{2,10},{3,11},{4,12},{5,13},{6,14},{7,15},{8,0},{9,1},... | collective-permute-start | bytes 3145736 | tf_op jit(solution)/shard_map/ppermute | solution.py:556
  670.5 72.0 %collective-permute-start.32 = (bf16[512,1024]{1,0:T(8,128)(2,1)S(1)}, bf16[512,1024]{1,0:T(8,128)(2,1)S(1)}, u32[]{:S(2)}, u32[]{:S(2)}) collective-permute-start(bf16[512,1024]{1,0:T(8,128)(2,1)S(1)} %copy-done.29), channel_id=1, source_target_pairs={{0,16},{1,17},{2,18},{3,19},{4,20},{5,21},{6,22},{7,23},{8,24},{9,... | collective-permute-start | bytes 3145736 | tf_op jit(solution)/shard_map/ppermute | solution.py:556
  670.6 71.9 %collective-permute-start.33 = (bf16[512,1024]{1,0:T(8,128)(2,1)S(1)}, bf16[512,1024]{1,0:T(8,128)(2,1)S(1)}, u32[]{:S(2)}, u32[]{:S(2)}) collective-permute-start(bf16[512,1024]{1,0:T(8,128)(2,1)S(1)} %copy-done.28), channel_id=1, source_target_pairs={{0,24},{1,25},{2,26},{3,27},{4,28},{5,29},{6,30},{7,31},{8,16},{9,... | collective-permute-start | bytes 3145736 | tf_op jit(solution)/shard_map/ppermute | solution.py:556
  673.1 73.4 %collective-permute-start.24 = (bf16[256,1024]{1,0:T(8,128)(2,1)S(1)}, bf16[256,1024]{1,0:T(8,128)(2,1)S(1)}, u32[]{:S(2)}, u32[]{:S(2)}) collective-permute-start(bf16[256,1024]{1,0:T(8,128)(2,1)S(1)} %select_convert_fusion.3), channel_id=1, source_target_pairs={{0,4},{1,5},{2,6},{3,7},{4,0},{5,1},{6,2},{7,3},{8,12},{9,13},{10,... | collective-permute-start | bytes 1572872 | tf_op jit(solution)/shard_map/ppermute | solution.py:556
  685.7 61.2 %collective-permute-start.11 = (bf16[256,2048]{1,0:T(8,128)(2,1)S(1)}, bf16[256,2048]{1,0:T(8,128)(2,1)S(1)}, u32[]{:S(2)}, u32[]{:S(2)}) collective-permute-start(bf16[256,2048]{1,0:T(8,128)(2,1)S(1)} %get-tuple-element.66), channel_id=1, source_target_pairs={{0,2},{1,3},{2,0},{3,1},{4,6},{5,7},{6,4},{7,5},{8,10},{9,11},{10,... | collective-permute-start | bytes 3145736 | tf_op jit(solution)/shard_map/ppermute | solution.py:556
  708.0 39.2 %collective-permute-start.28 = (bf16[256,1024]{1,0:T(8,128)(2,1)S(1)}, bf16[256,1024]{1,0:T(8,128)(2,1)S(1)}, u32[]{:S(2)}, u32[]{:S(2)}) collective-permute-start(bf16[256,1024]{1,0:T(8,128)(2,1)S(1)} %select_convert_fusion.2), channel_id=1, source_target_pairs={{0,4},{1,5},{2,6},{3,7},{4,0},{5,1},{6,2},{7,3},{8,12},{9,13},{10,... | collective-permute-start | bytes 1572872 | tf_op jit(solution)/shard_map/ppermute | solution.py:556
  745.5 61.0 %collective-permute-start.34 = (bf16[256,1024]{1,0:T(8,128)(2,1)}, bf16[256,1024]{1,0:T(8,128)(2,1)}, u32[]{:S(2)}, u32[]{:S(2)}) collective-permute-start(bf16[256,1024]{1,0:T(8,128)(2,1)} %select_convert_fusion.1), channel_id=1, source_target_pairs={{0,4},{1,5},{2,6},{3,7},{4,0},{5,1},{6,2},{7,3},{8,12},{9,13},{10,... | collective-permute-start | bytes 1572872 | tf_op jit(solution)/shard_map/ppermute | solution.py:556
  751.0 56.7 %collective-permute-start.29 = (f32[256]{0:T(256)S(1)}, f32[256]{0:T(256)S(1)}, u32[]{:S(2)}, u32[]{:S(2)}) collective-permute-start(f32[256]{0:T(256)S(1)} %add.252), channel_id=1, source_target_pairs={{0,1},{1,0},{2,3},{3,2},{4,5},{5,4},{6,7},{7,6},{8,9},{9,8},{10,11... | collective-permute-start | bytes 3080 | tf_op jit(solution)/shard_map/ppermute | solution.py:556
  801.4 70.6 %collective-permute-start.15 = (bf16[4,256,1536]{2,1,0:T(8,128)(2,1)}, bf16[4,256,1536]{2,1,0:T(8,128)(2,1)}, u32[]{:S(2)}, u32[]{:S(2)}) collective-permute-start(bf16[4,256,1536]{2,1,0:T(8,128)(2,1)} %select_bitcast_fusion), channel_id=1, source_target_pairs={{0,4},{1,5},{2,6},{3,7},{4,0},{5,1},{6,2},{7,3},{8,12},{9,13},{10,... | collective-permute-start | bytes 9437192 | tf_op jit(solution)/shard_map/ppermute | solution.py:556
  818.4 80.9 %collective-permute-start.14 = (bf16[256,2048]{1,0:T(8,128)(2,1)S(1)}, bf16[256,2048]{1,0:T(8,128)(2,1)S(1)}, u32[]{:S(2)}, u32[]{:S(2)}) collective-permute-start(bf16[256,2048]{1,0:T(8,128)(2,1)S(1)} %fusion.20), channel_id=1, source_target_pairs={{0,2},{1,3},{2,0},{3,1},{4,6},{5,7},{6,4},{7,5},{8,10},{9,11},{10,... | collective-permute-start | bytes 3145736 | tf_op jit(solution)/shard_map/ppermute | solution.py:556
  874.9 53.8 %collective-permute-start.16 = (bf16[256,1536]{1,0:T(8,128)(2,1)S(1)}, bf16[256,1536]{1,0:T(8,128)(2,1)S(1)}, u32[]{:S(2)}, u32[]{:S(2)}) collective-permute-start(bf16[256,1536]{1,0:T(8,128)(2,1)S(1)} %get-tuple-element.95), channel_id=1, source_target_pairs={{0,8},{1,9},{2,10},{3,11},{4,12},{5,13},{6,14},{7,15},{8,0},{9,1},... | collective-permute-start | bytes 2359304 | tf_op jit(solution)/shard_map/ppermute | solution.py:556
  896.8 55.1 %collective-permute-start.17 = (bf16[256,1536]{1,0:T(8,128)(2,1)S(1)}, bf16[256,1536]{1,0:T(8,128)(2,1)S(1)}, u32[]{:S(2)}, u32[]{:S(2)}) collective-permute-start(bf16[256,1536]{1,0:T(8,128)(2,1)S(1)} %get-tuple-element.97), channel_id=1, source_target_pairs={{0,16},{1,17},{2,18},{3,19},{4,20},{5,21},{6,22},{7,23},{8,24},{9,... | collective-permute-start | bytes 2359304 | tf_op jit(solution)/shard_map/ppermute | solution.py:556
  896.8 55.1 %collective-permute-start.18 = (bf16[256,1536]{1,0:T(8,128)(2,1)S(1)}, bf16[256,1536]{1,0:T(8,128)(2,1)S(1)}, u32[]{:S(2)}, u32[]{:S(2)}) collective-permute-start(bf16[256,1536]{1,0:T(8,128)(2,1)S(1)} %get-tuple-element.96), channel_id=1, source_target_pairs={{0,24},{1,25},{2,26},{3,27},{4,28},{5,29},{6,30},{7,31},{8,16},{9,... | collective-permute-start | bytes 2359304 | tf_op jit(solution)/shard_map/ppermute | solution.py:556
  (72 other events, 1054.6 us)

commit v3 on v2

v3 whole, which is shorter than its diff:
```python
import functools

import jax
import jax.numpy as jnp
from jax import lax
from jax.experimental import pallas as pl
from jax.experimental.pallas import tpu as pltpu
from jax.sharding import PartitionSpec as P

HEAD_SIZE = 256
BLK = 128


EPS = 1e-06
THETA = 1000042.0
NEG = -1e30
HIGH = lax.Precision.HIGHEST
F32 = jnp.float32
BF16 = jnp.bfloat16
MESH = pl.DeviceIdType.MESH
VMEM_LIMIT = 56 * 2**20


def tree_tables(parent_row, tree_len, block_len):
    blocks = parent_row.shape[0]
    nodes = jnp.arange(blocks, dtype=jnp.int32)
    hops = (parent_row[:, None] == nodes[None, :]).astype(F32)
    reach = jnp.eye(blocks, dtype=F32)
    walk = reach
    for hop_count in range(blocks):
        walk = jnp.dot(walk, hops, precision=HIGH)
        reach = jnp.maximum(reach, walk)
    depth = jnp.sum(reach, axis=1) - 1.0
    rows = jnp.arange(tree_len, dtype=jnp.int32)
    member = (rows[:, None] // block_len == nodes[None, :]).astype(F32)
    visible = jnp.dot(jnp.dot(member, reach, precision=HIGH), member.T, precision=HIGH) > 0.5
    allowed_mask = visible & (rows[None, :] <= rows[:, None])
    place = jnp.dot(member, depth, precision=HIGH) * block_len + (rows % block_len).astype(F32)
    return (allowed_mask, place)


def rope_tables(place, head_dim):
    half = head_dim // 2
    freq = THETA ** (-2.0 * jnp.arange(half, dtype=F32) / head_dim)
    angle = place[:, None] * freq[None, :]
    return (jnp.cos(angle), jnp.sin(angle))


def rotate(values, cosine, sine, sign):
    half = values.shape[-1] // 2
    first, second = values[..., :half], values[..., half:]
    return jnp.concatenate(
        [first * cosine - sign * second * sine, second * cosine + sign * first * sine], -1
    )


def normalize(values):
    inverse = lax.rsqrt(jnp.mean(values * values, axis=-1, keepdims=True) + EPS)
    return (values * inverse, inverse)


def norm_back(grad_normed, gain, values):
    scaled, inverse = normalize(values)
    grad_scaled = grad_normed * gain
    inner = jnp.mean(grad_scaled * scaled, axis=-1, keepdims=True)
    return inverse * (grad_scaled - scaled * inner)


def dot_nn(left, right):
    return jnp.dot(left, right, preferred_element_type=F32)


def dot_nt(left, right):
    return lax.dot_general(left, right, (((1,), (1,)), ((), ())), preferred_element_type=F32)


def dot_tn(left, right):
    return lax.dot_general(left, right, (((0,), (0,)), ((), ())), preferred_element_type=F32)


def flip(index, mask):
    out = index
    bit = 1
    while bit <= mask:
        if mask & bit:
            out = out + bit * (1 - 2 * (index // bit % 2))
        bit *= 2
    return out


class Links:
    def __init__(self, tp, send_sems, recv_sems, local_sems):
        self.tp = tp
        self.di = lax.axis_index("dp")
        self.ti = lax.axis_index("tensor")
        self.send_sems, self.recv_sems, self.local_sems = send_sems, recv_sems, local_sems
        self.used = 0
        self.used_local = 0

    def partner(self, mask):
        return (flip(self.di, mask // self.tp), flip(self.ti, mask % self.tp))

    def greet(self, masks):
        barrier = pltpu.get_barrier_semaphore()
        for mask in masks:
            pl.semaphore_signal(barrier, inc=1, device_id=self.partner(mask), device_id_type=MESH)
        pl.semaphore_wait(barrier, len(masks))

    def remote(self, src, dst, mask):
        index = self.used
        self.used += 1
        return pltpu.make_async_remote_copy(
            src_ref=src,
            dst_ref=dst,
            send_sem=self.send_sems.at[index],
            recv_sem=self.recv_sems.at[index],
            device_id=self.partner(mask),
            device_id_type=MESH,
        )

    def send(self, src, dst, mask):
        copy = self.remote(src, dst, mask)
        copy.start()
        return copy

    def local(self, src, dst):
        copy = pltpu.make_async_copy(src, dst, self.local_sems.at[self.used_local])
        self.used_local += 1
        copy.start()
        return copy


def line_middle(links):
    zi = links.di // 2
    return (zi == 1) | (zi == 2)


class Spread:
    def __init__(self, links, outer, own, block):
        self.links, self.outer = links, outer
        step = 2 * links.tp
        self.middle = line_middle(links)
        self.copies = {k: links.remote(own, block(k), k * step) for k in range(1, outer)}
        if outer == 4:
            self.onward = links.remote(block(2), block(3), step)

    def start(self):
        if self.outer != 4:
            for copy in self.copies.values():
                copy.start()
            return
        self.copies[2].start()
        self.copies[1].start()

        @pl.when(self.middle)
        def _():
            self.copies[3].start()

    def forward(self):
        self.copies[2].wait_recv()
        if self.outer != 4:
            return

        @pl.when(self.middle)
        def _():
            self.onward.start()

    def arrive(self, k):
        if k == 1 or (self.outer != 4 and k != 2):
            self.copies[k].wait_recv()
        elif k == 3:

            @pl.when(self.middle)
            def _():
                self.copies[3].wait_recv()

            @pl.when(jnp.logical_not(self.middle))
            def _():
                self.onward.wait_recv()

    def sent(self):
        if self.outer != 4:
            for copy in self.copies.values():
                copy.wait_send()
            return
        self.copies[1].wait_send()
        self.copies[2].wait_send()

        @pl.when(self.middle)
        def _():
            self.copies[3].wait_send()
            self.onward.wait_send()


class ReduceZ:
    def __init__(self, links, outer, block, held, staged):
        self.links, self.outer, self.block, self.held, self.staged = (
            links,
            outer,
            block,
            held,
            staged,
        )
        step = 2 * links.tp
        self.middle = line_middle(links)
        self.copies = {k: links.remote(block(k), held.at[k], k * step) for k in range(1, outer)}
        if outer == 4:
            self.inward = links.remote(block(3), held.at[0], step)
            self.summed = links.remote(staged, held.at[2], 2 * step)

    def on_ends(self, *actions):
        @pl.when(jnp.logical_not(self.middle))
        def _():
            for action in actions:
                action()

    def on_middle(self, *actions):
        @pl.when(self.middle)
        def _():
            for action in actions:
                action()

    def start(self, k):
        if self.outer != 4 or k == 1:
            self.copies[k].start()
        elif k == 3:
            self.on_ends(self.inward.start)
            self.on_middle(self.copies[3].start)
        elif k == 2:
            self.on_ends(self.copies[2].start)

    def start_all(self):
        for k in range(self.outer - 1, 0, -1):
            self.start(k)

    def pump(self):
        if self.outer != 4:
            return

        def add():
            rows, width = self.staged.shape
            spec = rows_spec(min(rows, 128), width)
            add_pipe(spec, rows, self.block(2), self.held.at[0], self.staged)

        self.on_middle(self.inward.wait_recv, add, self.summed.start)

    def arrive(self):
        if self.outer != 4:
            for copy in self.copies.values():
                copy.wait_recv()
            return
        self.copies[1].wait_recv()
        self.on_middle(self.copies[2].wait_recv, self.copies[3].wait_recv)
        self.on_ends(self.summed.wait_recv)

    def total(self, lo, rows, out):
        width = self.staged.shape[1]
        spec = rows_spec(min(rows, 128), width)

        def add(*refs):
            value = refs[0][...].astype(F32)
            for ref in refs[1:-1]:
                value = value + ref[...].astype(F32)
            refs[-1][...] = value.astype(refs[-1].dtype)

        def over(kept):
            parts = [self.block(0)] + [self.held.at[k] for k in kept]
            parts = [part.at[pl.ds(lo, rows)] for part in parts]
            grid = (rows // min(rows, 128),)
            pipe(add, grid, [spec] * len(parts), [spec], *parts, out)

        if self.outer != 4:
            over(range(1, self.outer))
            return
        self.on_middle(lambda: over([1, 2, 3]))
        self.on_ends(lambda: over([1, 2]))

    def sent(self):
        if self.outer != 4:
            for copy in self.copies.values():
                copy.wait_send()
            return
        self.copies[1].wait_send()
        self.on_middle(self.copies[3].wait_send, self.summed.wait_send)
        self.on_ends(self.copies[2].wait_send, self.inward.wait_send)


def gather_units(links, full, rows):
    tp = links.tp

    def block(m, lo=0, n=None):
        return full.at[pl.ds(m * rows + lo, rows if n is None else n)]

    half = rows // 2
    sent = []

    def send(m, mask, lo=0, n=None):
        copy = links.send(block(m, lo, n), block(m ^ mask, lo, n), mask)
        sent.append(copy)
        return copy

    x = send(0, tp)
    y = send(0, 2)
    c0 = send(0, 1)
    yield
    y.wait_recv()
    low = send(2, tp, half, half)
    c2 = send(2, 1)
    x.wait_recv()
    high = send(tp, 2, 0, half)
    c4 = send(tp, 1)
    yield
    low.wait_recv()
    high.wait_recv()
    c6 = send(tp + 2, 1)
    yield
    for copy in (c0, c2, c4, c6):
        copy.wait_recv()
    for copy in sent:
        copy.wait_send()
    yield


def run(stages):
    for _ in stages:
        pass


def pipe(body, grid, in_specs, out_specs, *refs):
    pltpu.emit_pipeline(body, grid=grid, in_specs=in_specs, out_specs=out_specs)(*refs)


def rows_spec(rows, width):
    return pl.BlockSpec((rows, width), lambda i: (i, 0))


def whole_spec(rows, width):
    return pl.BlockSpec((rows, width), lambda i: (0, 0))


def add_refs(a_ref, b_ref, o_ref):
    o_ref[...] = (a_ref[...].astype(F32) + b_ref[...].astype(F32)).astype(o_ref.dtype)


def add_pipe(spec, rows, a, b, out):
    pipe(add_refs, (rows // spec.block_shape[0],), [spec, spec], [spec], a, b, out)


def nt_body(a_ref, b_ref, o_ref):
    o_ref[...] = dot_nt(a_ref[...], b_ref[...]).astype(BF16)


def nn_body(a_ref, b_ref, o_ref):
    o_ref[...] = dot_nn(a_ref[...], b_ref[...]).astype(BF16)


def tn_body(a_ref, b_ref, o_ref):
    o_ref[...] = dot_tn(a_ref[...], b_ref[...]).astype(BF16)


def weight_grad(acts, grads, out, blocks, first=0, count=None):
    tokens, model = acts.shape
    width = grads.shape[1]
    size = model // blocks
    count = blocks if count is None else count
    pipe(
        tn_body,
        (count,),
        [pl.BlockSpec((tokens, size), lambda i: (0, first + i)), whole_spec(tokens, width)],
        [pl.BlockSpec((size, width), lambda i: (first + i, 0))],
        acts,
        grads,
        out,
    )


class ScatterTensor:
    def __init__(self, links, part, got_c, got_y, far, rows):
        self.links, self.part, self.got_c, self.got_y, self.far = links, part, got_c, got_y, far
        self.rows = rows
        self.model = part.shape[1]
        self.spec = rows_spec(rows // 2, self.model)

    def block(self, mask):
        rows = self.rows
        return self.part.at[
            pl.ds(pl.multiple_of(flip(self.links.ti, mask) * rows, rows), rows)
        ]

    def start(self):
        self.copies = [
            self.links.send(self.block(3), self.got_c.at[1], 1),
            self.links.send(self.block(1), self.got_c.at[0], 1),
        ]

    def across(self):
        self.copies[0].wait_recv()
        add_pipe(self.spec, self.rows, self.block(2), self.got_c.at[1], self.far)
        self.copies.append(self.links.send(self.far, self.got_y, 2))

    def arrive(self):
        self.copies[1].wait_recv()
        self.copies[2].wait_recv()
        return [self.block(0), self.got_c.at[0], self.got_y]

    def sent(self):
        for copy in self.copies:
            copy.wait_send()


class ScatterUnits:
    def __init__(self, links, part, got_c, near, got, rows):
        self.links, self.part, self.got_c, self.near, self.got = links, part, got_c, near, got
        self.rows, self.model = rows, part.shape[1]
        self.sends = []

    def send(self, src, dst, mask):
        copy = self.links.send(src, dst, mask)
        self.sends.append(copy)
        return copy

    def block(self, m):
        return self.part.at[pl.ds(m * self.rows, self.rows)]

    def start(self):
        self.from_c = [self.send(self.block(2 * i + 1), self.got_c.at[i], 1) for i in range(4)]

    def add(self, m, slot, lo, n):
        rows = pl.ds(lo, n)
        add_pipe(
            rows_spec(n, self.model),
            n,
            self.block(m).at[rows],
            self.got_c.at[m // 2].at[rows],
            self.near.at[slot].at[rows],
        )

    def across(self):
        tp, rows, half = self.links.tp, self.rows, self.rows // 2
        low, high = pl.ds(0, half), pl.ds(half, half)
        near, got = self.near, self.got
        for copy in self.from_c:
            copy.wait_recv()
        self.add(6, 2, 0, half)
        self.top = self.send(near.at[2].at[low], got.at[2].at[low], tp)
        self.add(6, 2, half, half)
        self.bottom = self.send(near.at[2].at[high], got.at[2].at[high], 2)
        self.add(4, 0, 0, half)
        self.x_low = self.send(near.at[0].at[low], got.at[0].at[low], tp)
        self.add(2, 1, half, half)
        self.y_high = self.send(near.at[1].at[high], got.at[1].at[high], 2)

    def finish(self):
        tp, half = self.links.tp, self.rows // 2
        low, high = pl.ds(0, half), pl.ds(half, half)
        near, got = self.near, self.got

        def add3(m, slot, rows):
            def body(a_ref, b_ref, c_ref, o_ref):
                o_ref[...] = (
                    a_ref[...].astype(F32) + b_ref[...].astype(F32) + c_ref[...].astype(F32)
                ).astype(BF16)

            spec = rows_spec(half, self.model)
            pipe(
                body,
                (1,),
                [spec] * 3,
                [spec],
                self.block(m).at[rows],
                self.got_c.at[m // 2].at[rows],
                got.at[2].at[rows],
                near.at[slot].at[rows],
            )

        self.top.wait_recv()
        add3(2, 1, low)
        self.y_low = self.send(near.at[1].at[low], got.at[1].at[low], 2)
        self.bottom.wait_recv()
        add3(4, 0, high)
        self.x_high = self.send(near.at[0].at[high], got.at[0].at[high], tp)

    def arrive(self):
        for copy in (self.x_low, self.x_high, self.y_low, self.y_high):
            copy.wait_recv()
        return [self.block(0), self.got_c.at[0], self.got.at[0], self.got.at[1]]

    def sent(self):
        for copy in self.sends:
            copy.wait_send()


def sum_refs(refs):
    value = refs[0][...].astype(F32)
    for ref in refs[1:]:
        value = value + ref[...].astype(F32)
    return value


class GatherTree:
    def __init__(self, links, full, rows):
        self.links, self.full, self.rows = links, full, rows

    def block(self, mask):
        rows = self.rows
        return self.full.at[
            pl.ds(pl.multiple_of(flip(self.links.ti, mask) * rows, rows), rows)
        ]

    def start(self):
        self.y = self.links.send(self.block(0), self.block(0), 2)
        self.c = self.links.send(self.block(0), self.block(0), 1)

    def across(self):
        self.y.wait_recv()
        self.yc = self.links.send(self.block(2), self.block(2), 1)

    def arrive(self):
        self.c.wait_recv()
        self.yc.wait_recv()

    def sent(self):
        for copy in (self.y, self.c, self.yc):
            copy.wait_send()


def greet_all(links, outer):
    step = 2 * links.tp
    links.greet([1, 2, links.tp] + [k * step for k in range(1, outer)])


def forward_kernel(
    outer,
    tp,
    wa,
    wg,
    wu,
    wd,
    gn,
    x,
    xh,
    cot,
    cosine,
    sine,
    bias,
    wa_all,
    gate_w,
    up_w,
    down_w,
    gain_rows,
    h1,
    qkv,
    probs,
    att,
    x1,
    h2,
    cot_all,
    gate,
    upper,
    hid,
    grad_down,
    gn_all,
    part,
    got_c,
    got_y,
    far,
    send_sems,
    recv_sems,
    local_sems,
):
    links = Links(tp, send_sems, recv_sems, local_sems)
    shard, attn_width = wa.shape
    units = gate_w.shape[1]
    rows, model = xh.shape
    tree_len = rows * tp
    q_width = att.shape[1]
    qkv_width = qkv.shape[1]
    kv_width = (qkv_width - q_width) // 2
    head = HEAD_SIZE
    xi = links.di % 2
    greet_all(links, outer)

    def shard_block(full, k):
        return full.at[pl.ds(pl.multiple_of((2 * k + xi) * shard, shard), shard)]

    mine = pl.ds(pl.multiple_of(xi * units, units), units)
    peers = pl.ds(pl.multiple_of((1 - xi) * units, units), units)
    place = pl.ds(pl.multiple_of(xi * shard, shard), shard)

    def send_pair(w, full):
        return links.send(w.at[:, peers], full.at[place], tp)

    def mlp_spread(full):
        return Spread(
            links,
            outer,
            full.at[pl.ds(0, 2 * shard)],
            lambda k: full.at[pl.ds(k * 2 * shard, 2 * shard)],
        )

    gains = Spread(links, outer, gn, lambda k: shard_block(gn_all, k))
    attn = Spread(links, outer, wa, lambda k: shard_block(wa_all, k))
    gains.start()
    across_gn = [links.send(gn, shard_block(gn_all, 0), tp)]
    attn.start()
    across = [links.send(wa, shard_block(wa_all, 0), tp)]
    pair = [send_pair(wg, gate_w)]
    here = [
        links.local(gn, shard_block(gn_all, 0)),
        links.local(wa, shard_block(wa_all, 0)),
        links.local(cot, cot_all.at[pl.ds(0, rows)]),
    ]
    for w, full in ((wg, gate_w), (wu, up_w), (wd, down_w)):
        here.append(links.local(w.at[:, mine], full.at[place]))

    gains.forward()
    for k in range(1, outer):
        gains.arrive(k)
        across_gn.append(links.send(shard_block(gn_all, k), shard_block(gn_all, k), tp))
    for copy in across_gn:
        copy.wait_recv()
    for copy in here:
        copy.wait()

    def gain_rows_of(g_ref, o_ref):
        lane = lax.broadcasted_iota(jnp.int32, (8, 128), 1)
        row = lax.broadcasted_iota(jnp.int32, (8, 128), 0)
        pick = jnp.where((row < 2) & (lane == row * 64), 1.0, 0.0).astype(BF16)
        o_ref[...] = dot_nt(pick, g_ref[...])

    pipe(gain_rows_of, (1,), [whole_spec(model, 128)], [whole_spec(8, model)], gn_all, gain_rows)
    spec = rows_spec(rows // 2, model)
    gain_spec = whole_spec(8, model)

    def scale_tokens(x_ref, g_ref, o_ref):
        o_ref[...] = (x_ref[...] * g_ref[0:1]).astype(BF16)

    tree = GatherTree(links, h1, rows)
    pipe(scale_tokens, (2,), [spec, gain_spec], [spec], xh, gain_rows, tree.block(0))
    tree.start()

    spreads = [mlp_spread(full) for full in (gate_w, up_w, down_w)]
    attn.forward()
    across.append(links.send(shard_block(wa_all, 2), shard_block(wa_all, 2), tp))
    pair[0].wait_recv()
    spreads[0].start()
    tree.across()
    for k in range(1, outer):
        if k != 2:
            attn.arrive(k)
            across.append(links.send(shard_block(wa_all, k), shard_block(wa_all, k), tp))
        if k == 1:
            pair.append(send_pair(wu, up_w))
    pair.append(send_pair(wd, down_w))
    tree.arrive()
    pair[1].wait_recv()
    spreads[1].start()
    for copy in across:
        copy.wait_recv()

    def project(x_ref, w_ref, cos_ref, sin_ref, out_ref):
        raw = dot_nn(x_ref[...], w_ref[...])
        for slot in range((q_width + kv_width) // head):
            cols = slice(slot * head, (slot + 1) * head)
            out_ref[:, cols] = rotate(raw[:, cols], cos_ref[...], sin_ref[...], 1.0).astype(BF16)
        out_ref[:, q_width + kv_width :] = raw[:, q_width + kv_width :].astype(BF16)

    pipe(
        project,
        (tp,),
        [
            rows_spec(rows, model),
            whole_spec(model, qkv_width),
            rows_spec(rows, head // 2),
            rows_spec(rows, head // 2),
        ],
        [rows_spec(rows, qkv_width)],
        h1,
        wa_all.at[:, pl.ds(0, qkv_width)],
        cosine,
        sine,
        qkv,
    )
    spreads[0].forward()
    pair[2].wait_recv()
    spreads[2].start()

    group = q_width // kv_width

    def attend(q_ref, k_ref, v_ref, b_ref, p_ref, o_ref):
        scores = dot_nt(q_ref[...], k_ref[...]) * (head**-0.5) + b_ref[...].astype(F32)
        weights = jnp.exp(scores - jnp.max(scores, axis=-1, keepdims=True))
        weights = (weights / jnp.sum(weights, axis=-1, keepdims=True)).astype(BF16)
        p_ref[0] = weights
        o_ref[...] = dot_nn(weights, v_ref[...]).astype(BF16)

    k_at, v_at = q_width // head, (q_width + kv_width) // head
    pipe(
        attend,
        (tp, q_width // head),
        [
            pl.BlockSpec((rows, head), lambda i, h: (i, h)),
            pl.BlockSpec((tree_len, head), lambda i, h: (0, k_at + h // group)),
            pl.BlockSpec((tree_len, head), lambda i, h: (0, v_at + h // group)),
            pl.BlockSpec((rows, tree_len), lambda i, h: (i, 0)),
        ],
        [
            pl.BlockSpec((1, rows, tree_len), lambda i, h: (h, i, 0)),
            pl.BlockSpec((rows, head), lambda i, h: (i, h)),
        ],
        qkv,
        qkv,
        qkv,
        bias,
        probs,
        att,
    )
    pipe(
        nt_body,
        (tp,),
        [rows_spec(rows, q_width), whole_spec(model, q_width)],
        [rows_spec(rows, model)],
        att,
        wa_all.at[:, pl.ds(qkv_width, q_width)],
        part,
    )
    mixed = ScatterTensor(links, part, got_c, got_y, far, rows)
    mixed.start()
    mixed.across()
    parts = mixed.arrive()

    def residual(x_ref, a_ref, b_ref, c_ref, g_ref, x1_ref, h_ref):
        total = x_ref[...] + sum_refs((a_ref, b_ref, c_ref))
        x1_ref[...] = total
        h_ref[...] = (normalize(total)[0] * g_ref[1:2]).astype(BF16)

    pipe(
        residual,
        (2,),
        [spec] * 4 + [gain_spec],
        [spec] * 2,
        x,
        *parts,
        gain_rows,
        x1,
        h2.at[pl.ds(0, rows)],
    )
    stages = gather_units(links, h2, rows)
    next(stages)
    later = gather_units(links, cot_all, rows)
    next(later)
    next(stages)
    spreads[1].forward()
    next(stages)
    next(later)
    next(stages)

    for spread in spreads[:2]:
        for k in range(1, outer):
            spread.arrive(k)

    def expand(x_ref, g_ref, u_ref, go_ref, uo_ref, h_ref):
        g = dot_nn(x_ref[...], g_ref[...])
        u = dot_nn(x_ref[...], u_ref[...])
        go_ref[...] = g.astype(BF16)
        uo_ref[...] = u.astype(BF16)
        h_ref[...] = (g * jax.nn.sigmoid(g) * u).astype(BF16)

    pipe(
        expand,
        (2 * tp,),
        [rows_spec(rows, model), whole_spec(model, units), whole_spec(model, units)],
        [rows_spec(rows, units)] * 3,
        h2,
        gate_w,
        up_w,
        gate,
        upper,
        hid,
    )
    run(later)
    spreads[2].forward()
    weight_grad(cot_all, hid, grad_down, 4)
    for k in range(1, outer):
        spreads[2].arrive(k)
    for spread in [gains, attn] + spreads:
        spread.sent()
    for copy in across_gn + across + pair:
        copy.wait_send()
    tree.sent()
    mixed.sent()


def backward_kernel(
    outer,
    tp,
    wa_all,
    gate_w,
    up_w,
    down_w,
    gain_rows,
    h1,
    qkv,
    probs,
    att,
    x1,
    h2,
    cot_all,
    gate,
    upper,
    hid,
    grad_down,
    x,
    cosine,
    sine,
    out,
    grad_tok,
    down_mine,
    down_theirs,
    gate_mine,
    gate_theirs,
    up_mine,
    up_theirs,
    out_total,
    qkv_total,
    dgate,
    dupper,
    e_part,
    y_part,
    e_got_c,
    y_got_c,
    e_near,
    y_near,
    e_got,
    y_got,
    dx1,
    dx1_low,
    dout,
    dscores,
    dqkv,
    f_part,
    f_got_c,
    f_got_y,
    f_far,
    grad_gate,
    grad_up,
    grad_out,
    grad_qkv,
    out_pair,
    qkv_pair,
    out_sum,
    qkv_sum,
    down_held,
    gate_held,
    up_held,
    out_held,
    qkv_held,
    down_staged,
    gate_staged,
    up_staged,
    out_staged,
    qkv_staged,
    down_give,
    gate_give,
    up_give,
    send_sems,
    recv_sems,
    local_sems,
):
    links = Links(tp, send_sems, recv_sems, local_sems)
    rows, model = x.shape
    tree_len = rows * tp
    units = gate_w.shape[1]
    q_width = att.shape[1]
    qkv_width = qkv.shape[1]
    kv_width = (qkv_width - q_width) // 2
    head = HEAD_SIZE
    group = q_width // kv_width
    shard = model // (2 * outer)
    xi = links.di % 2
    half = pl.multiple_of(xi * shard, shard)
    other = pl.multiple_of((1 - xi) * shard, shard)
    spec = rows_spec(rows // 2, model)
    gain_spec = whole_spec(8, model)
    greet_all(links, outer)

    def mlp_reduce(grad, held, staged):
        return ReduceZ(
            links, outer, lambda k: grad.at[pl.ds(k * 2 * shard, 2 * shard)], held, staged
        )

    def trade(reduce, mine, give, theirs):
        reduce.arrive()
        reduce.total(other, shard, give)
        copy = links.send(give, theirs, tp)
        reduce.total(half, shard, mine)
        return copy

    red_down = mlp_reduce(grad_down, down_held, down_staged)
    red_gate = mlp_reduce(grad_gate, gate_held, gate_staged)
    red_up = mlp_reduce(grad_up, up_held, up_staged)
    red_down.start_all()

    def contract(c_ref, w_ref, g_ref, u_ref, dg_ref, du_ref):
        dhid = dot_nn(c_ref[...], w_ref[...])
        g = g_ref[...].astype(F32)
        sigma = jax.nn.sigmoid(g)
        dg_ref[...] = (dhid * u_ref[...].astype(F32) * sigma * (1.0 + g * (1.0 - sigma))).astype(
            BF16
        )
        du_ref[...] = (dhid * g * sigma).astype(BF16)

    unit_spec = rows_spec(rows, units)
    pipe(
        contract,
        (2 * tp,),
        [rows_spec(rows, model), whole_spec(model, units), unit_spec, unit_spec],
        [unit_spec] * 2,
        cot_all,
        down_w,
        gate,
        upper,
        dgate,
        dupper,
    )

    def every_other(first, block_rows, width):
        return pl.BlockSpec((block_rows, width), lambda i: (2 * i + first, 0))

    def back(dg_ref, du_ref, g_ref, u_ref, o_ref):
        o_ref[...] = (dot_nt(dg_ref[...], g_ref[...]) + dot_nt(du_ref[...], u_ref[...])).astype(
            BF16
        )

    def back_blocks(first):
        pipe(
            back,
            (tp,),
            [every_other(first, rows, units)] * 2 + [whole_spec(model, units)] * 2,
            [every_other(first, rows, model)],
            dgate,
            dupper,
            gate_w,
            up_w,
            e_part,
        )

    def down_blocks(first):
        pipe(
            nt_body,
            (tp,),
            [every_other(first, rows, units), whole_spec(model, units)],
            [every_other(first, rows, model)],
            hid,
            down_w,
            y_part,
        )

    e_sum = ScatterUnits(links, e_part, e_got_c, e_near, e_got, rows)
    y_sum = ScatterUnits(links, y_part, y_got_c, y_near, y_got, rows)
    back_blocks(1)
    e_sum.start()
    red_down.pump()
    back_blocks(0)
    e_sum.across()
    weight_grad(h2, dgate, grad_gate, 4)
    red_gate.start_all()
    e_sum.finish()
    weight_grad(h2, dupper, grad_up, 4)
    red_up.start_all()
    down_blocks(1)
    y_sum.start()
    down_blocks(0)
    trades = [trade(red_down, down_mine, down_give, down_theirs)]

    tree = GatherTree(links, dx1_low, rows)

    def through_norm(c_ref, x_ref, g_ref, *refs):
        value = c_ref[...].astype(F32) + norm_back(sum_refs(refs[:-2]), g_ref[1:2], x_ref[...])
        refs[-2][...] = value
        refs[-1][...] = value.astype(BF16)

    parts = e_sum.arrive()
    pipe(
        through_norm,
        (2,),
        [spec, spec, gain_spec] + [spec] * len(parts),
        [spec] * 2,
        cot_all.at[pl.ds(0, rows)],
        x1,
        gain_rows,
        *parts,
        dx1,
        tree.block(0),
    )
    tree.start()
    y_sum.across()
    red_gate.pump()
    tree.across()
    tree.arrive()

    pipe(
        nn_body,
        (tp,),
        [rows_spec(rows, model), whole_spec(model, q_width)],
        [rows_spec(rows, q_width)],
        dx1_low,
        wa_all.at[:, pl.ds(qkv_width, q_width)],
        dout,
    )

    def pair_block(full, k, at):
        return full.at[pl.ds(pl.multiple_of(k * 2 * shard + at, shard), shard)]

    def pair_send(grad, held, k):
        return links.send(pair_block(grad, k, other), held.at[k], tp)

    red_out = ReduceZ(links, outer, lambda k: out_sum.at[k], out_held, out_staged)
    red_qkv = ReduceZ(links, outer, lambda k: qkv_sum.at[k], qkv_held, qkv_staged)
    weight_grad(dx1_low, att, grad_out, 4)
    order = list(range(outer - 1, -1, -1))
    out_across = {k: pair_send(grad_out, out_pair, k) for k in order}
    y_sum.finish()

    def score_grads(do_ref, k_ref, v_ref, p_ref, cos_ref, sin_ref, ds_ref, dq_ref):
        p = p_ref[0].astype(F32)
        dp = dot_nt(do_ref[...], v_ref[...])
        inner = jnp.sum(p * dp, axis=-1, keepdims=True)
        ds = (p * (dp - inner) * (head**-0.5)).astype(BF16)
        ds_ref[0] = ds
        dq_ref[...] = rotate(dot_nn(ds, k_ref[...]), cos_ref[...], sin_ref[...], -1.0).astype(BF16)

    k_at, v_at = q_width // head, (q_width + kv_width) // head
    pipe(
        score_grads,
        (tp, q_width // head),
        [
            pl.BlockSpec((rows, head), lambda i, h: (i, h)),
            pl.BlockSpec((tree_len, head), lambda i, h: (0, k_at + h // group)),
            pl.BlockSpec((tree_len, head), lambda i, h: (0, v_at + h // group)),
            pl.BlockSpec((1, rows, tree_len), lambda i, h: (h, i, 0)),
            pl.BlockSpec((rows, head // 2), lambda i, h: (i, 0)),
            pl.BlockSpec((rows, head // 2), lambda i, h: (i, 0)),
        ],
        [
            pl.BlockSpec((1, rows, tree_len), lambda i, h: (h, i, 0)),
            pl.BlockSpec((rows, head), lambda i, h: (i, h)),
        ],
        dout,
        qkv,
        qkv,
        probs,
        cosine,
        sine,
        dscores,
        dqkv,
    )

    def key_grads(ds_ref, p_ref, q_ref, do_ref, cos_ref, sin_ref, dkv_ref):
        dk = jnp.zeros((rows, head), F32)
        dv = jnp.zeros((rows, head), F32)
        for h in range(group):
            cols = slice(h * head, (h + 1) * head)
            dk = dk + dot_tn(ds_ref[h], q_ref[:, cols])
            dv = dv + dot_tn(p_ref[h], do_ref[:, cols])
        dkv_ref[:, :head] = rotate(dk, cos_ref[...], sin_ref[...], -1.0).astype(BF16)
        dkv_ref[:, head:] = dv.astype(BF16)

    by_key = pl.BlockSpec((group, tree_len, rows), lambda i: (0, 0, i))
    pipe(
        key_grads,
        (tp,),
        [by_key, by_key]
        + [whole_spec(tree_len, q_width)] * 2
        + [rows_spec(rows, head // 2)] * 2,
        [rows_spec(rows, 2 * kv_width)],
        dscores,
        probs,
        qkv.at[:, pl.ds(0, q_width)],
        dout,
        cosine,
        sine,
        dqkv.at[:, pl.ds(q_width, 2 * kv_width)],
    )

    def pair_add(grad, held, total, k):
        add_pipe(
            rows_spec(min(shard, 128), grad.shape[1]),
            shard,
            pair_block(grad, k, half),
            held.at[k],
            total.at[k],
        )

    qkv_across = {}
    for k in order:
        weight_grad(h1, dqkv, grad_qkv, outer, k, 1)
        qkv_across[k] = pair_send(grad_qkv, qkv_pair, k)
    pipe(
        nt_body,
        (tp,),
        [rows_spec(rows, qkv_width), whole_spec(model, qkv_width)],
        [rows_spec(rows, model)],
        dqkv,
        wa_all.at[:, pl.ds(0, qkv_width)],
        f_part,
    )
    f_sum = ScatterTensor(links, f_part, f_got_c, f_got_y, f_far, rows)
    f_sum.start()
    f_sum.across()
    red_up.pump()
    for k in order:
        out_across[k].wait_recv()
        pair_add(grad_out, out_pair, out_sum, k)
        if k:
            red_out.start(k)
    trades.append(trade(red_gate, gate_mine, gate_give, gate_theirs))

    def finish_output(x_ref, *refs):
        refs[-1][...] = (x_ref[...] + sum_refs(refs[:-1])).astype(BF16)

    parts = y_sum.arrive()
    pipe(finish_output, (2,), [spec] * (1 + len(parts)), [spec], x1, *parts, out)

    for k in order:
        qkv_across[k].wait_recv()
        pair_add(grad_qkv, qkv_pair, qkv_sum, k)
        if k:
            red_qkv.start(k)

    def finish_tokens(d_ref, x_ref, g_ref, *refs):
        refs[-1][...] = (
            d_ref[...] + norm_back(sum_refs(refs[:-1]), g_ref[0:1], x_ref[...])
        ).astype(BF16)

    parts = f_sum.arrive()
    pipe(
        finish_tokens,
        (2,),
        [spec, spec, gain_spec] + [spec] * len(parts),
        [spec],
        dx1,
        x,
        gain_rows,
        *parts,
        grad_tok,
    )
    trades.append(trade(red_up, up_mine, up_give, up_theirs))
    red_out.pump()
    red_qkv.pump()
    red_out.arrive()
    red_out.total(0, shard, out_total)
    red_qkv.arrive()
    red_qkv.total(0, shard, qkv_total)
    for copy in trades:
        copy.wait()
    for copy in list(out_across.values()) + list(qkv_across.values()):
        copy.wait_send()
    for item in (red_down, red_gate, red_up, red_out, red_qkv, e_sum, y_sum, f_sum, tree):
        item.sent()


def call(kernel, name, collective, count, shapes, operands):
    anywhere = pl.BlockSpec(memory_space=pl.ANY)
    return pl.pallas_call(
        kernel,
        out_shape=[jax.ShapeDtypeStruct(shape, dtype) for shape, dtype in shapes],
        in_specs=[anywhere] * len(operands),
        out_specs=[anywhere] * len(shapes),
        scratch_shapes=[
            pltpu.SemaphoreType.DMA((count,)),
            pltpu.SemaphoreType.DMA((count,)),
            pltpu.SemaphoreType.DMA((8,)),
        ],
        compiler_params=pltpu.CompilerParams(
            collective_id=collective, has_side_effects=True, vmem_limit_bytes=VMEM_LIMIT
        ),
        name=name,
    )(*operands)


def make_body(dp, tp):
    outer = dp // 2
    assert tp == 4 and dp == 2 * outer and outer >= 4 and outer & (outer - 1) == 0

    def swap(value, mask):
        return lax.ppermute(value, ("dp", "tensor"), [(i, i ^ mask) for i in range(dp * tp)])

    def relative(value, zi):
        width = value.shape[-1] // outer
        step = 1
        while step < outer:
            blocks = [value[..., i * width : (i + 1) * width] for i in range(outer)]
            swapped = jnp.concatenate([blocks[i ^ step] for i in range(outer)], -1)
            value = jnp.where((zi // step) % 2 == 1, swapped, value)
            step *= 2
        return value

    def body(
        tokens,
        parents,
        attn_gain,
        w_query,
        key_matrix,
        value_matrix,
        w_out,
        mlp_gain,
        w_gate,
        w_up,
        w_down,
        cotangent,
    ):
        di = lax.axis_index("dp")
        zi = di // 2
        upper_x = di % 2 == 1
        rows, model = tokens.shape
        tree_len = rows * tp
        q_width = w_query.shape[1]
        kv_width = key_matrix.shape[1]
        qkv_width = q_width + 2 * kv_width
        heads = q_width // HEAD_SIZE
        assert kv_width == HEAD_SIZE
        shard = w_query.shape[0]
        units = w_gate.shape[1] // 2

        wa = jnp.concatenate([w_query, key_matrix, value_matrix, w_out.T], 1)
        gn = jnp.concatenate(
            [
                jnp.broadcast_to(attn_gain[:, None], (shard, 64)),
                jnp.broadcast_to(mlp_gain[:, None], (shard, 64)),
            ],
            1,
        )
        allowed_mask, place = tree_tables(parents[0], tree_len, BLK)
        cosine, sine = rope_tables(place, HEAD_SIZE)
        bias = jnp.where(allowed_mask, 0.0, NEG).astype(BF16)
        x = relative(tokens, zi).astype(F32)
        xh = normalize(x)[0]
        cot = relative(cotangent, zi)
        (
            wa_all,
            gate_w,
            up_w,
            down_w,
            gain_rows,
            h1,
            qkv,
            probs,
            att,
            x1,
            h2,
            cot_all,
            gate,
            upper,
            hid,
            grad_down,
        ) = call(
            functools.partial(forward_kernel, outer, tp),
            "layer_forward",
            0,
            50 + 7 * outer,
            [
                ((model, qkv_width + q_width), BF16),
                ((model, units), BF16),
                ((model, units), BF16),
                ((model, units), BF16),
                ((8, model), F32),
                ((tree_len, model), BF16),
                ((tree_len, qkv_width), BF16),
                ((heads, tree_len, tree_len), BF16),
                ((tree_len, q_width), BF16),
                ((rows, model), F32),
                ((2 * tree_len, model), BF16),
                ((2 * tree_len, model), BF16),
                ((2 * tree_len, units), BF16),
                ((2 * tree_len, units), BF16),
                ((2 * tree_len, units), BF16),
                ((model, units), BF16),
                ((model, 128), BF16),
                ((tree_len, model), BF16),
                ((2, rows, model), BF16),
                ((rows, model), BF16),
                ((rows, model), BF16),
            ],
            (wa, w_gate, w_up, w_down.T, gn, x, xh, cot, cosine, sine, bias),
        )[:16]

        mlp_held = [((outer, 2 * shard, units), BF16)]
        (
            out,
            grad_tok,
            down_mine,
            down_theirs,
            gate_mine,
            gate_theirs,
            up_mine,
            up_theirs,
            out_total,
            qkv_total,
        ) = call(
            functools.partial(backward_kernel, outer, tp),
            "layer_backward",
            1,
            60 + 10 * outer,
            [((rows, model), BF16)] * 2
            + [((shard, units), F32), ((shard, units), BF16)] * 3
            + [((shard, q_width), F32), ((shard, qkv_width), F32)]
            + [((2 * tree_len, units), BF16)] * 2
            + [((2 * tree_len, model), BF16)] * 2
            + [((4, rows, model), BF16)] * 2
            + [((3, rows, model), BF16)] * 4
            + [((rows, model), F32), ((tree_len, model), BF16)]
            + [((tree_len, q_width), BF16), ((heads, tree_len, tree_len), BF16)]
            + [((tree_len, qkv_width), BF16), ((tree_len, model), BF16)]
            + [((2, rows, model), BF16)]
            + [((rows, model), BF16)] * 2
            + [((model, units), BF16)] * 2
            + [((model, q_width), BF16), ((model, qkv_width), BF16)]
            + [((outer, shard, q_width), BF16), ((outer, shard, qkv_width), BF16)] * 2
            + mlp_held * 3
            + [((outer, shard, q_width), BF16), ((outer, shard, qkv_width), BF16)]
            + [((2 * shard, units), BF16)] * 3
            + [((shard, q_width), BF16), ((shard, qkv_width), BF16)]
            + [((shard, units), BF16)] * 3,
            (
                wa_all,
                gate_w,
                up_w,
                down_w,
                gain_rows,
                h1,
                qkv,
                probs,
                att,
                x1,
                h2,
                cot_all,
                gate,
                upper,
                hid,
                grad_down,
                x,
                cosine,
                sine,
            ),
        )[:10]

        def order_x(mine, theirs):
            theirs = theirs.astype(F32)
            low = jnp.where(upper_x, theirs, mine)
            high = jnp.where(upper_x, mine, theirs)
            return jnp.concatenate([low, high], 1)

        grad_gate = order_x(gate_mine, gate_theirs)
        grad_up = order_x(up_mine, up_theirs)
        grad_query = qkv_total[:, :q_width]
        grad_key = qkv_total[:, q_width : q_width + kv_width]
        grad_value = qkv_total[:, q_width + kv_width :]

        gain_sums = jnp.stack(
            [
                jnp.sum(w_query.astype(F32) * grad_query, 1)
                + jnp.sum(key_matrix.astype(F32) * grad_key, 1)
                + jnp.sum(value_matrix.astype(F32) * grad_value, 1),
                jnp.sum(w_gate.astype(F32) * grad_gate, 1)
                + jnp.sum(w_up.astype(F32) * grad_up, 1),
            ]
        )
        gain_sums = gain_sums + swap(gain_sums, 1)
        gain_sums = gain_sums + swap(gain_sums, 2)
        return (
            relative(out, zi),
            relative(grad_tok, zi),
            gain_sums[0] / attn_gain.astype(F32),
            grad_query,
            grad_key,
            grad_value,
            out_total.T,
            gain_sums[1] / mlp_gain.astype(F32),
            grad_gate,
            grad_up,
            order_x(down_mine, down_theirs).T,
        )

    return body


def solution(mesh):
    in_specs = (
        P(("dp", "tensor"), None),
        P("dp", None),
        P("dp"),
        P("dp", "tensor"),
        P("dp", "tensor"),
        P("dp", "tensor"),
        P("tensor", "dp"),
        P("dp"),
        P("dp", "tensor"),
        P("dp", "tensor"),
        P("tensor", "dp"),
        P(("dp", "tensor"), None),
    )
    out_specs = (
        P(("dp", "tensor"), None),
        P(("dp", "tensor"), None),
        P("dp"),
        P("dp", "tensor"),
        P("dp", "tensor"),
        P("dp", "tensor"),
        P("tensor", "dp"),
        P("dp"),
        P("dp", "tensor"),
        P("dp", "tensor"),
        P("tensor", "dp"),
    )
    body = make_body(mesh.shape["dp"], mesh.shape["tensor"])
    return jax.shard_map(body, mesh=mesh, in_specs=in_specs, out_specs=out_specs, check_vma=False)
```

time: 976 us -> 748 us (0.77)
  Pallas kernels: 396 us -> 686 us
  waiting for transfers between devices: 242 us -> 0.01 us
  matrix products: 118 us -> 12.5 us
  other arithmetic: 89 us -> 21.5 us
  starting transfers between devices: 64.8 us -> 1.48 us
  local copies, waits for them, and re-layouts: 46.7 us -> 11.4 us
    pallas_call x1 -> x2, Pallas kernels: 396 us -> 686 us  [call(): pl.pallas_call(kernel, out_shape=[jax.ShapeDtypeStruct(shape, dtype) for...]
    ppermute x35 -> x2, waiting for transfers between devices: 242 us -> 0.01 us  [swap(): lax.ppermute(value, ('dp', 'tensor'), [(i, i ^ mask) for i in range(dp *...]
    dot_general x14 -> x0, matrix products: 111 us -> none  [the longest x4 51.1 us: dot_nt(): lax.dot_general(left, right, (((1,), (1,)), ((), ())), preferred_element_...]
    ppermute x35 -> x2, starting transfers between devices: 64.8 us -> 1.48 us  [swap(): lax.ppermute(value, ('dp', 'tensor'), [(i, i ^ mask) for i in range(dp *...]
    add x10 -> x3, other arithmetic: 20.8 us -> 0.02 us  [the longest x1 0.01 us: body(): gain_sums = gain_sums + swap(gain_sums, 1)]
    convert_element_type x15 -> x0, other arithmetic: 18.3 us -> none  [the longest x2 4.3 us: scatter_units(): got = swap(jnp.stack([part[1], part[3], part[5], part[7]]), 1).astype(F32)]
    slice x14 -> x1, local copies, waits for them, and re-layouts: 11.8 us -> 0.01 us  [body(): gain_sums[1] / mlp_gain.astype(F32)]
  transfers between devices with their start and end apart: 35 -> 2, of which waited for: 11 -> 0; matrix products, arithmetic and copies ran while one was open for 20% -> 1% of each run, Pallas kernels for 0% -> 0%
where the time goes in v3:
time: 748 us; the launch traced here: 734 us
  Pallas kernels  686 us (92%)
  other arithmetic  21.5 us (3%)
  matrix products  12.5 us (2%)
  local copies, waits for them, and re-layouts  11.4 us (2%)
    pallas_call x2, Pallas kernels, call(): pl.pallas_call(kernel, out_shape=[jax.ShapeDtypeStruct(shape, dtype) for...  686 us
  transfers between devices with their start and end apart: 2, of which 0 were waited for; matrix products, arithmetic and copies ran while one was open for 1% of the time, Pallas kernels for 0%

profile of v3, /device:TPU:0, one launch (start us, length us, event | category | flops | bytes accessed | tf_op | source)
XLA Modules:
  0.0 734.2 jit_solution(8914106502412025213)
XLA Ops:
  0.8 1.0 fusion.22
  1.7 1.0 fusion.21
  7.3 0.9 fusion.46
  8.7 1.1 copy.23
  9.8 1.3 fusion.2
  11.1 1.4 copy.24
  14.1 1.3 copy-done.15
  15.4 3.4 select_convert_fusion.bias
  19.7 3.0 multiply_sine_fusion
  22.7 1.4 maximum_select_fusion.3.cot
  24.1 1.5 broadcast_multiply_fusion.xh
  25.7 1.0 pad_maximum_fusion.2.wa
  26.7 365.6 %layer_forward.1 = (bf16[2048,1536]{1,0:T(8,128)(2,1)}, bf16[2048,1024]{1,0:T(8,128)(2,1)}, bf16[2048,1024]{1,0:T(8,128)(2,1)}, bf16[2048,1024]{1,0:T(8,128)(2,1...) custom-call(bf16[256,1536]{1,0:T(8,128)(2,1)} %pad_maximum_fusion.2., ...), custom_call_target="tpu_custom_call" | custom-call | tf_op jit(solution)/shard_map/layer_forward/pallas_call | solution.py:1165
  392.4 320.1 %layer_backward.1 = (bf16[256,2048]{1,0:T(8,128)(2,1)}, bf16[256,2048]{1,0:T(8,128)(2,1)}, f32[256,1024]{1,0:T(8,128)}, bf16[256,1024]{1,0:T(8,128)(2,1)}, f32[2...) custom-call(bf16[2048,1536]{1,0:T(8,128)(2,1)} %get-tuple-element.37, ...), custom_call_target="tpu_custom_call" | custom-call | tf_op jit(solution)/shard_map/layer_backward/pallas_call | solution.py:1165
  712.5 2.0 multiply_reduce_fusion.3
  714.5 1.9 multiply_reduce_fusion.5
  717.6 1.6 multiply_reduce_fusion.1
  720.4 1.6 multiply_reduce_fusion
  722.3 1.0 copy-done.6
  724.2 1.4 maximum_select_fusion.7
  725.5 1.4 maximum_select_fusion.5
  727.3 1.4 collective-permute-start.1
  729.8 1.0 copy.25
  730.8 1.8 copy.26
  (80 shorter events, 13.6 us)
Async XLA Ops:
  0.6 10.4 %copy-start.7 = (bf16[2048,256]{1,0:T(8,128)(2,1)S(1)}, bf16[2048,256]{1,0:T(8,128)(2,1)}, u32[]{:S(2)}) copy-start(bf16[2048,256]{1,0:T(8,128)(2,1)} %param.22) | copy-start | bytes 3145732
  1.7 10.7 %copy-start.1 = (bf16[256,2048]{1,0:T(8,128)(2,1)S(1)}, bf16[256,2048]{1,0:T(8,128)(2,1)}, u32[]{:S(2)}) copy-start(bf16[256,2048]{1,0:T(8,128)(2,1)} %param.12) | copy-start | bytes 3145732
  11.0 1.5 copy-start.2
  13.9 10.2 %copy-start = (f32[256,2048]{1,0:T(8,128)}, f32[256,2048]{1,0:T(8,128)S(1)}, u32[]{:S(2)}) copy-start(f32[256,2048]{1,0:T(8,128)S(1)} %get-tuple-element.85.x) | copy-start | bytes 6291460
  13.9 1.4 copy-start.15
  15.4 3.4 copy-start.20
  15.4 3.5 copy-start.19
  24.1 1.5 copy-start.11
  24.1 1.5 copy-start.12
  24.1 1.5 copy-start.13
  712.4 3.9 copy-start.10
  712.5 3.9 copy-start.18
  716.3 1.2 copy-start.3
  717.6 1.6 copy-start.9
  717.6 1.8 copy-start.17
  719.2 1.3 copy-start.4
  720.4 1.7 copy-start.5
  722.0 1.2 copy-start.6
  722.1 5.2 collective-permute-start
  725.5 1.4 copy-start.8
  725.5 1.5 copy-start.16
  727.3 5.3 collective-permute-start.1
  728.7 1.0 copy-start.14

commit v4 on v3

--- a/solution.py
+++ b/solution.py
@@ -89,13 +89,12 @@
 
 
 class Links:
-    def __init__(self, tp, send_sems, recv_sems, local_sems):
+    def __init__(self, tp, send_sems, recv_sems):
         self.tp = tp
         self.di = lax.axis_index("dp")
         self.ti = lax.axis_index("tensor")
-        self.send_sems, self.recv_sems, self.local_sems = send_sems, recv_sems, local_sems
+        self.send_sems, self.recv_sems = send_sems, recv_sems
         self.used = 0
-        self.used_local = 0
 
     def partner(self, mask):
         return (flip(self.di, mask // self.tp), flip(self.ti, mask % self.tp))
@@ -120,12 +119,6 @@
 
     def send(self, src, dst, mask):
         copy = self.remote(src, dst, mask)
-        copy.start()
-        return copy
-
-    def local(self, src, dst):
-        copy = pltpu.make_async_copy(src, dst, self.local_sems.at[self.used_local])
-        self.used_local += 1
         copy.start()
         return copy
 
@@ -344,6 +337,16 @@
 
 def add_pipe(spec, rows, a, b, out):
     pipe(add_refs, (rows // spec.block_shape[0],), [spec, spec], [spec], a, b, out)
+
+
+def copy_body(a_ref, o_ref):
+    o_ref[...] = a_ref[...]
+
+
+def keep(src, dst):
+    rows, width = src.shape
+    spec = rows_spec(min(rows, 128), width)
+    pipe(copy_body, (rows // min(rows, 128),), [spec], [spec], src, dst)
 
 
 def nt_body(a_ref, b_ref, o_ref):
@@ -566,9 +569,8 @@
     far,
     send_sems,
     recv_sems,
-    local_sems,
 ):
-    links = Links(tp, send_sems, recv_sems, local_sems)
+    links = Links(tp, send_sems, recv_sems)
     shard, attn_width = wa.shape
     units = gate_w.shape[1]
     rows, model = xh.shape
@@ -605,22 +607,16 @@
     attn.start()
     across = [links.send(wa, shard_block(wa_all, 0), tp)]
     pair = [send_pair(wg, gate_w)]
-    here = [
-        links.local(gn, shard_block(gn_all, 0)),
-        links.local(wa, shard_block(wa_all, 0)),
-        links.local(cot, cot_all.at[pl.ds(0, rows)]),
-    ]
-    for w, full in ((wg, gate_w), (wu, up_w), (wd, down_w)):
-        here.append(links.local(w.at[:, mine], full.at[place]))
+    keep(gn, shard_block(gn_all, 0))
+    keep(wg.at[:, mine], gate_w.at[place])
 
     gains.forward()
     for k in range(1, outer):
         gains.arrive(k)
         across_gn.append(links.send(shard_block(gn_all, k), shard_block(gn_all, k), tp))
+    keep(wa, shard_block(wa_all, 0))
     for copy in across_gn:
         copy.wait_recv()
-    for copy in here:
-        copy.wait()
 
     def gain_rows_of(g_ref, o_ref):
         lane = lax.broadcasted_iota(jnp.int32, (8, 128), 1)
@@ -638,6 +634,9 @@
     tree = GatherTree(links, h1, rows)
     pipe(scale_tokens, (2,), [spec, gain_spec], [spec], xh, gain_rows, tree.block(0))
     tree.start()
+    keep(wu.at[:, mine], up_w.at[place])
+    keep(wd.at[:, mine], down_w.at[place])
+    keep(cot, cot_all.at[pl.ds(0, rows)])
 
     spreads = [mlp_spread(full) for full in (gate_w, up_w, down_w)]
     attn.forward()
@@ -865,9 +864,8 @@
     up_give,
     send_sems,
     recv_sems,
-    local_sems,
 ):
-    links = Links(tp, send_sems, recv_sems, local_sems)
+    links = Links(tp, send_sems, recv_sems)
     rows, model = x.shape
     tree_len = rows * tp
     units = gate_w.shape[1]
@@ -1170,7 +1168,6 @@
         scratch_shapes=[
             pltpu.SemaphoreType.DMA((count,)),
             pltpu.SemaphoreType.DMA((count,)),
-            pltpu.SemaphoreType.DMA((8,)),
         ],
         compiler_params=pltpu.CompilerParams(
             collective_id=collective, has_side_effects=True, vmem_limit_bytes=VMEM_LIMIT

time: 748 us -> 680 us (0.909)
  Pallas kernels: 686 us -> 623 us
    pallas_call x2, Pallas kernels: 686 us -> 623 us  [call(): pl.pallas_call(kernel, out_shape=[jax.ShapeDtypeStruct(shape, dtype) for...]
where the time goes in v4:
time: 680 us; the launch traced here: 670 us
  Pallas kernels  623 us (92%)
  other arithmetic  21.5 us (3%)
  matrix products  12.6 us (2%)
  local copies, waits for them, and re-layouts  11.4 us (2%)
    pallas_call x2, Pallas kernels, call(): pl.pallas_call(kernel, out_shape=[jax.ShapeDtypeStruct(shape, dtype) for...  623 us
  transfers between devices with their start and end apart: 2, of which 0 were waited for; matrix products, arithmetic and copies ran while one was open for 1% of the time, Pallas kernels for 0%

profile of v4, /device:TPU:0, one launch (start us, length us, event | category | flops | bytes accessed | tf_op | source)
XLA Modules:
  0.0 670.4 jit_solution(6223109730479460693)
XLA Ops:
  0.8 1.0 fusion.22
  1.7 1.0 fusion.21
  3.6 0.9 fusion.19
  7.3 0.9 fusion.46
  8.7 1.1 copy.23
  9.8 1.3 fusion.2
  11.0 1.4 copy.24
  14.1 1.3 copy-done.15
  15.4 3.4 select_convert_fusion.bias
  19.7 3.0 multiply_sine_fusion
  22.7 1.4 maximum_select_fusion.3.cot
  24.1 1.5 broadcast_multiply_fusion.xh
  25.7 1.0 pad_maximum_fusion.2.wa
  26.7 293.3 %layer_forward.1 = (bf16[2048,1536]{1,0:T(8,128)(2,1)}, bf16[2048,1024]{1,0:T(8,128)(2,1)}, bf16[2048,1024]{1,0:T(8,128)(2,1)}, bf16[2048,1024]{1,0:T(8,128)(2,1...) custom-call(bf16[256,1536]{1,0:T(8,128)(2,1)} %pad_maximum_fusion.2., ...), custom_call_target="tpu_custom_call" | custom-call | tf_op jit(solution)/shard_map/layer_forward/pallas_call | solution.py:1163
  320.0 329.8 %layer_backward.1 = (bf16[256,2048]{1,0:T(8,128)(2,1)}, bf16[256,2048]{1,0:T(8,128)(2,1)}, f32[256,1024]{1,0:T(8,128)}, bf16[256,1024]{1,0:T(8,128)(2,1)}, f32[2...) custom-call(bf16[2048,1536]{1,0:T(8,128)(2,1)} %get-tuple-element.37, ...), custom_call_target="tpu_custom_call" | custom-call | tf_op jit(solution)/shard_map/layer_backward/pallas_call | solution.py:1163
  649.8 2.0 multiply_reduce_fusion.3
  651.8 1.9 multiply_reduce_fusion.5
  654.9 1.6 multiply_reduce_fusion.1
  657.8 1.6 multiply_reduce_fusion
  659.6 1.0 copy-done.6
  661.5 1.4 maximum_select_fusion.7
  662.9 1.4 maximum_select_fusion.5
  666.3 1.0 copy.25
  667.2 1.8 copy.26
  (80 shorter events, 13.2 us)
Async XLA Ops:
  0.6 10.4 %copy-start.7 = (bf16[2048,256]{1,0:T(8,128)(2,1)S(1)}, bf16[2048,256]{1,0:T(8,128)(2,1)}, u32[]{:S(2)}) copy-start(bf16[2048,256]{1,0:T(8,128)(2,1)} %param.22) | copy-start | bytes 3145732
  1.7 10.7 %copy-start.1 = (bf16[256,2048]{1,0:T(8,128)(2,1)S(1)}, bf16[256,2048]{1,0:T(8,128)(2,1)}, u32[]{:S(2)}) copy-start(bf16[256,2048]{1,0:T(8,128)(2,1)} %param.12) | copy-start | bytes 3145732
  11.0 1.5 copy-start.2
  13.9 10.2 %copy-start = (f32[256,2048]{1,0:T(8,128)}, f32[256,2048]{1,0:T(8,128)S(1)}, u32[]{:S(2)}) copy-start(f32[256,2048]{1,0:T(8,128)S(1)} %get-tuple-element.85.x) | copy-start | bytes 6291460
  13.9 1.4 copy-start.15
  15.4 3.4 copy-start.20
  15.4 3.5 copy-start.19
  24.1 1.5 copy-start.11
  24.1 1.5 copy-start.12
  24.1 1.5 copy-start.13
  649.8 3.9 copy-start.10
  649.8 3.9 copy-start.18
  653.7 1.2 copy-start.3
  654.9 1.6 copy-start.9
  654.9 1.8 copy-start.17
  656.5 1.3 copy-start.4
  657.8 1.7 copy-start.5
  659.4 1.2 copy-start.6
  659.4 5.2 collective-permute-start
  662.9 1.4 copy-start.8
  662.9 1.5 copy-start.16
  664.7 4.4 collective-permute-start.1
  665.2 1.0 copy-start.14

commit v5 on v4

--- a/solution.py
+++ b/solution.py
@@ -18,7 +18,7 @@
 F32 = jnp.float32
 BF16 = jnp.bfloat16
 MESH = pl.DeviceIdType.MESH
-VMEM_LIMIT = 56 * 2**20
+VMEM_LIMIT = 60 * 2**20
 
 
 def tree_tables(parent_row, tree_len, block_len):
@@ -331,6 +331,10 @@
     return pl.BlockSpec((rows, width), lambda i: (0, 0))
 
 
+def once_spec(rows, width):
+    return pl.BlockSpec((rows, width), lambda i: (0, 0), pipeline_mode=pl.Buffered(1))
+
+
 def add_refs(a_ref, b_ref, o_ref):
     o_ref[...] = (a_ref[...].astype(F32) + b_ref[...].astype(F32)).astype(o_ref.dtype)
 
@@ -369,7 +373,7 @@
     pipe(
         tn_body,
         (count,),
-        [pl.BlockSpec((tokens, size), lambda i: (0, first + i)), whole_spec(tokens, width)],
+        [pl.BlockSpec((tokens, size), lambda i: (0, first + i)), once_spec(tokens, width)],
         [pl.BlockSpec((size, width), lambda i: (first + i, 0))],
         acts,
         grads,
@@ -535,7 +539,8 @@
 def forward_kernel(
     outer,
     tp,
-    wa,
+    wq,
+    wo,
     wg,
     wu,
     wd,
@@ -546,10 +551,10 @@
     cosine,
     sine,
     bias,
-    wa_all,
+    wq_all,
+    wo_all,
     gate_w,
     up_w,
-    down_w,
     gain_rows,
     h1,
     qkv,
@@ -558,25 +563,28 @@
     x1,
     h2,
     cot_all,
+    dgate,
+    dupper,
+    hid,
+    down_w,
+    grad_down,
     gate,
     upper,
-    hid,
-    grad_down,
     gn_all,
     part,
     got_c,
     got_y,
     far,
+    dhid,
     send_sems,
     recv_sems,
 ):
     links = Links(tp, send_sems, recv_sems)
-    shard, attn_width = wa.shape
+    shard, qkv_width = wq.shape
     units = gate_w.shape[1]
     rows, model = xh.shape
     tree_len = rows * tp
     q_width = att.shape[1]
-    qkv_width = qkv.shape[1]
     kv_width = (qkv_width - q_width) // 2
     head = HEAD_SIZE
     xi = links.di % 2
@@ -601,12 +609,19 @@
         )
 
     gains = Spread(links, outer, gn, lambda k: shard_block(gn_all, k))
-    attn = Spread(links, outer, wa, lambda k: shard_block(wa_all, k))
+    attn = Spread(links, outer, wq, lambda k: shard_block(wq_all, k))
+    attn_out = Spread(links, outer, wo, lambda k: shard_block(wo_all, k))
     gains.start()
     across_gn = [links.send(gn, shard_block(gn_all, 0), tp)]
     attn.start()
-    across = [links.send(wa, shard_block(wa_all, 0), tp)]
+    across = [links.send(wq, shard_block(wq_all, 0), tp)]
+    attn_out.start()
     pair = [send_pair(wg, gate_w)]
+    across_out = [links.send(wo, shard_block(wo_all, 0), tp)]
+
+    def cross(full, k, copies):
+        copies.append(links.send(shard_block(full, k), shard_block(full, k), tp))
+
     keep(gn, shard_block(gn_all, 0))
     keep(wg.at[:, mine], gate_w.at[place])
 
@@ -614,7 +629,8 @@
     for k in range(1, outer):
         gains.arrive(k)
         across_gn.append(links.send(shard_block(gn_all, k), shard_block(gn_all, k), tp))
-    keep(wa, shard_block(wa_all, 0))
+    keep(wq, shard_block(wq_all, 0))
+    keep(wo, shard_block(wo_all, 0))
     for copy in across_gn:
         copy.wait_recv()
 
@@ -640,20 +656,25 @@
 
     spreads = [mlp_spread(full) for full in (gate_w, up_w, down_w)]
     attn.forward()
-    across.append(links.send(shard_block(wa_all, 2), shard_block(wa_all, 2), tp))
-    pair[0].wait_recv()
-    spreads[0].start()
-    tree.across()
+    cross(wq_all, 2, across)
     for k in range(1, outer):
         if k != 2:
             attn.arrive(k)
-            across.append(links.send(shard_block(wa_all, k), shard_block(wa_all, k), tp))
-        if k == 1:
-            pair.append(send_pair(wu, up_w))
+            cross(wq_all, k, across)
+    tree.across()
+    attn_out.forward()
+    cross(wo_all, 2, across_out)
+    pair[0].wait_recv()
+    spreads[0].start()
+    for k in range(1, outer):
+        if k != 2:
+            attn_out.arrive(k)
+            cross(wo_all, k, across_out)
+    pair.append(send_pair(wu, up_w))
+    later = gather_units(links, cot_all, rows)
+    next(later)
     pair.append(send_pair(wd, down_w))
     tree.arrive()
-    pair[1].wait_recv()
-    spreads[1].start()
     for copy in across:
         copy.wait_recv()
 
@@ -675,14 +696,11 @@
         ],
         [rows_spec(rows, qkv_width)],
         h1,
-        wa_all.at[:, pl.ds(0, qkv_width)],
+        wq_all,
         cosine,
         sine,
         qkv,
     )
-    spreads[0].forward()
-    pair[2].wait_recv()
-    spreads[2].start()
 
     group = q_width // kv_width
 
@@ -714,18 +732,24 @@
         probs,
         att,
     )
+    for copy in across_out:
+        copy.wait_recv()
     pipe(
         nt_body,
         (tp,),
         [rows_spec(rows, q_width), whole_spec(model, q_width)],
         [rows_spec(rows, model)],
         att,
-        wa_all.at[:, pl.ds(qkv_width, q_width)],
+        wo_all,
         part,
     )
     mixed = ScatterTensor(links, part, got_c, got_y, far, rows)
     mixed.start()
+    spreads[0].forward()
+    pair[1].wait_recv()
+    spreads[1].start()
     mixed.across()
+    next(later)
     parts = mixed.arrive()
 
     def residual(x_ref, a_ref, b_ref, c_ref, g_ref, x1_ref, h_ref):
@@ -746,24 +770,31 @@
     )
     stages = gather_units(links, h2, rows)
     next(stages)
-    later = gather_units(links, cot_all, rows)
     next(later)
     next(stages)
     spreads[1].forward()
+    pair[2].wait_recv()
+    spreads[2].start()
     next(stages)
-    next(later)
     next(stages)
+    run(later)
 
     for spread in spreads[:2]:
         for k in range(1, outer):
             spread.arrive(k)
 
-    def expand(x_ref, g_ref, u_ref, go_ref, uo_ref, h_ref):
+    def expand(x_ref, g_ref, u_ref, a_ref, b_ref, h_ref):
+        @pl.when(pl.program_id(0) == tp)
+        def _():
+            spreads[2].forward()
+
         g = dot_nn(x_ref[...], g_ref[...])
         u = dot_nn(x_ref[...], u_ref[...])
-        go_ref[...] = g.astype(BF16)
-        uo_ref[...] = u.astype(BF16)
-        h_ref[...] = (g * jax.nn.sigmoid(g) * u).astype(BF16)
+        sigma = jax.nn.sigmoid(g)
+        swish = g * sigma
+        a_ref[...] = (u * sigma * (1.0 + g * (1.0 - sigma))).astype(BF16)
+        b_ref[...] = swish.astype(BF16)
+        h_ref[...] = (swish * u).astype(BF16)
 
     pipe(
         expand,
@@ -777,14 +808,47 @@
         upper,
         hid,
     )
-    run(later)
-    spreads[2].forward()
     weight_grad(cot_all, hid, grad_down, 4)
-    for k in range(1, outer):
+
+    known = (outer - 1) * 2 * shard
+    unit_spec = rows_spec(rows, units)
+
+    def contract_known(c_ref, d_ref):
+        at = pl.ds(pl.multiple_of(pl.program_id(0) * rows, rows), rows)
+        dhid[at] = dot_nn(c_ref[...], d_ref[...])
+
+    def contract_last(c_ref, d_ref, a_ref, b_ref, dg_ref, du_ref):
+        at = pl.ds(pl.multiple_of(pl.program_id(0) * rows, rows), rows)
+        value = dhid[at] + dot_nn(c_ref[...], d_ref[...])
+        dg_ref[...] = (value * a_ref[...].astype(F32)).astype(BF16)
+        du_ref[...] = (value * b_ref[...].astype(F32)).astype(BF16)
+
+    for k in range(1, outer - 1):
         spreads[2].arrive(k)
-    for spread in [gains, attn] + spreads:
+    pipe(
+        contract_known,
+        (2 * tp,),
+        [rows_spec(rows, known), once_spec(known, units)],
+        [],
+        cot_all.at[:, pl.ds(0, known)],
+        down_w.at[pl.ds(0, known)],
+    )
+    spreads[2].arrive(outer - 1)
+    pipe(
+        contract_last,
+        (2 * tp,),
+        [rows_spec(rows, model - known), once_spec(model - known, units), unit_spec, unit_spec],
+        [unit_spec] * 2,
+        cot_all.at[:, pl.ds(known, model - known)],
+        down_w.at[pl.ds(known, model - known)],
+        gate,
+        upper,
+        dgate,
+        dupper,
+    )
+    for spread in [gains, attn, attn_out] + spreads:
         spread.sent()
-    for copy in across_gn + across + pair:
+    for copy in across_gn + across + across_out + pair:
         copy.wait_send()
     tree.sent()
     mixed.sent()
@@ -793,10 +857,10 @@
 def backward_kernel(
     outer,
     tp,
-    wa_all,
+    wq_all,
+    wo_all,
     gate_w,
     up_w,
-    down_w,
     gain_rows,
     h1,
     qkv,
@@ -804,10 +868,11 @@
     att,
     x1,
     h2,
-    cot_all,
-    gate,
-    upper,
+    cot,
+    dgate,
+    dupper,
     hid,
+    down_w,
     grad_down,
     x,
     cosine,
@@ -822,33 +887,12 @@
     up_theirs,
     out_total,
     qkv_total,
-    dgate,
-    dupper,
-    e_part,
-    y_part,
-    e_got_c,
-    y_got_c,
-    e_near,
-    y_near,
-    e_got,
-    y_got,
     dx1,
-    dx1_low,
-    dout,
     dscores,
-    dqkv,
-    f_part,
-    f_got_c,
-    f_got_y,
-    f_far,
     grad_gate,
     grad_up,
     grad_out,
     grad_qkv,
-    out_pair,
-    qkv_pair,
-    out_sum,
-    qkv_sum,
     down_held,
     gate_held,
     up_held,
@@ -862,6 +906,24 @@
     down_give,
     gate_give,
     up_give,
+    y_part,
+    e_part,
+    e_got_c,
+    y_got_c,
+    e_near,
+    y_near,
+    e_got,
+    y_got,
+    dx1_low,
+    dout,
+    dqkv,
+    f_got_c,
+    f_got_y,
+    f_far,
+    out_pair,
+    qkv_pair,
+    out_sum,
+    qkv_sum,
     send_sems,
     recv_sems,
 ):
@@ -899,28 +961,7 @@
     red_up = mlp_reduce(grad_up, up_held, up_staged)
     red_down.start_all()
 
-    def contract(c_ref, w_ref, g_ref, u_ref, dg_ref, du_ref):
-        dhid = dot_nn(c_ref[...], w_ref[...])
-        g = g_ref[...].astype(F32)
-        sigma = jax.nn.sigmoid(g)
-        dg_ref[...] = (dhid * u_ref[...].astype(F32) * sigma * (1.0 + g * (1.0 - sigma))).astype(
-            BF16
-        )
-        du_ref[...] = (dhid * g * sigma).astype(BF16)
-
-    unit_spec = rows_spec(rows, units)
-    pipe(
-        contract,
-        (2 * tp,),
-        [rows_spec(rows, model), whole_spec(model, units), unit_spec, unit_spec],
-        [unit_spec] * 2,
-        cot_all,
-        down_w,
-        gate,
-        upper,
-        dgate,
-        dupper,
-    )
+    y_sum = ScatterUnits(links, y_part, y_got_c, y_near, y_got, rows)
 
     def every_other(first, block_rows, width):
         return pl.BlockSpec((block_rows, width), lambda i: (2 * i + first, 0))
@@ -934,7 +975,7 @@
         pipe(
             back,
             (tp,),
-            [every_other(first, rows, units)] * 2 + [whole_spec(model, units)] * 2,
+            [every_other(first, rows, units)] * 2 + [once_spec(model, units)] * 2,
             [every_other(first, rows, model)],
             dgate,
             dupper,
@@ -943,19 +984,7 @@
             e_part,
         )
 
-    def down_blocks(first):
-        pipe(
-            nt_body,
-            (tp,),
-            [every_other(first, rows, units), whole_spec(model, units)],
-            [every_other(first, rows, model)],
-            hid,
-            down_w,
-            y_part,
-        )
-
     e_sum = ScatterUnits(links, e_part, e_got_c, e_near, e_got, rows)
-    y_sum = ScatterUnits(links, y_part, y_got_c, y_near, y_got, rows)
     back_blocks(1)
     e_sum.start()
     red_down.pump()
@@ -966,9 +995,6 @@
     e_sum.finish()
     weight_grad(h2, dupper, grad_up, 4)
     red_up.start_all()
-    down_blocks(1)
-    y_sum.start()
-    down_blocks(0)
     trades = [trade(red_down, down_mine, down_give, down_theirs)]
 
     tree = GatherTree(links, dx1_low, rows)
@@ -984,7 +1010,7 @@
         (2,),
         [spec, spec, gain_spec] + [spec] * len(parts),
         [spec] * 2,
-        cot_all.at[pl.ds(0, rows)],
+        cot,
         x1,
         gain_rows,
         *parts,
@@ -992,9 +1018,18 @@
         tree.block(0),
     )
     tree.start()
-    y_sum.across()
     red_gate.pump()
+    pipe(
+        nt_body,
+        (2 * tp,),
+        [rows_spec(rows, units), once_spec(model, units)],
+        [rows_spec(rows, model)],
+        hid,
+        down_w,
+        y_part,
+    )
     tree.across()
+    y_sum.start()
     tree.arrive()
 
     pipe(
@@ -1003,7 +1038,7 @@
         [rows_spec(rows, model), whole_spec(model, q_width)],
         [rows_spec(rows, q_width)],
         dx1_low,
-        wa_all.at[:, pl.ds(qkv_width, q_width)],
+        wo_all,
         dout,
     )
 
@@ -1018,7 +1053,7 @@
     weight_grad(dx1_low, att, grad_out, 4)
     order = list(range(outer - 1, -1, -1))
     out_across = {k: pair_send(grad_out, out_pair, k) for k in order}
-    y_sum.finish()
+    y_sum.across()
 
     def score_grads(do_ref, k_ref, v_ref, p_ref, cos_ref, sin_ref, ds_ref, dq_ref):
         p = p_ref[0].astype(F32)
@@ -1081,6 +1116,8 @@
         dqkv.at[:, pl.ds(q_width, 2 * kv_width)],
     )
 
+    y_sum.finish()
+
     def pair_add(grad, held, total, k):
         add_pipe(
             rows_spec(min(shard, 128), grad.shape[1]),
@@ -1091,16 +1128,18 @@
         )
 
     qkv_across = {}
+    weight_grad(h1, dqkv, grad_qkv, 4)
     for k in order:
-        weight_grad(h1, dqkv, grad_qkv, outer, k, 1)
         qkv_across[k] = pair_send(grad_qkv, qkv_pair, k)
+    e_sum.sent()
+    f_part = e_part.at[pl.ds(0, tree_len)]
     pipe(
         nt_body,
         (tp,),
         [rows_spec(rows, qkv_width), whole_spec(model, qkv_width)],
         [rows_spec(rows, model)],
         dqkv,
-        wa_all.at[:, pl.ds(0, qkv_width)],
+        wq_all,
         f_part,
     )
     f_sum = ScatterTensor(links, f_part, f_got_c, f_got_y, f_far, rows)
@@ -1154,18 +1193,19 @@
         copy.wait()
     for copy in list(out_across.values()) + list(qkv_across.values()):
         copy.wait_send()
-    for item in (red_down, red_gate, red_up, red_out, red_qkv, e_sum, y_sum, f_sum, tree):
+    for item in (red_down, red_gate, red_up, red_out, red_qkv, y_sum, f_sum, tree):
         item.sent()
 
 
-def call(kernel, name, collective, count, shapes, operands):
+def call(kernel, name, collective, count, shapes, scratch, operands):
     anywhere = pl.BlockSpec(memory_space=pl.ANY)
     return pl.pallas_call(
         kernel,
         out_shape=[jax.ShapeDtypeStruct(shape, dtype) for shape, dtype in shapes],
         in_specs=[anywhere] * len(operands),
         out_specs=[anywhere] * len(shapes),
-        scratch_shapes=[
+        scratch_shapes=[pltpu.VMEM(shape, dtype) for shape, dtype in scratch]
+        + [
             pltpu.SemaphoreType.DMA((count,)),
             pltpu.SemaphoreType.DMA((count,)),
         ],
@@ -1220,7 +1260,7 @@
         shard = w_query.shape[0]
         units = w_gate.shape[1] // 2
 
-        wa = jnp.concatenate([w_query, key_matrix, value_matrix, w_out.T], 1)
+        wq = jnp.concatenate([w_query, key_matrix, value_matrix], 1)
         gn = jnp.concatenate(
             [
                 jnp.broadcast_to(attn_gain[:, None], (shard, 64)),
@@ -1235,10 +1275,10 @@
         xh = normalize(x)[0]
         cot = relative(cotangent, zi)
         (
-            wa_all,
+            wq_all,
+            wo_all,
             gate_w,
             up_w,
-            down_w,
             gain_rows,
             h1,
             qkv,
@@ -1247,18 +1287,19 @@
             x1,
             h2,
             cot_all,
-            gate,
-            upper,
+            dgate,
+            dupper,
             hid,
+            down_w,
             grad_down,
         ) = call(
             functools.partial(forward_kernel, outer, tp),
             "layer_forward",
             0,
-            50 + 7 * outer,
+            60 + 9 * outer,
             [
-                ((model, qkv_width + q_width), BF16),
-                ((model, units), BF16),
+                ((model, qkv_width), BF16),
+                ((model, q_width), BF16),
                 ((model, units), BF16),
                 ((model, units), BF16),
                 ((8, model), F32),
@@ -1273,16 +1314,21 @@
                 ((2 * tree_len, units), BF16),
                 ((2 * tree_len, units), BF16),
                 ((model, units), BF16),
+                ((model, units), BF16),
+                ((2 * tree_len, units), BF16),
+                ((2 * tree_len, units), BF16),
                 ((model, 128), BF16),
+            ],
+            [
                 ((tree_len, model), BF16),
                 ((2, rows, model), BF16),
                 ((rows, model), BF16),
                 ((rows, model), BF16),
+                ((2 * tree_len, units), F32),
             ],
-            (wa, w_gate, w_up, w_down.T, gn, x, xh, cot, cosine, sine, bias),
-        )[:16]
-
-        mlp_held = [((outer, 2 * shard, units), BF16)]
+            (wq, w_out.T, w_gate, w_up, w_down.T, gn, x, xh, cot, cosine, sine, bias),
+        )[:17]
+
         (
             out,
             grad_tok,
@@ -1302,28 +1348,27 @@
             [((rows, model), BF16)] * 2
             + [((shard, units), F32), ((shard, units), BF16)] * 3
             + [((shard, q_width), F32), ((shard, qkv_width), F32)]
-            + [((2 * tree_len, units), BF16)] * 2
-            + [((2 * tree_len, model), BF16)] * 2
-            + [((4, rows, model), BF16)] * 2
-            + [((3, rows, model), BF16)] * 4
-            + [((rows, model), F32), ((tree_len, model), BF16)]
-            + [((tree_len, q_width), BF16), ((heads, tree_len, tree_len), BF16)]
-            + [((tree_len, qkv_width), BF16), ((tree_len, model), BF16)]
-            + [((2, rows, model), BF16)]
-            + [((rows, model), BF16)] * 2
+            + [((rows, model), F32), ((heads, tree_len, tree_len), BF16)]
             + [((model, units), BF16)] * 2
             + [((model, q_width), BF16), ((model, qkv_width), BF16)]
-            + [((outer, shard, q_width), BF16), ((outer, shard, qkv_width), BF16)] * 2
-            + mlp_held * 3
+            + [((outer, 2 * shard, units), BF16)] * 3
             + [((outer, shard, q_width), BF16), ((outer, shard, qkv_width), BF16)]
             + [((2 * shard, units), BF16)] * 3
             + [((shard, q_width), BF16), ((shard, qkv_width), BF16)]
-            + [((shard, units), BF16)] * 3,
+            + [((shard, units), BF16)] * 3
+            + [((2 * tree_len, model), BF16)],
+            [((2 * tree_len, model), BF16)]
+            + [((4, rows, model), BF16)] * 2
+            + [((3, rows, model), BF16)] * 4
+            + [((tree_len, model), BF16), ((tree_len, q_width), BF16)]
+            + [((tree_len, qkv_width), BF16), ((2, rows, model), BF16)]
+            + [((rows, model), BF16)] * 2
+            + [((outer, shard, q_width), BF16), ((outer, shard, qkv_width), BF16)] * 2,
             (
-                wa_all,
+                wq_all,
+                wo_all,
                 gate_w,
                 up_w,
-                down_w,
                 gain_rows,
                 h1,
                 qkv,
@@ -1331,10 +1376,11 @@
                 att,
                 x1,
                 h2,
-                cot_all,
-                gate,
-                upper,
+                cot,
+                dgate,
+                dupper,
                 hid,
+                down_w,
                 grad_down,
                 x,
                 cosine,

time: 680 us -> 630 us (0.926)
  Pallas kernels: 623 us -> 569 us
    pallas_call x2, Pallas kernels: 623 us -> 569 us  [call(): pl.pallas_call(kernel, out_shape=[jax.ShapeDtypeStruct(shape, dtype) for...]
where the time goes in v5:
time: 630 us; the launch traced here: 617 us
  Pallas kernels  569 us (90%)
  other arithmetic  21.4 us (3%)
  matrix products  12.5 us (2%)
  local copies, waits for them, and re-layouts  11.6 us (2%)
    pallas_call x2, Pallas kernels, call(): pl.pallas_call(kernel, out_shape=[jax.ShapeDtypeStruct(shape, dtype) for...  569 us
  transfers between devices with their start and end apart: 2, of which 0 were waited for; matrix products, arithmetic and copies ran while one was open for 1% of the time, Pallas kernels for 0%

profile of v5, /device:TPU:0, one launch (start us, length us, event | category | flops | bytes accessed | tf_op | source)
XLA Modules:
  0.0 617.3 jit_solution(9791556085287936619)
XLA Ops:
  0.8 1.0 fusion.22
  1.7 1.0 fusion.21
  2.7 0.9 fusion.20
  4.6 0.9 fusion.18
  6.4 0.9 fusion.16
  7.3 0.9 fusion.46
  8.7 1.8 copy.23
  10.5 1.3 fusion.2
  11.7 1.4 copy.24
  14.8 1.3 copy-done.13
  16.1 3.4 select_convert_fusion.bias
  20.4 3.0 multiply_sine_fusion
  23.4 1.4 maximum_select_fusion.3.cot
  24.8 1.5 broadcast_multiply_fusion.xh
  27.2 302.4 %layer_forward.1 = (bf16[2048,1024]{1,0:T(8,128)(2,1)}, bf16[2048,512]{1,0:T(8,128)(2,1)}, bf16[2048,1024]{1,0:T(8,128)(2,1)}, bf16[2048,1024]{1,0:T(8,128)(2,1)...) custom-call(bf16[256,1024]{1,0:T(8,128)(2,1)} %pad_maximum_fusion.2., ...), custom_call_target="tpu_custom_call" | custom-call | tf_op jit(solution)/shard_map/layer_forward/pallas_call | solution.py:1202
  329.6 267.0 %layer_backward.1 = (bf16[256,2048]{1,0:T(8,128)(2,1)}, bf16[256,2048]{1,0:T(8,128)(2,1)}, f32[256,1024]{1,0:T(8,128)}, bf16[256,1024]{1,0:T(8,128)(2,1)}, f32[2...) custom-call(bf16[2048,1024]{1,0:T(8,128)(2,1)} %get-tuple-element.37, ...), custom_call_target="tpu_custom_call" | custom-call | tf_op jit(solution)/shard_map/layer_backward/pallas_call | solution.py:1202
  596.6 2.0 multiply_reduce_fusion.3
  598.6 1.9 multiply_reduce_fusion.5
  601.7 1.6 multiply_reduce_fusion.1
  604.6 1.6 multiply_reduce_fusion
  608.3 1.4 maximum_select_fusion.7
  609.7 1.4 maximum_select_fusion.5
  612.9 1.0 copy.25
  613.9 1.8 copy.26
  (80 shorter events, 13.2 us)
Async XLA Ops:
  0.6 11.1 %copy-start.7 = (bf16[2048,256]{1,0:T(8,128)(2,1)S(1)}, bf16[2048,256]{1,0:T(8,128)(2,1)}, u32[]{:S(2)}) copy-start(bf16[2048,256]{1,0:T(8,128)(2,1)} %param.22) | copy-start | bytes 3145732
  1.7 11.4 %copy-start.1 = (bf16[256,2048]{1,0:T(8,128)(2,1)S(1)}, bf16[256,2048]{1,0:T(8,128)(2,1)}, u32[]{:S(2)}) copy-start(bf16[256,2048]{1,0:T(8,128)(2,1)} %param.12) | copy-start | bytes 3145732
  11.7 1.5 copy-start.2
  14.6 10.2 %copy-start = (f32[256,2048]{1,0:T(8,128)}, f32[256,2048]{1,0:T(8,128)S(1)}, u32[]{:S(2)}) copy-start(f32[256,2048]{1,0:T(8,128)S(1)} %get-tuple-element.85.x) | copy-start | bytes 6291460
  14.6 1.4 copy-start.13
  16.1 3.4 copy-start.20
  16.1 3.5 copy-start.19
  24.8 1.5 copy-start.11
  24.8 1.5 copy-start.17
  24.8 1.5 copy-start.18
  596.6 3.9 copy-start.10
  596.6 3.9 copy-start.16
  600.5 1.2 copy-start.3
  601.7 1.6 copy-start.9
  601.7 1.8 copy-start.15
  603.3 1.3 copy-start.4
  604.6 2.2 copy-start.5
  606.2 1.2 copy-start.6
  606.2 5.2 collective-permute-start
  609.7 1.4 copy-start.8
  609.7 1.5 copy-start.14
  611.5 4.3 collective-permute-start.1
  611.9 1.0 copy-start.12

commit v6 on v5

--- a/solution.py
+++ b/solution.py
@@ -24,19 +24,16 @@
 def tree_tables(parent_row, tree_len, block_len):
     blocks = parent_row.shape[0]
     nodes = jnp.arange(blocks, dtype=jnp.int32)
-    hops = (parent_row[:, None] == nodes[None, :]).astype(F32)
-    reach = jnp.eye(blocks, dtype=F32)
-    walk = reach
-    for hop_count in range(blocks):
-        walk = jnp.dot(walk, hops, precision=HIGH)
-        reach = jnp.maximum(reach, walk)
+    walks = jnp.eye(blocks, dtype=F32) + (parent_row[:, None] == nodes[None, :]).astype(F32)
+    hops = 1
+    while hops < blocks - 1:
+        walks = jnp.dot(walks, walks, precision=HIGH)
+        hops *= 2
+    reach = (walks > 0.5).astype(F32)
     depth = jnp.sum(reach, axis=1) - 1.0
-    rows = jnp.arange(tree_len, dtype=jnp.int32)
-    member = (rows[:, None] // block_len == nodes[None, :]).astype(F32)
-    visible = jnp.dot(jnp.dot(member, reach, precision=HIGH), member.T, precision=HIGH) > 0.5
-    allowed_mask = visible & (rows[None, :] <= rows[:, None])
-    place = jnp.dot(member, depth, precision=HIGH) * block_len + (rows % block_len).astype(F32)
-    return (allowed_mask, place)
+    row_reach = jnp.repeat(jnp.pad(reach, ((0, 0), (0, 128 - blocks))), block_len, axis=0)
+    place = depth[:, None] * block_len + jnp.arange(block_len, dtype=F32)[None, :]
+    return (row_reach.astype(BF16), place.reshape(tree_len))
 
 
 def rope_tables(place, head_dim):
@@ -137,17 +134,30 @@
         if outer == 4:
             self.onward = links.remote(block(2), block(3), step)
 
-    def start(self):
+    def start(self, near=True):
         if self.outer != 4:
             for copy in self.copies.values():
                 copy.start()
             return
         self.copies[2].start()
-        self.copies[1].start()
+        if near:
+            self.copies[1].start()
+        else:
+
+            @pl.when(jnp.logical_not(self.middle))
+            def _():
+                self.copies[1].start()
 
         @pl.when(self.middle)
         def _():
             self.copies[3].start()
+
+    def start_near(self):
+        if self.outer == 4:
+
+            @pl.when(self.middle)
+            def _():
+                self.copies[1].start()
 
     def forward(self):
         self.copies[2].wait_recv()
@@ -550,7 +560,7 @@
     cot,
     cosine,
     sine,
-    bias,
+    row_reach,
     wq_all,
     wo_all,
     gate_w,
@@ -568,14 +578,14 @@
     hid,
     down_w,
     grad_down,
-    gate,
-    upper,
     gn_all,
     part,
     got_c,
     got_y,
     far,
     dhid,
+    gate,
+    upper,
     send_sems,
     recv_sems,
 ):
@@ -701,11 +711,20 @@
         sine,
         qkv,
     )
+    pair[1].wait_recv()
+    spreads[1].start(near=False)
 
     group = q_width // kv_width
 
-    def attend(q_ref, k_ref, v_ref, b_ref, p_ref, o_ref):
-        scores = dot_nt(q_ref[...], k_ref[...]) * (head**-0.5) + b_ref[...].astype(F32)
+    def attend(q_ref, k_ref, v_ref, r_ref, p_ref, o_ref):
+        segment = lax.broadcasted_iota(jnp.int32, (128, tree_len), 0)
+        key_row = lax.broadcasted_iota(jnp.int32, (128, tree_len), 1)
+        member = jnp.where(key_row // BLK == segment, 1.0, 0.0).astype(BF16)
+        seen = dot_nn(r_ref[...], member)
+        query = lax.broadcasted_iota(jnp.int32, (rows, tree_len), 0) + pl.program_id(0) * rows
+        key = lax.broadcasted_iota(jnp.int32, (rows, tree_len), 1)
+        scores = dot_nt(q_ref[...], k_ref[...]) * (head**-0.5)
+        scores = jnp.where((seen > 0.5) & (key <= query), scores, NEG)
         weights = jnp.exp(scores - jnp.max(scores, axis=-1, keepdims=True))
         weights = (weights / jnp.sum(weights, axis=-1, keepdims=True)).astype(BF16)
         p_ref[0] = weights
@@ -719,7 +738,7 @@
             pl.BlockSpec((rows, head), lambda i, h: (i, h)),
             pl.BlockSpec((tree_len, head), lambda i, h: (0, k_at + h // group)),
             pl.BlockSpec((tree_len, head), lambda i, h: (0, v_at + h // group)),
-            pl.BlockSpec((rows, tree_len), lambda i, h: (i, 0)),
+            pl.BlockSpec((rows, 128), lambda i, h: (i, 0)),
         ],
         [
             pl.BlockSpec((1, rows, tree_len), lambda i, h: (h, i, 0)),
@@ -728,7 +747,7 @@
         qkv,
         qkv,
         qkv,
-        bias,
+        row_reach,
         probs,
         att,
     )
@@ -746,10 +765,11 @@
     mixed = ScatterTensor(links, part, got_c, got_y, far, rows)
     mixed.start()
     spreads[0].forward()
-    pair[1].wait_recv()
-    spreads[1].start()
+    spreads[1].start_near()
     mixed.across()
     next(later)
+    pair[2].wait_recv()
+    spreads[2].start(near=False)
     parts = mixed.arrive()
 
     def residual(x_ref, a_ref, b_ref, c_ref, g_ref, x1_ref, h_ref):
@@ -773,8 +793,7 @@
     next(later)
     next(stages)
     spreads[1].forward()
-    pair[2].wait_recv()
-    spreads[2].start()
+    spreads[2].start_near()
     next(stages)
     next(stages)
     run(later)
@@ -799,7 +818,7 @@
     pipe(
         expand,
         (2 * tp,),
-        [rows_spec(rows, model), whole_spec(model, units), whole_spec(model, units)],
+        [rows_spec(rows, model), once_spec(model, units), once_spec(model, units)],
         [rows_spec(rows, units)] * 3,
         h2,
         gate_w,
@@ -1268,9 +1287,8 @@
             ],
             1,
         )
-        allowed_mask, place = tree_tables(parents[0], tree_len, BLK)
+        row_reach, place = tree_tables(parents[0], tree_len, BLK)
         cosine, sine = rope_tables(place, HEAD_SIZE)
-        bias = jnp.where(allowed_mask, 0.0, NEG).astype(BF16)
         x = relative(tokens, zi).astype(F32)
         xh = normalize(x)[0]
         cot = relative(cotangent, zi)
@@ -1315,8 +1333,6 @@
                 ((2 * tree_len, units), BF16),
                 ((model, units), BF16),
                 ((model, units), BF16),
-                ((2 * tree_len, units), BF16),
-                ((2 * tree_len, units), BF16),
                 ((model, 128), BF16),
             ],
             [
@@ -1325,8 +1341,10 @@
                 ((rows, model), BF16),
                 ((rows, model), BF16),
                 ((2 * tree_len, units), F32),
+                ((2 * tree_len, units), BF16),
+                ((2 * tree_len, units), BF16),
             ],
-            (wq, w_out.T, w_gate, w_up, w_down.T, gn, x, xh, cot, cosine, sine, bias),
+            (wq, w_out.T, w_gate, w_up, w_down.T, gn, x, xh, cot, cosine, sine, row_reach),
         )[:17]
 
         (

time: 630 us -> 624 us (level)
  matrix products: 12.5 us -> 1.32 us
    dot_general x11 -> x3, matrix products: 12.5 us -> 1.32 us  [tree_tables(): walks = jnp.dot(walks, walks, precision=HIGH)]
where the time goes in v6:
time: 624 us; the launch traced here: 612 us
  Pallas kernels  574 us (92%)
  other arithmetic  21.5 us (3%)
  local copies, waits for them, and re-layouts  12.9 us (2%)
    pallas_call x2, Pallas kernels, call(): pl.pallas_call(kernel, out_shape=[jax.ShapeDtypeStruct(shape, dtype) for...  574 us
  transfers between devices with their start and end apart: 2, of which 0 were waited for; matrix products, arithmetic and copies ran while one was open for 1% of the time, Pallas kernels for 0%

profile of v6, /device:TPU:0, one launch (start us, length us, event | category | flops | bytes accessed | tf_op | source)
XLA Modules:
  0.0 612.2 jit_solution(9694390359675209904)
XLA Ops:
  0.7 0.9 fusion.2
  2.2 1.8 copy.23
  4.0 2.4 copy.24
  6.5 0.7 maximum_select_fusion
  8.7 0.7 pad_maximum_fusion.3.gn
  9.4 3.0 multiply_sine_fusion
  12.5 1.4 maximum_select_fusion.3.cot
  13.9 1.5 broadcast_multiply_fusion.xh
  15.4 0.9 pad_maximum_fusion.2.wq
  16.3 0.7 broadcast_in_dim.8
  17.0 306.6 %layer_forward.1 = (bf16[2048,1024]{1,0:T(8,128)(2,1)}, bf16[2048,512]{1,0:T(8,128)(2,1)}, bf16[2048,1024]{1,0:T(8,128)(2,1)}, bf16[2048,1024]{1,0:T(8,128)(2,1)...) custom-call(bf16[256,1024]{1,0:T(8,128)(2,1)} %pad_maximum_fusion.2., ...), custom_call_target="tpu_custom_call" | custom-call | tf_op jit(solution)/shard_map/layer_forward/pallas_call | solution.py:1221
  323.7 267.6 %layer_backward.1 = (bf16[256,2048]{1,0:T(8,128)(2,1)}, bf16[256,2048]{1,0:T(8,128)(2,1)}, f32[256,1024]{1,0:T(8,128)}, bf16[256,1024]{1,0:T(8,128)(2,1)}, f32[2...) custom-call(bf16[2048,1024]{1,0:T(8,128)(2,1)} %get-tuple-element.37, ...), custom_call_target="tpu_custom_call" | custom-call | tf_op jit(solution)/shard_map/layer_backward/pallas_call | solution.py:1221
  591.3 2.0 multiply_reduce_fusion.3
  593.3 1.9 multiply_reduce_fusion.5
  595.5 0.9 copy-done.3
  596.4 1.6 multiply_reduce_fusion.1
  598.5 0.8 copy-done.4
  599.3 1.6 multiply_reduce_fusion
  601.2 0.9 copy-done.6
  603.0 1.4 maximum_select_fusion.7
  604.4 1.4 maximum_select_fusion.5
  606.9 0.9 copy-done.11
  607.8 1.0 copy.25
  608.8 1.8 copy.26
  (70 shorter events, 6.3 us)
Async XLA Ops:
  0.6 5.7 copy-start.1
  4.0 2.4 copy-start.2
  7.8 6.1 copy-start
  7.8 0.7 copy-start.18
  7.8 0.8 copy-start.17
  13.9 1.5 copy-start.10
  13.9 1.5 copy-start.15
  13.9 1.5 copy-start.16
  591.3 3.9 copy-start.9
  591.3 3.9 copy-start.14
  595.2 1.2 copy-start.3
  596.4 1.6 copy-start.8
  596.4 1.8 copy-start.13
  598.0 1.3 copy-start.4
  599.3 1.8 copy-start.5
  600.9 1.2 copy-start.6
  600.9 5.2 collective-permute-start
  604.4 1.4 copy-start.7
  604.4 1.5 copy-start.12
  606.1 4.4 collective-permute-start.1
  606.7 1.0 copy-start.11

commit v7 on v6

--- a/solution.py
+++ b/solution.py
@@ -134,30 +134,17 @@
         if outer == 4:
             self.onward = links.remote(block(2), block(3), step)
 
-    def start(self, near=True):
+    def start(self):
         if self.outer != 4:
             for copy in self.copies.values():
                 copy.start()
             return
         self.copies[2].start()
-        if near:
-            self.copies[1].start()
-        else:
-
-            @pl.when(jnp.logical_not(self.middle))
-            def _():
-                self.copies[1].start()
+        self.copies[1].start()
 
         @pl.when(self.middle)
         def _():
             self.copies[3].start()
-
-    def start_near(self):
-        if self.outer == 4:
-
-            @pl.when(self.middle)
-            def _():
-                self.copies[1].start()
 
     def forward(self):
         self.copies[2].wait_recv()
@@ -711,8 +698,6 @@
         sine,
         qkv,
     )
-    pair[1].wait_recv()
-    spreads[1].start(near=False)
 
     group = q_width // kv_width
 
@@ -765,11 +750,10 @@
     mixed = ScatterTensor(links, part, got_c, got_y, far, rows)
     mixed.start()
     spreads[0].forward()
-    spreads[1].start_near()
+    pair[1].wait_recv()
+    spreads[1].start()
     mixed.across()
     next(later)
-    pair[2].wait_recv()
-    spreads[2].start(near=False)
     parts = mixed.arrive()
 
     def residual(x_ref, a_ref, b_ref, c_ref, g_ref, x1_ref, h_ref):
@@ -793,7 +777,8 @@
     next(later)
     next(stages)
     spreads[1].forward()
-    spreads[2].start_near()
+    pair[2].wait_recv()
+    spreads[2].start()
     next(stages)
     next(stages)
     run(later)
@@ -1427,8 +1412,8 @@
                 + jnp.sum(w_up.astype(F32) * grad_up, 1),
             ]
         )
-        gain_sums = gain_sums + swap(gain_sums, 1)
-        gain_sums = gain_sums + swap(gain_sums, 2)
+        others = [swap(gain_sums, mask) for mask in (1, 2, 3)]
+        gain_sums = (gain_sums + others[0]) + (others[1] + others[2])
         return (
             relative(out, zi),
             relative(grad_tok, zi),

time: 624 us -> 617 us (0.989)
  Pallas kernels: 574 us -> 566 us
    pallas_call x2, Pallas kernels: 574 us -> 566 us  [call(): pl.pallas_call(kernel, out_shape=[jax.ShapeDtypeStruct(shape, dtype) for...]
  transfers between devices with their start and end apart: 2 -> 3, of which waited for: 0 -> 0; matrix products, arithmetic and copies ran while one was open for 1% -> 1% of each run, Pallas kernels for 0% -> 0%
where the time goes in v7:
time: 617 us; the launch traced here: 605 us
  Pallas kernels  566 us (92%)
  other arithmetic  21.4 us (3%)
  local copies, waits for them, and re-layouts  12 us (2%)
    pallas_call x2, Pallas kernels, call(): pl.pallas_call(kernel, out_shape=[jax.ShapeDtypeStruct(shape, dtype) for...  566 us
  transfers between devices with their start and end apart: 3, of which 0 were waited for; matrix products, arithmetic and copies ran while one was open for 1% of the time, Pallas kernels for 0%

profile of v7, /device:TPU:0, one launch (start us, length us, event | category | flops | bytes accessed | tf_op | source)
XLA Modules:
  0.0 604.9 jit_solution(14100845195579941675)
XLA Ops:
  0.7 0.9 fusion.2
  2.2 1.8 copy.23
  4.0 2.4 copy.24
  6.5 0.7 maximum_select_fusion
  8.7 0.7 pad_maximum_fusion.3.gn
  9.4 3.0 multiply_sine_fusion
  12.4 1.4 maximum_select_fusion.3.cot
  13.8 1.5 broadcast_multiply_fusion.xh
  15.4 0.9 pad_maximum_fusion.2.wq
  16.2 0.7 broadcast_in_dim.8
  17.0 299.6 %layer_forward.1 = (bf16[2048,1024]{1,0:T(8,128)(2,1)}, bf16[2048,512]{1,0:T(8,128)(2,1)}, bf16[2048,1024]{1,0:T(8,128)(2,1)}, bf16[2048,1024]{1,0:T(8,128)(2,1)...) custom-call(bf16[256,1024]{1,0:T(8,128)(2,1)} %pad_maximum_fusion.2., ...), custom_call_target="tpu_custom_call" | custom-call | tf_op jit(solution)/shard_map/layer_forward/pallas_call | solution.py:1206
  316.5 266.9 %layer_backward.1 = (bf16[256,2048]{1,0:T(8,128)(2,1)}, bf16[256,2048]{1,0:T(8,128)(2,1)}, f32[256,1024]{1,0:T(8,128)}, bf16[256,1024]{1,0:T(8,128)(2,1)}, f32[2...) custom-call(bf16[2048,1024]{1,0:T(8,128)(2,1)} %get-tuple-element.37, ...), custom_call_target="tpu_custom_call" | custom-call | tf_op jit(solution)/shard_map/layer_backward/pallas_call | solution.py:1206
  583.5 2.0 multiply_reduce_fusion.3
  585.5 1.9 multiply_reduce_fusion.5
  587.7 0.9 copy-done.3
  588.6 1.6 multiply_reduce_fusion.1
  590.6 0.8 copy-done.4
  591.4 1.6 multiply_reduce_fusion
  593.6 1.4 collective-permute-start.2
  596.3 1.4 maximum_select_fusion.7
  597.7 1.4 maximum_select_fusion.5
  599.6 0.9 copy-done.11
  600.5 1.0 copy.25
  601.5 1.8 copy.26
  (71 shorter events, 6.3 us)
Async XLA Ops:
  0.6 5.7 copy-start.1
  4.0 2.4 copy-start.2
  7.8 6.0 copy-start
  7.8 0.7 copy-start.18
  7.8 0.8 copy-start.17
  13.8 1.5 copy-start.10
  13.8 1.5 copy-start.15
  13.8 1.5 copy-start.16
  583.5 3.9 copy-start.9
  583.5 3.9 copy-start.14
  587.3 1.2 copy-start.3
  588.6 1.6 copy-start.8
  588.6 1.8 copy-start.13
  590.2 1.3 copy-start.4
  591.4 3.8 copy-start.5
  593.0 2.3 copy-start.6
  593.1 10.2 %collective-permute-start.1 = (f32[2,256]{1,0:T(2,128)S(1)}, f32[2,256]{1,0:T(2,128)S(1)}, u32[]{:S(2)}, u32[]{:S(2)}) collective-permute-start(f32[2,256]{1,0:T(2,128)S(1)} %pad_maximum_fusion.4), channel_id=1, source_target_pairs={{0,2},{1,3},{2,0},{3,1},{4,6},{5,7},{6,4},{7,5},{8,10},{9,11},{10,... | collective-permute-start | bytes 6152 | tf_op jit(solution)/shard_map/ppermute | solution.py:1228
  593.6 9.7 %collective-permute-start.2 = (f32[2,256]{1,0:T(2,128)S(1)}, f32[2,256]{1,0:T(2,128)S(1)}, u32[]{:S(2)}, u32[]{:S(2)}) collective-permute-start(f32[2,256]{1,0:T(2,128)S(1)} %pad_maximum_fusion.4), channel_id=1, source_target_pairs={{0,3},{1,2},{2,1},{3,0},{4,7},{5,6},{6,5},{7,4},{8,11},{9,10},{10,... | collective-permute-start | bytes 6152 | tf_op jit(solution)/shard_map/ppermute | solution.py:1228
  595.0 8.3 %collective-permute-start = (f32[2,256]{1,0:T(2,128)S(1)}, f32[2,256]{1,0:T(2,128)S(1)}, u32[]{:S(2)}, u32[]{:S(2)}) collective-permute-start(f32[2,256]{1,0:T(2,128)S(1)} %pad_maximum_fusion.4), channel_id=1, source_target_pairs={{0,1},{1,0},{2,3},{3,2},{4,5},{5,4},{6,7},{7,6},{8,9},{9,8},{10,11... | collective-permute-start | bytes 6152 | tf_op jit(solution)/shard_map/ppermute | solution.py:1228
  597.7 1.4 copy-start.7
  597.7 1.5 copy-start.12
  599.4 1.0 copy-start.11
